TPU v7x, 32 devices: a whole 2x2x4 slice. The times are simulated.
32 devices in a mesh: row: 4 (over z), col: 2 (over y), depth: 4 (over x, core).
Axes of the slice: x: 2, y: 2, z: 4, core: 2. Of those that a mesh axis runs over, the one named last changes fastest.
Arguments:
- right_sides: float32 [64, 4096], P('depth', ('row', 'col')), may hold values from -12 to 12
- blocks: float32 [4, 2, 16, 256, 256], P('row', 'col'), may hold values from -0.06 to 6.1, as said below
- block_rows: int32 [4, 2, 16], P('row', 'col'), may hold values from 0 to 3, as said below
- block_cols: int32 [4, 2, 16], P('row', 'col'), may hold values from 0 to 7, as said below
- block_count: int32 [4, 2], P('row', 'col'), may hold values from 2 to 16
Outputs:
- solution: float32 [64, 4096], P('depth', ('row', 'col'))
- residual: float32 [64, 4096], P('depth', ('row', 'col'))
Inputs may be any that keep to these rules, and one draw needn't show every extreme that they name: Slot s < 2 of row index r and col index c holds the diagonal block with block_rows = c * 2 + s and block_cols = r * 2 + s. The valid later slots name distinct blocks whose I is below J. At slots from block_count on, block_rows and block_cols hold 0; blocks there hold arbitrary values and are not part of A. `block_cols`: see block_rows. Diagonal-slot blocks are symmetric; A is positive definite. Slots from block_count on are not part of A.
All inputs are finite; a program needn't handle non-finite values.
Results may differ from a plain program's by a relative error of at most 0.0003.
Values sent between devices are 32-bit elements; how exact they have to be, the bound alone decides.
No kernel may reach another device: no remote copies, remote signals or barrier semaphores. Data moves between devices by JAX's collectives and lax.ppermute only.
A program may use at most 64 MiB of HBM per device.

v0:
```python
import jax
import jax.numpy as jnp
from jax import lax
from jax.sharding import PartitionSpec as P

BLK = 256
ITERS = 2
SEG = 2


def per_device(right_sides, blocks, block_rows, block_cols, block_count):
    highest = lax.Precision.HIGHEST
    own_width = right_sides.shape[0]
    depth_index = lax.axis_index("depth")
    tile_blocks = blocks[0, 0]
    rows_here = block_rows[0, 0]
    cols_here = block_cols[0, 0]
    live_count = block_count[0, 0]
    row_span = SEG * lax.axis_size("col")
    col_span = SEG * lax.axis_size("row")
    slot_index = jnp.arange(tile_blocks.shape[0], dtype=jnp.int32)
    residual_all = lax.all_gather(right_sides, "depth", axis=0, tiled=True)
    direction_all = residual_all
    solution = jnp.zeros_like(right_sides)
    current = lax.psum(jnp.dot(residual_all, residual_all.T, precision=highest), ("row", "col"))
    for iteration in range(ITERS):
        own_direction = lax.dynamic_slice_in_dim(
            direction_all, depth_index * own_width, own_width, 0
        )
        row_part = lax.all_gather(own_direction, "col", axis=1, tiled=True).reshape(
            own_width, row_span, BLK
        )
        col_part = lax.all_gather(own_direction, "row", axis=1, tiled=True).reshape(
            own_width, col_span, BLK
        )
        live_mask = (slot_index < live_count).astype(jnp.float32)
        mirror_mask = live_mask * (slot_index >= SEG).astype(jnp.float32)
        toward_rows = jnp.einsum(
            "csk,smk->csm", col_part[:, cols_here], tile_blocks, precision=highest
        )
        toward_cols = jnp.einsum(
            "csm,smk->csk", row_part[:, rows_here], tile_blocks, precision=highest
        )
        toward_rows = toward_rows * live_mask[None, :, None]
        toward_cols = toward_cols * mirror_mask[None, :, None]
        row_select = (rows_here[:, None] == jnp.arange(row_span, dtype=jnp.int32)[None, :]).astype(
            jnp.float32
        )
        col_select = (cols_here[:, None] == jnp.arange(col_span, dtype=jnp.int32)[None, :]).astype(
            jnp.float32
        )
        row_terms = jnp.einsum("si,csm->cim", row_select, toward_rows, precision=highest)
        col_terms = jnp.einsum("sj,csk->cjk", col_select, toward_cols, precision=highest)
        row_sum = lax.psum_scatter(
            row_terms.reshape(own_width, row_span * BLK), "col", scatter_dimension=1, tiled=True
        )
        col_sum = lax.psum_scatter(
            col_terms.reshape(own_width, col_span * BLK), "row", scatter_dimension=1, tiled=True
        )
        mapped = row_sum + col_sum
        mapped_all = lax.all_gather(mapped, "depth", axis=0, tiled=True)
        curvature, cross_gram, image_gram = lax.psum(
            (
                jnp.dot(direction_all, mapped_all.T, precision=highest),
                jnp.dot(residual_all, mapped_all.T, precision=highest),
                jnp.dot(mapped_all, mapped_all.T, precision=highest),
            ),
            ("row", "col"),
        )
        step_size = jax.scipy.linalg.cho_solve((jnp.linalg.cholesky(curvature), True), current)
        own_step = lax.dynamic_slice_in_dim(step_size, depth_index * own_width, own_width, 1)
        solution = solution + lax.dot_general(
            own_step, direction_all, (((0,), (0,)), ((), ())), precision=highest
        )
        residual_all = residual_all - lax.dot_general(
            step_size, mapped_all, (((0,), (0,)), ((), ())), precision=highest
        )
        if iteration + 1 < ITERS:
            coupling = jnp.dot(cross_gram, step_size, precision=highest)
            quadratic = lax.dot_general(
                step_size,
                jnp.dot(image_gram, step_size, precision=highest),
                (((0,), (0,)), ((), ())),
                precision=highest,
            )
            renewed = current - coupling - coupling.T + quadratic
            conjugate = jax.scipy.linalg.cho_solve((jnp.linalg.cholesky(current), True), renewed)
            direction_all = residual_all + lax.dot_general(
                conjugate, direction_all, (((0,), (0,)), ((), ())), precision=highest
            )
            current = renewed
    own_residual = lax.dynamic_slice_in_dim(residual_all, depth_index * own_width, own_width, 0)
    return (solution, own_residual)


def solution(mesh):
    return jax.shard_map(
        per_device,
        mesh=mesh,
        in_specs=(
            P("depth", ("row", "col")),
            P("row", "col", None, None, None),
            P("row", "col", None),
            P("row", "col", None),
            P("row", "col"),
        ),
        out_specs=(P("depth", ("row", "col")), P("depth", ("row", "col"))),
        check_vma=False,
    )
```

profile of v0, /device:TPU:0, one launch (start us, length us, event | category | flops | bytes accessed | tf_op | source)
XLA Modules:
  0.0 254.3 jit_solution(11665464484053111125)
XLA Ops:
  7.2 6.7 %all_gather.21 = f32[64,512]{1,0:T(8,128)S(1)} all-gather(f32[16,512]{1,0:T(8,128)} %param.8), channel_id=1, replica_groups=mesh['row'=4,'col'=2,'depth'=4] {'depth'}, dimensions={0}, use_global_device_ids=true | all-gather | bytes 163840 | tf_op jit(solution)/shard_map/all_gather | solution.py:22
  13.9 13.9 %all_gather.22 = f32[16,2048]{1,0:T(8,128)S(1)} all-gather(f32[16,512]{1,0:T(8,128)S(1)} %constant_dynamic-slice_fusion.1), channel_id=1, replica_groups=mesh['row'=4,'col'=2,'depth'=4] {'row'}, dimensions={1}, use_global_device_ids=true | all-gather | bytes 163840 | tf_op jit(solution)/shard_map/all_gather | solution.py:33
  27.9 0.7 fusion.57
  29.2 0.6 gather_fusion
  29.8 5.7 %fusion.6 = f32[16,16,256]{2,1,0:T(8,128)S(1)} fusion(f32[1,1,16,256,256]{4,3,2,1,0:T(8,128)} %param.9, f32[16,16,256]{2,1,0:T(8,128)S(1)} %gather_fusion), kind=kOutput, calls=%fused_computation.10 | convolution fusion | flops 201326592 | bytes 4718592 | tf_op jit(solution)/shard_map/csk,smk->csm/dot_general | solution.py:38
  35.5 0.4 fusion.17
  35.9 0.6 copy.36
  36.6 4.6 %all_gather.23 = f32[16,1024]{1,0:T(8,128)S(1)} all-gather(f32[16,512]{1,0:T(8,128)S(1)} %constant_dynamic-slice_fusion.1), channel_id=1, replica_groups=mesh['row'=4,'col'=2,'depth'=4] {'col'}, dimensions={1}, use_global_device_ids=true | all-gather | bytes 98304 | tf_op jit(solution)/shard_map/all_gather | solution.py:30
  41.2 0.6 gather_fusion.1
  41.8 4.3 %fusion.4 = f32[16,16,256]{2,1,0:T(8,128)S(1)} fusion(f32[1,1,16,256,256]{4,3,2,1,0:T(8,128)} %param.9, f32[16,16,256]{2,1,0:T(8,128)S(1)} %gather_fusion.1), kind=kOutput, calls=%fused_computation.8 | convolution fusion | flops 201326592 | bytes 4718592 | tf_op jit(solution)/shard_map/csm,smk->csk/dot_general | solution.py:41
  46.1 0.4 fusion.14
  46.5 0.7 copy.37
  47.5 0.3 reduce-scatter.5.cloned.1.call-done
  47.8 21.8 %reduce-scatter.7.cloned.1.call-done = f32[16,512]{1,0:T(8,128)} async-done(((f32[16,2048]{1,0:T(8,128)}), f32[16,512]{1,0:T(8,128)}) %reduce-scatter.7.cloned.1.call-update) | async-done | bytes 32784 | tf_op jit(solution)/shard_map/reduce_scatter | solution.py:57
  69.6 0.8 add.75
  70.4 5.4 %all_gather.24 = f32[64,512]{1,0:T(8,128)S(1)} all-gather(f32[16,512]{1,0:T(8,128)S(1)} %add.75), channel_id=1, replica_groups=mesh['row'=4,'col'=2,'depth'=4] {'depth'}, dimensions={0}, use_global_device_ids=true | all-gather | bytes 163840 | tf_op jit(solution)/shard_map/all_gather | solution.py:61
  76.3 35.3 %all-reduce = (f32[64,64]{0,1:T(8,128)S(1)}, f32[64,64]{0,1:T(8,128)S(1)}, f32[64,64]{1,0:T(8,128)S(1)}) all-reduce(f32[64,64]{0,1:T(8,128)S(1)} %fusion.59, f32[64,64]{0,1:T(8,128)S(1)} %convolution_bitcast_fusion, f32[64,64]{1,0:T(8,128)S(1)} %fusion.61), channel_id=1, replica_groups=mesh['row'=4,'col'=2,'depth'=4] {'row','col'}, use_global_device_ids=true, to_apply=%region_5.7 | all-reduce | flops 12288 | bytes 98304 | tf_op jit(solution)/shard_map/psum | solution.py:25
  111.8 5.8 %cholesky.59 = f32[64,64]{1,0:T(8,128)S(1)} custom-call(f32[64,64]{1,0:T(8,128)S(1)} %get-tuple-element.8), custom_call_target="Cholesky" | custom-call | tf_op jit(solution)/shard_map/jit(cholesky)/cholesky | solution.py:70
  117.7 0.6 compare_reduce_fusion.2
  118.3 0.7 fusion.24
  119.0 4.9 %custom-call.9 = f32[1,64,64]{1,2,0:T(8,128)S(1)} custom-call(f32[1,64,64]{2,1,0:T(8,128)S(1)} %fusion.24), custom_call_target="InvertDiagBlocksLowerTriangular" | custom-call | tf_op jit(solution)/shard_map/jit(_cho_solve)/triangular_solve | solution.py:70
  125.2 5.9 %cholesky.70 = f32[64,64]{1,0:T(8,128)S(1)} custom-call(f32[64,64]{1,0:T(8,128)S(1)} %get-tuple-element.7), custom_call_target="Cholesky" | custom-call | tf_op jit(solution)/shard_map/jit(cholesky)/cholesky | solution.py:87
  131.1 0.6 compare_reduce_fusion.1
  131.7 0.7 fusion.25
  132.4 4.9 %custom-call.10 = f32[1,64,64]{1,2,0:T(8,128)S(1)} custom-call(f32[1,64,64]{2,1,0:T(8,128)S(1)} %fusion.25), custom_call_target="InvertDiagBlocksLowerTriangular" | custom-call | tf_op jit(solution)/shard_map/jit(_cho_solve)/triangular_solve | solution.py:87
  137.9 0.3 convolution_add_fusion
  138.3 13.3 %all_gather.25 = f32[16,2048]{1,0:T(8,128)S(1)} all-gather(f32[16,512]{1,0:T(8,128)S(1)} %constant_dynamic-slice_fusion), channel_id=1, replica_groups=mesh['row'=4,'col'=2,'depth'=4] {'row'}, dimensions={1}, use_global_device_ids=true | all-gather | bytes 163840 | tf_op jit(solution)/shard_map/all_gather | solution.py:33
  151.6 4.6 %all_gather.26 = f32[16,1024]{1,0:T(8,128)S(1)} all-gather(f32[16,512]{1,0:T(8,128)S(1)} %constant_dynamic-slice_fusion), channel_id=1, replica_groups=mesh['row'=4,'col'=2,'depth'=4] {'col'}, dimensions={1}, use_global_device_ids=true | all-gather | bytes 98304 | tf_op jit(solution)/shard_map/all_gather | solution.py:30
  156.2 0.6 gather_fusion.2
  156.8 5.7 %fusion.2 = f32[16,16,256]{2,1,0:T(8,128)S(1)} fusion(f32[1,1,16,256,256]{4,3,2,1,0:T(8,128)} %param.9, f32[16,16,256]{2,1,0:T(8,128)S(1)} %gather_fusion.2), kind=kOutput, calls=%fused_computation.6 | convolution fusion | flops 201326592 | bytes 4718592 | tf_op jit(solution)/shard_map/csk,smk->csm/dot_general | solution.py:38
  162.5 0.4 fusion.11
  162.9 0.6 copy.38
  163.6 0.6 gather_fusion.3
  164.2 4.3 %fusion = f32[16,16,256]{2,1,0:T(8,128)S(1)} fusion(f32[1,1,16,256,256]{4,3,2,1,0:T(8,128)} %param.9, f32[16,16,256]{2,1,0:T(8,128)S(1)} %gather_fusion.3), kind=kOutput, calls=%fused_computation.4 | convolution fusion | flops 201326592 | bytes 4718592 | tf_op jit(solution)/shard_map/csm,smk->csk/dot_general | solution.py:41
  168.5 0.4 fusion.8
  168.8 0.7 copy.39
  169.7 1.3 reduce-scatter.9.cloned.1.call-done
  171.0 21.6 %reduce-scatter.11.cloned.1.call-done = f32[16,512]{1,0:T(8,128)} async-done(((f32[16,2048]{1,0:T(8,128)}), f32[16,512]{1,0:T(8,128)}) %reduce-scatter.11.cloned.1.call-update) | async-done | bytes 32784 | tf_op jit(solution)/shard_map/reduce_scatter | solution.py:57
  192.6 0.8 add.78
  193.4 5.4 %all_gather.27 = f32[64,512]{1,0:T(8,128)S(1)} all-gather(f32[16,512]{1,0:T(8,128)S(1)} %add.78), channel_id=1, replica_groups=mesh['row'=4,'col'=2,'depth'=4] {'depth'}, dimensions={0}, use_global_device_ids=true | all-gather | bytes 163840 | tf_op jit(solution)/shard_map/all_gather | solution.py:61
  199.1 34.3 %psum.34 = f32[64,64]{0,1:T(8,128)S(1)} all-reduce(f32[64,64]{0,1:T(8,128)S(1)} %fusion.63), channel_id=1, replica_groups=mesh['row'=4,'col'=2,'depth'=4] {'row','col'}, use_global_device_ids=true, to_apply=%region_9.12 | all-reduce | flops 4096 | bytes 32768 | tf_op jit(solution)/shard_map/psum | solution.py:62
  233.5 5.8 %cholesky.81 = f32[64,64]{1,0:T(8,128)S(1)} custom-call(f32[64,64]{1,0:T(8,128)S(1)} %fusion.31), custom_call_target="Cholesky" | custom-call | tf_op jit(solution)/shard_map/jit(cholesky)/cholesky | solution.py:70
  239.4 0.6 compare_reduce_fusion
  240.0 0.7 fusion.26
  240.7 4.9 %custom-call.11 = f32[1,64,64]{1,2,0:T(8,128)S(1)} custom-call(f32[1,64,64]{2,1,0:T(8,128)S(1)} %fusion.26), custom_call_target="InvertDiagBlocksLowerTriangular" | custom-call | tf_op jit(solution)/shard_map/jit(_cho_solve)/triangular_solve | solution.py:70
  246.1 0.3 fusion.64
  246.3 0.8 convolution_add_fusion.1
  247.2 0.6 dynamic-slice_subtract_fusion
  (47 shorter events, 4.2 us)
Async XLA Ops:
  7.2 28.4 %copy-start = (s32[1,1,16]{2,1,0:T(1,128)S(1)}, s32[1,1,16]{2,1,0:T(1,128)}, u32[]{:S(2)}) copy-start(s32[1,1,16]{2,1,0:T(1,128)} %param.10) | copy-start | bytes 196
  7.2 40.7 %reduce-scatter.5.cloned.1.call-start = ((), (), s32[]{:S(2)}) async-start(), calls=%async_computation.4 | async-start | bytes 98304 | tf_op jit(solution)/shard_map/reduce_scatter | solution.py:54
  29.8 16.3 %copy-start.1 = (s32[1,1,16]{2,1,0:T(1,128)S(1)}, s32[1,1,16]{2,1,0:T(1,128)}, u32[]{:S(2)}) copy-start(s32[1,1,16]{2,1,0:T(1,128)} %param.11) | copy-start | bytes 196
  36.6 33.0 %reduce-scatter.7.cloned.1.call-start = ((), (), s32[]{:S(2)}) async-start(), calls=%async_computation.5 | async-start | bytes 163840 | tf_op jit(solution)/shard_map/reduce_scatter | solution.py:57
  47.2 123.8 %reduce-scatter.9.cloned.1.call-start = ((), (), s32[]{:S(2)}) async-start(), calls=%async_computation.6 | async-start | bytes 98304 | tf_op jit(solution)/shard_map/reduce_scatter | solution.py:54
  163.5 29.1 %reduce-scatter.11.cloned.1.call-start = ((), (), s32[]{:S(2)}) async-start(), calls=%async_computation.7 | async-start | bytes 163840 | tf_op jit(solution)/shard_map/reduce_scatter | solution.py:57
Sparse Core Ops, SparseCore 0:
  36.7 11.1 reduce-scatter.4
  50.1 19.4 reduce-scatter.6
  163.6 7.3 reduce-scatter.8
  173.1 19.4 reduce-scatter.10
where the time goes:
time: 255 us; the launch traced here: 254 us
  blocking collectives  124 us (49%)
  waiting for transfers between devices  45 us (18%)
  other arithmetic  39.1 us (15%)
  matrix products  26.4 us (10%)
  between operations  14.8 us (6%)
  local copies, waits for them, and re-layouts  5.25 us (2%)
    reduce_scatter x2, waiting for transfers between devices, per_device(): lax.psum_scatter(col_terms.reshape(own_width, col_span * BLK), 'row', sca...  43.4 us
    psum x1, blocking collectives, per_device(): lax.psum(jnp.dot(residual_all, residual_all.T, precision=highest), ('row'...  35.3 us
    psum x1, blocking collectives, per_device(): lax.psum((jnp.dot(direction_all, mapped_all.T, precision=highest), jnp.do...  34.3 us
    all_gather x2, blocking collectives, per_device(): lax.all_gather(own_direction, 'row', axis=1, tiled=True)  27.3 us
    another operation x6, other arithmetic, per_device(): jnp.linalg.cholesky(curvature)  13 us
    dot_general x2, matrix products, per_device(): jnp.einsum('csk,smk->csm', col_part[:, cols_here], tile_blocks, precision...  11.4 us
    another operation x4, other arithmetic, per_device(): jax.scipy.linalg.cho_solve((jnp.linalg.cholesky(curvature), True), current)  11.1 us
    all_gather x2, blocking collectives, per_device(): mapped_all = lax.all_gather(mapped, 'depth', axis=0, tiled=True)  10.8 us
  transfers between devices with their start and end apart: 4, of which 4 were waited for; matrix products, arithmetic and copies ran while one was open for 5% of the time, Pallas kernels for 0%

commit v1 on v0

v1 whole, which is shorter than its diff:
```python
import functools

import jax
import jax.numpy as jnp
from jax import lax
from jax.experimental import pallas as pl
from jax.experimental.pallas import tpu as pltpu
from jax.sharding import PartitionSpec as P

BLK = 256
SEG = 2
HIGHEST = lax.Precision.HIGHEST
VMEM = pl.BlockSpec(memory_space=pltpu.VMEM)
SMEM = pl.BlockSpec(memory_space=pltpu.SMEM)
PARAMS = pltpu.CompilerParams(vmem_limit_bytes=40 << 20)


def partner(index, step, size):
    return index ^ step if size & (size - 1) == 0 else (index + step) % size


def source(index, step, size):
    return index ^ step if size & (size - 1) == 0 else (index + size - step) % size


def send_all(arrays, axis):
    size = lax.axis_size(axis)
    return [
        lax.ppermute(arrays[k - 1], axis, [(i, partner(i, k, size)) for i in range(size)])
        for k in range(1, size)
    ]


def source_of(axis, step):
    index, size = lax.axis_index(axis), lax.axis_size(axis)
    if size & (size - 1) == 0:
        return index ^ step
    return lax.rem(index + size - step, size)


def partner_of(axis, step):
    index, size = lax.axis_index(axis), lax.axis_size(axis)
    if size & (size - 1) == 0:
        return index ^ step
    return lax.rem(index + step, size)


def dot_nt(a, b):
    return lax.dot_general(a, b, (((1,), (1,)), ((), ())), precision=HIGHEST, preferred_element_type=jnp.float32)


def dot_tn(a, b):
    return lax.dot_general(a, b, (((0,), (0,)), ((), ())), precision=HIGHEST, preferred_element_type=jnp.float32)


def dot_nn(a, b):
    return lax.dot_general(a, b, (((1,), (0,)), ((), ())), precision=HIGHEST, preferred_element_type=jnp.float32)


def halves(x):
    high = x.astype(jnp.bfloat16)
    return high, (x - high.astype(jnp.float32)).astype(jnp.bfloat16)


def bf16_dot(a, b, contract):
    return lax.dot_general(a, b, (contract, ((), ())), preferred_element_type=jnp.float32)


def stack_fields(all_ref, own_ref, depth_refs):
    width, points = own_ref.shape[0], all_ref.shape[1]
    for step, ref in enumerate([own_ref] + depth_refs):
        place = source_of("depth", step)
        all_ref[pl.ds(pl.multiple_of(place * width, width), width), :] = ref[:, 0:points]


def products(
    n_row, n_col, count_ref, rows_ref, cols_ref, blocks_ref, own_ref, z_refs, y_refs, own_out, z_outs, y_outs,
    col_in, row_in, col_acc, row_acc,
):
    width, points = own_ref.shape[0], SEG * BLK
    row_at, col_at = lax.axis_index("row"), lax.axis_index("col")
    for step, ref in enumerate([own_ref] + z_refs):
        place = source_of("row", step) if step else row_at
        for part in range(SEG):
            high, low = halves(ref[:, part * BLK : (part + 1) * BLK])
            col_in[place * SEG + part] = jnp.concatenate([high, low], axis=0)
    for step, ref in enumerate([own_ref] + y_refs):
        place = source_of("col", step) if step else col_at
        for part in range(SEG):
            high, low = halves(ref[:, part * BLK : (part + 1) * BLK])
            row_in[place * SEG + part] = jnp.concatenate([high, low], axis=0)
    col_acc[...] = jnp.zeros_like(col_acc)
    row_acc[...] = jnp.zeros_like(row_acc)
    count = count_ref[0, 0]
    for slot in range(blocks_ref.shape[0]):
        high, low = halves(blocks_ref[slot])
        row_place, col_place = rows_ref[0, 0, slot], cols_ref[0, 0, slot]
        live = slot < count
        for vec, acc, at_in, at_out, contract in (
            (col_in, row_acc, col_place, row_place, ((1,), (1,))),
            (row_in, col_acc, row_place, col_place, ((1,), (0,))),
        ):
            if slot < SEG and acc is col_acc:
                continue
            both = vec[at_in]
            wide = bf16_dot(both, high, contract)
            term = wide[:width] + wide[width:] + bf16_dot(both[:width], low, contract)
            acc[at_out] += jnp.where(live, term, 0.0)
    for part in range(SEG):
        lanes = slice(part * BLK, (part + 1) * BLK)
        own_out[:, lanes] = row_acc[col_at * SEG + part] + col_acc[row_at * SEG + part]
        for step, ref in enumerate(z_outs, 1):
            ref[:, lanes] = col_acc[partner_of("row", step) * SEG + part]
        for step, ref in enumerate(y_outs, 1):
            ref[:, lanes] = row_acc[partner_of("col", step) * SEG + part]


def split(refs, *sizes):
    out = []
    for size in sizes:
        out.append(list(refs[:size]))
        refs = refs[size:]
    return out


def first_products(n_row, n_col, n_depth, *refs):
    (head, own, z_in, y_in, d_in, outs, z_outs, y_outs, scratch) = split(
        refs, 4, 1, n_row - 1, n_col - 1, n_depth - 1, 2, n_row - 1, n_col - 1, 5
    )
    *scratch, fields = scratch
    points = own[0].shape[1]
    products(n_row, n_col, *head, own[0], z_in, y_in, outs[0], z_outs, y_outs, *scratch)
    stack_fields(fields, own[0], d_in)
    gram = dot_nt(own[0][...], fields[...])
    extra = jnp.concatenate([gram, jnp.zeros_like(gram)], axis=1)
    outs[1][...] = extra
    for ref in z_outs:
        ref[:, points:] = extra


def first_combine(n_row, n_col, n_depth, *refs):
    partial, gram, z_in, y_in, field_refs, out, out_wide, fields = split(
        refs, 1, 1, n_row - 1, n_col - 1, n_depth, 1, 1, 1
    )
    points = partial[0].shape[1]
    total = partial[0][...]
    first = gram[0][:, : gram[0].shape[1] // 2]
    for ref in z_in:
        total += ref[:, :points]
        first += ref[:, points : points + first.shape[1]]
    for ref in y_in:
        total += ref[...]
    stack_fields(fields[0], field_refs[0], field_refs[1:])
    second = dot_nt(total, fields[0][...])
    out[0][...] = total
    out_wide[0][:, :points] = total
    out_wide[0][:, points:] = jnp.concatenate([first, second], axis=1)


def second_products(n_row, n_col, *refs):
    (head, own, z_in, y_in, outs, z_outs, y_outs, scratch) = split(
        refs, 4, 1, n_row - 1, n_col - 1, 2, n_row - 1, n_col - 1, 4
    )
    points = outs[0].shape[1]
    products(n_row, n_col, *head, own[0], z_in, y_in, outs[0], z_outs, y_outs, *scratch)
    grams = own[0][:, points:]
    for ref in y_in:
        grams += ref[:, points:]
    outs[1][...] = grams
    for ref in z_outs:
        ref[:, points:] = grams


def second_combine(n_row, n_col, n_depth, *refs):
    partial, gram, z_in, y_in, base_refs, image_refs, out_wide, out_gram, fields = split(
        refs, 1, 1, n_row - 1, n_col - 1, n_depth, n_depth, 1, 1, 1
    )
    points = partial[0].shape[1]
    half = gram[0].shape[1] // 2
    total = partial[0][...]
    second = gram[0][:, half:]
    for ref in z_in:
        total += ref[:, :points]
        second += ref[:, points + half :]
    for ref in y_in:
        total += ref[...]
    out_wide[0][:, :points] = total
    out_wide[0][:, points:] = jnp.concatenate([gram[0][:, :half], second], axis=1)
    stack_fields(fields[0], base_refs[0], base_refs[1:])
    third = dot_nt(total, fields[0][...])
    stack_fields(fields[0], image_refs[0], image_refs[1:])
    fourth = dot_nt(total, fields[0][...])
    out_gram[0][...] = jnp.concatenate([third, fourth], axis=1)


def eliminate(tables):
    size = tables[0].shape[0]
    at_row = lax.broadcasted_iota(jnp.int32, tables[0].shape, 0)
    for k in range(size):
        for i, table in enumerate(tables):
            pivot_row = table[k : k + 1, :] * (1.0 / table[k : k + 1, k : k + 1])
            tables[i] = jnp.where(at_row == k, pivot_row, table - table[:, k : k + 1] * pivot_row)
    return tables


def finish(n_depth, *refs):
    gathered, wide_refs, base_refs, image_refs, outs, scratch = split(refs, 1, n_depth, n_depth, n_depth, 2, 3)
    base, image, mapped = scratch
    solution_out, residual_out = outs
    width, points = solution_out.shape
    size = n_depth * width
    groups = gathered[0].shape[0] // n_depth
    stack_fields(base, base_refs[0], base_refs[1:])
    stack_fields(image, image_refs[0], image_refs[1:])
    late = [sum(gathered[0][g * n_depth + d] for g in range(groups)) for d in range(n_depth)]
    late = jnp.concatenate(late, axis=0)
    stack_fields(mapped, wide_refs[0], wide_refs[1:])
    early = mapped[:, points:]
    gram0, gram1 = early[:, :size], early[:, size:]
    gram2, gram3 = late[:, :size], late[:, size:]
    gram0, gram1, gram2, gram3 = (0.5 * (g + g.T) for g in (gram0, gram1, gram2, gram3))
    identity = (
        lax.broadcasted_iota(jnp.int32, (size, size), 0) == lax.broadcasted_iota(jnp.int32, (size, size), 1)
    ).astype(jnp.float32)
    first, inverse = eliminate(
        [jnp.concatenate([gram1, gram0], axis=1), jnp.concatenate([gram0, identity], axis=1)]
    )
    step1, inverse = first[:, size:], inverse[:, size:]
    coupling = dot_nn(gram1, step1)
    quadratic = dot_tn(step1, dot_nn(gram2, step1))
    renewed = gram0 - coupling - coupling.T + quadratic
    blend = identity + dot_nn(inverse, renewed)
    upper = dot_nn(gram1, blend) - dot_nn(gram2, step1)
    lower = dot_nn(gram2, blend) - dot_nn(gram3, step1)
    curvature = dot_tn(blend, upper) - dot_tn(step1, lower)
    curvature = 0.5 * (curvature + curvature.T)
    (second,) = eliminate([jnp.concatenate([curvature, renewed], axis=1)])
    own = lax.axis_index("depth") * width
    pick = (
        lax.broadcasted_iota(jnp.int32, (size, width), 0) == lax.broadcasted_iota(jnp.int32, (size, width), 1) + own
    ).astype(jnp.float32)
    step2 = dot_nn(second[:, size:], pick)
    weight0 = dot_nn(step1, pick) + dot_nn(blend, step2)
    weight1 = -dot_nn(step1, step2)
    base_all, image_all = base[...], image[...]
    solution_out[...] = dot_tn(weight0, base_all) + dot_tn(weight1, image_all)
    residual_out[...] = (
        base_refs[0][...] - dot_tn(weight0, image_all) - dot_tn(weight1, mapped[:, :points])
    )


def call(body, name, operands, n_smem, out_shapes, scratch):
    return pl.pallas_call(
        body,
        name=name,
        out_shape=[jax.ShapeDtypeStruct(s, jnp.float32) for s in out_shapes],
        in_specs=[SMEM] * n_smem + [VMEM] * (len(operands) - n_smem),
        out_specs=[VMEM] * len(out_shapes),
        scratch_shapes=scratch,
        compiler_params=PARAMS,
    )(*operands)


def per_device(right_sides, blocks, block_rows, block_cols, block_count):
    n_row, n_col, n_depth = (lax.axis_size(a) for a in ("row", "col", "depth"))
    width, points = right_sides.shape
    size = n_depth * width
    blocks = blocks[0, 0]
    head = [block_count, block_rows, block_cols, blocks]
    f32, b16 = jnp.float32, jnp.bfloat16
    work = [
        pltpu.VMEM((n_row * SEG, 2 * width, BLK), b16),
        pltpu.VMEM((n_col * SEG, 2 * width, BLK), b16),
        pltpu.VMEM((n_row * SEG, width, BLK), f32),
        pltpu.VMEM((n_col * SEG, width, BLK), f32),
    ]
    fields = pltpu.VMEM((size, points), f32)
    narrow, wide, tail = (width, points), (width, points + 2 * size), (width, 2 * size)

    y = send_all([right_sides] * (n_col - 1), "col")
    z = send_all([right_sides] * (n_row - 1), "row")
    base = [right_sides] + send_all([right_sides] * (n_depth - 1), "depth")
    partial, gram, *rest = call(
        functools.partial(first_products, n_row, n_col, n_depth), "first_products",
        head + [right_sides] + z + y + base[1:], 3,
        [narrow, tail] + [wide] * (n_row - 1) + [narrow] * (n_col - 1), work + [fields],
    )
    y = send_all(rest[n_row - 1 :], "col")
    z = send_all(rest[: n_row - 1], "row")
    image, image_wide = call(
        functools.partial(first_combine, n_row, n_col, n_depth), "first_combine",
        [partial, gram] + z + y + base, 0, [narrow, wide], [fields],
    )
    y = send_all([image_wide] * (n_col - 1), "col")
    z = send_all([image] * (n_row - 1), "row")
    image = [image] + send_all([image] * (n_depth - 1), "depth")
    partial, gram, *rest = call(
        functools.partial(second_products, n_row, n_col), "second_products",
        head + [image_wide] + z + y, 3,
        [narrow, tail] + [wide] * (n_row - 1) + [narrow] * (n_col - 1), work,
    )
    y = send_all(rest[n_row - 1 :], "col")
    z = send_all(rest[: n_row - 1], "row")
    mapped, late = call(
        functools.partial(second_combine, n_row, n_col, n_depth), "second_combine",
        [partial, gram] + z + y + base + image, 0, [wide, tail], [fields],
    )
    mapped = [mapped] + send_all([mapped] * (n_depth - 1), "depth")
    everyone = ("row", "col", "depth")
    late = lax.all_to_all(
        jnp.broadcast_to(late[None], (n_row * n_col * n_depth,) + late.shape), everyone, 0, 0
    )
    solution, residual = call(
        functools.partial(finish, n_depth), "finish",
        [late] + mapped + base + image, 0, [narrow, narrow],
        [fields, fields, pltpu.VMEM((size, points + 2 * size), f32)],
    )
    return solution, residual


def solution(mesh):
    return jax.shard_map(
        per_device,
        mesh=mesh,
        in_specs=(
            P("depth", ("row", "col")),
            P("row", "col", None, None, None),
            P("row", "col", None),
            P("row", "col", None),
            P("row", "col"),
        ),
        out_specs=(P("depth", ("row", "col")), P("depth", ("row", "col"))),
        check_vma=False,
    )
```

time: 255 us -> 79.5 us (0.31)
  blocking collectives: 124 us -> 0 us
  other arithmetic: 39.1 us -> 0 us
  starting transfers between devices: 0.16 us -> 32.7 us
  matrix products: 26.4 us -> 0 us
  waiting for transfers between devices: 45 us -> 20.5 us
  Pallas kernels: 0 us -> 19.4 us
  between operations: 14.8 us -> 1.39 us
    psum x2 -> x0, blocking collectives: 69.7 us -> none  [the longest x1 35.3 us: per_device(): lax.psum(jnp.dot(residual_all, residual_all.T, precision=highest), ('row'...]
    all_gather x7 -> x0, blocking collectives: 54 us -> none  [the longest x2 27.3 us: per_device(): lax.all_gather(own_direction, 'row', axis=1, tiled=True)]
    reduce_scatter x4 -> x0, waiting for transfers between devices: 45 us -> none  [the longest x2 43.4 us: per_device(): lax.psum_scatter(col_terms.reshape(own_width, col_span * BLK), 'row', sca...]
    another operation x15 -> x0, other arithmetic: 36.2 us -> none  [the longest x6 13 us: per_device(): jnp.linalg.cholesky(curvature)]
    ppermute x0 -> x25, starting transfers between devices: none -> 29.7 us  [send_all(): lax.ppermute(arrays[k - 1], axis, [(i, partner(i, k, size)) for i in rang...]
    dot_general x20 -> x0, matrix products: 25 us -> none  [the longest x2 11.4 us: per_device(): jnp.einsum('csk,smk->csm', col_part[:, cols_here], tile_blocks, precision...]
    pallas_call x0 -> x5, Pallas kernels: none -> 19.4 us  [call(): pl.pallas_call(body, name=name, out_shape=[jax.ShapeDtypeStruct(s, jnp.fl...]
    ppermute x0 -> x25, waiting for transfers between devices: none -> 16.5 us  [send_all(): lax.ppermute(arrays[k - 1], axis, [(i, partner(i, k, size)) for i in rang...]
  transfers between devices with their start and end apart: 4 -> 26, of which waited for: 4 -> 9; matrix products, arithmetic and copies ran while one was open for 5% -> 0% of each run, Pallas kernels for 0% -> 3%
where the time goes in v1:
time: 79.5 us; the launch traced here: 79.2 us
  starting transfers between devices  32.7 us (41%)
  waiting for transfers between devices  20.5 us (26%)
  Pallas kernels  19.4 us (24%)
  local copies, waits for them, and re-layouts  5.07 us (6%)
  between operations  1.39 us (2%)
    ppermute x25, starting transfers between devices, send_all(): lax.ppermute(arrays[k - 1], axis, [(i, partner(i, k, size)) for i in rang...  29.7 us
    pallas_call x5, Pallas kernels, call(): pl.pallas_call(body, name=name, out_shape=[jax.ShapeDtypeStruct(s, jnp.fl...  19.4 us
    ppermute x25, waiting for transfers between devices, send_all(): lax.ppermute(arrays[k - 1], axis, [(i, partner(i, k, size)) for i in rang...  16.5 us
    unnamed x12, local copies, waits for them, and re-layouts  4.26 us
    all_to_all x1, waiting for transfers between devices, per_device(): lax.all_to_all(jnp.broadcast_to(late[None], (n_row * n_col * n_depth,) +...  4.07 us
    all_to_all x1, starting transfers between devices, per_device(): lax.all_to_all(jnp.broadcast_to(late[None], (n_row * n_col * n_depth,) +...  3.07 us
  transfers between devices with their start and end apart: 26, of which 9 were waited for; matrix products, arithmetic and copies ran while one was open for 0% of the time, Pallas kernels for 3%

profile of v1, /device:TPU:0, one launch (start us, length us, event | category | flops | bytes accessed | tf_op | source)
XLA Modules:
  0.0 79.2 jit_solution(15889830494116823468)
XLA Ops:
  0.6 0.6 collective-permute-start.4
  1.2 2.6 %collective-permute-start.5 = (f32[16,512]{1,0:T(8,128)}, f32[16,512]{1,0:T(8,128)S(1)}, u32[]{:S(2)}, u32[]{:S(2)}) collective-permute-start(f32[16,512]{1,0:T(8,128)} %refs_5_.1), channel_id=1, source_target_pairs={{0,2},{1,3},{2,0},{3,1},{4,6},{5,7},{6,4},{7,5},{8,10},{9,11},{10,... | collective-permute-start | bytes 98312 | tf_op jit(solution)/shard_map/ppermute | solution.py:29
  3.7 0.0 collective-permute-start.6
  3.8 1.8 %collective-permute-start = (f32[16,512]{1,0:T(8,128)}, f32[16,512]{1,0:T(8,128)S(1)}, u32[]{:S(2)}, u32[]{:S(2)}) collective-permute-start(f32[16,512]{1,0:T(8,128)} %refs_5_.1), channel_id=1, source_target_pairs={{0,8},{8,0},{16,24},{24,16},{1,9},{9,1},{17,25},{25,17},{2,10},{10... | collective-permute-start | bytes 98312 | tf_op jit(solution)/shard_map/ppermute | solution.py:29
  5.6 2.6 %collective-permute-start.1 = (f32[16,512]{1,0:T(8,128)}, f32[16,512]{1,0:T(8,128)S(1)}, u32[]{:S(2)}, u32[]{:S(2)}) collective-permute-start(f32[16,512]{1,0:T(8,128)} %refs_5_.1), channel_id=1, source_target_pairs={{0,16},{8,24},{16,0},{24,8},{1,17},{9,25},{17,1},{25,9},{2,18},{10... | collective-permute-start | bytes 98312 | tf_op jit(solution)/shard_map/ppermute | solution.py:29
  8.2 0.0 collective-permute-done.4.refs_9_.refs_7_.refs_6_
  8.2 0.0 collective-permute-start.2
  8.2 0.0 collective-permute-done.5.refs_10_.refs_8_.refs_7_
  8.2 1.7 %collective-permute-start.3 = (f32[16,512]{1,0:T(8,128)}, f32[16,512]{1,0:T(8,128)S(1)}, u32[]{:S(2)}, u32[]{:S(2)}) collective-permute-start(f32[16,512]{1,0:T(8,128)} %refs_5_.1), channel_id=1, source_target_pairs={{0,4},{4,0},{1,5},{5,1},{2,6},{6,2},{3,7},{7,3},{8,12},{12,8},{9,1... | collective-permute-start | bytes 98312 | tf_op jit(solution)/shard_map/ppermute | solution.py:29
  10.6 0.0 collective-permute-done.refs_5_
  10.6 0.6 collective-permute-done.1.refs_6_
  11.3 2.9 %collective-permute-done.2.refs_7_ = f32[16,512]{1,0:T(8,128)S(1)} collective-permute-done((f32[16,512]{1,0:T(8,128)}, f32[16,512]{1,0:T(8,128)S(1)}, u32[]{:S(2)}, u32[]{:S(2)}) %collective-permute-start.2) | collective-permute-done | bytes 32800 | tf_op jit(solution)/shard_map/ppermute | solution.py:29
  14.1 2.2 %copy-done = f32[1,1,16,256,256]{4,3,2,1,0:T(8,128)S(1)} copy-done((f32[1,1,16,256,256]{4,3,2,1,0:T(8,128)S(1)}, f32[1,1,16,256,256]{4,3,2,1,0:T(8,128)}, u32[]{:S(2)}) %copy-start) | copy-done | bytes 4194328
  16.3 0.8 copy-done.2
  17.1 0.7 copy-done.4
  17.7 0.7 copy-done.5
  18.4 2.4 %first_products.1 = (f32[16,512]{1,0:T(8,128)S(1)}, f32[16,128]{1,0:T(8,128)S(1)}, f32[16,640]{1,0:T(8,128)S(1)}, f32[16,640]{1,0:T(8,128)S(1)}, f32[16,640]{1,0:T(8,128)S(1)}, /*index=5*/f32[16,512]{1,0:T(8,128)S(1)}) custom-call(s32[1,1]{1,0:T(1,128)S(6)} %copy.7.refs_0_, s32[1,1,16]{2,1,0:T(1,128)S(1)} %copy-done.4, s32[1,1,16]{2,1,0:T(1,128)S(1)} %copy-done.5, ...), custom_call_target="tpu_custom_call" | custom-call | tf_op jit(solution)/shard_map/first_products/pallas_call | solution.py:253
  20.8 0.1 collective-permute-start.7
  20.9 2.6 %collective-permute-start.8 = (f32[16,640]{1,0:T(8,128)S(1)}, f32[16,640]{1,0:T(8,128)S(1)}, u32[]{:S(2)}, u32[]{:S(2)}) collective-permute-start(f32[16,640]{1,0:T(8,128)S(1)} %get-tuple-element.21), channel_id=1, source_target_pairs={{0,16},{8,24},{16,0},{24,8},{1,17},{9,25},{17,1},{25,9},{2,18},{10... | collective-permute-start | bytes 122888 | tf_op jit(solution)/shard_map/ppermute | solution.py:29
  23.5 1.8 %collective-permute-start.9 = (f32[16,640]{1,0:T(8,128)S(1)}, f32[16,640]{1,0:T(8,128)S(1)}, u32[]{:S(2)}, u32[]{:S(2)}) collective-permute-start(f32[16,640]{1,0:T(8,128)S(1)} %get-tuple-element.22), channel_id=1, source_target_pairs={{0,24},{8,16},{16,8},{24,0},{1,25},{9,17},{17,9},{25,1},{2,26},{10... | collective-permute-start | bytes 122888 | tf_op jit(solution)/shard_map/ppermute | solution.py:29
  25.3 1.5 %collective-permute-start.10 = (f32[16,512]{1,0:T(8,128)S(1)}, f32[16,512]{1,0:T(8,128)S(1)}, u32[]{:S(2)}, u32[]{:S(2)}) collective-permute-start(f32[16,512]{1,0:T(8,128)S(1)} %get-tuple-element.23), channel_id=1, source_target_pairs={{0,4},{4,0},{1,5},{5,1},{2,6},{6,2},{3,7},{7,3},{8,12},{12,8},{9,1... | collective-permute-start | bytes 98312 | tf_op jit(solution)/shard_map/ppermute | solution.py:29
  26.8 2.5 %collective-permute-done.10.refs_5_ = f32[16,512]{1,0:T(8,128)S(1)} collective-permute-done((f32[16,512]{1,0:T(8,128)S(1)}, f32[16,512]{1,0:T(8,128)S(1)}, u32[]{:S(2)}, u32[]{:S(2)}) %collective-permute-start.10) | collective-permute-done | bytes 32800 | tf_op jit(solution)/shard_map/ppermute | solution.py:29
  29.3 0.0 collective-permute-done.8.refs_3_
  29.3 0.0 collective-permute-done.9.refs_4_
  29.3 0.3 first_combine.1
  29.6 1.5 %collective-permute-start.14 = (f32[16,640]{1,0:T(8,128)S(1)}, f32[16,640]{1,0:T(8,128)S(1)}, u32[]{:S(2)}, u32[]{:S(2)}) collective-permute-start(f32[16,640]{1,0:T(8,128)S(1)} %get-tuple-element.24.refs_4_), channel_id=1, source_target_pairs={{0,4},{4,0},{1,5},{5,1},{2,6},{6,2},{3,7},{7,3},{8,12},{12,8},{9,1... | collective-permute-start | bytes 122888 | tf_op jit(solution)/shard_map/ppermute | solution.py:29
  31.2 2.6 %collective-permute-start.12 = (f32[16,512]{1,0:T(8,128)S(1)}, f32[16,512]{1,0:T(8,128)S(1)}, u32[]{:S(2)}, u32[]{:S(2)}) collective-permute-start(f32[16,512]{1,0:T(8,128)S(1)} %get-tuple-element.25.refs_10_.refs_9_), channel_id=1, source_target_pairs={{0,16},{8,24},{16,0},{24,8},{1,17},{9,25},{17,1},{25,9},{2,18},{10... | collective-permute-start | bytes 98312 | tf_op jit(solution)/shard_map/ppermute | solution.py:29
  33.8 1.8 %collective-permute-start.13 = (f32[16,512]{1,0:T(8,128)S(1)}, f32[16,512]{1,0:T(8,128)S(1)}, u32[]{:S(2)}, u32[]{:S(2)}) collective-permute-start(f32[16,512]{1,0:T(8,128)S(1)} %get-tuple-element.25.refs_10_.refs_9_), channel_id=1, source_target_pairs={{0,24},{8,16},{16,8},{24,0},{1,25},{9,17},{17,9},{25,1},{2,26},{10... | collective-permute-start | bytes 98312 | tf_op jit(solution)/shard_map/ppermute | solution.py:29
  35.6 1.5 %collective-permute-start.20 = (f32[16,512]{1,0:T(8,128)S(1)}, f32[16,512]{1,0:T(8,128)S(1)}, u32[]{:S(2)}, u32[]{:S(2)}) collective-permute-start(f32[16,512]{1,0:T(8,128)S(1)} %get-tuple-element.25.refs_10_.refs_9_), channel_id=1, source_target_pairs={{0,2},{1,3},{2,0},{3,1},{4,6},{5,7},{6,4},{7,5},{8,10},{9,11},{10,... | collective-permute-start | bytes 98312 | tf_op jit(solution)/shard_map/ppermute | solution.py:29
  37.1 2.5 %collective-permute-done.13.refs_7_ = f32[16,512]{1,0:T(8,128)S(1)} collective-permute-done((f32[16,512]{1,0:T(8,128)S(1)}, f32[16,512]{1,0:T(8,128)S(1)}, u32[]{:S(2)}, u32[]{:S(2)}) %collective-permute-start.13) | collective-permute-done | bytes 32800 | tf_op jit(solution)/shard_map/ppermute | solution.py:29
  39.5 0.0 collective-permute-done.14.refs_8_
  39.5 2.3 %second_products.1 = (f32[16,512]{1,0:T(8,128)S(1)}, f32[16,128]{1,0:T(8,128)S(1)}, f32[16,640]{1,0:T(8,128)S(1)}, f32[16,640]{1,0:T(8,128)S(1)}, f32[16,640]{1,0:T(8,128)S(1)}, /*index=5*/f32[16,512]{1,0:T(8,128)S(1)}) custom-call(s32[1,1]{1,0:T(1,128)S(6)} %copy.7.refs_0_, s32[1,1,16]{2,1,0:T(1,128)S(1)} %copy-done.4, s32[1,1,16]{2,1,0:T(1,128)S(1)} %copy-done.5, ...), custom_call_target="tpu_custom_call" | custom-call | tf_op jit(solution)/shard_map/second_products/pallas_call | solution.py:253
  41.8 0.1 collective-permute-start.15
  41.9 2.3 %collective-permute-start.16 = (f32[16,640]{1,0:T(8,128)S(1)}, f32[16,640]{1,0:T(8,128)S(1)}, u32[]{:S(2)}, u32[]{:S(2)}) collective-permute-start(f32[16,640]{1,0:T(8,128)S(1)} %get-tuple-element.29), channel_id=1, source_target_pairs={{0,16},{8,24},{16,0},{24,8},{1,17},{9,25},{17,1},{25,9},{2,18},{10... | collective-permute-start | bytes 122888 | tf_op jit(solution)/shard_map/ppermute | solution.py:29
  44.2 2.1 %collective-permute-start.17 = (f32[16,640]{1,0:T(8,128)S(1)}, f32[16,640]{1,0:T(8,128)S(1)}, u32[]{:S(2)}, u32[]{:S(2)}) collective-permute-start(f32[16,640]{1,0:T(8,128)S(1)} %get-tuple-element.30), channel_id=1, source_target_pairs={{0,24},{8,16},{16,8},{24,0},{1,25},{9,17},{17,9},{25,1},{2,26},{10... | collective-permute-start | bytes 122888 | tf_op jit(solution)/shard_map/ppermute | solution.py:29
  46.3 0.0 collective-permute-done.19.refs_11_.refs_10_
  46.3 0.6 collective-permute-start.18
  46.9 3.1 %collective-permute-done.21.refs_13_.refs_12_ = f32[16,512]{1,0:T(8,128)S(1)} collective-permute-done((f32[16,512]{1,0:T(8,128)S(1)}, f32[16,512]{1,0:T(8,128)S(1)}, u32[]{:S(2)}, u32[]{:S(2)}) %collective-permute-start.21) | collective-permute-done | bytes 32800 | tf_op jit(solution)/shard_map/ppermute | solution.py:29
  49.9 0.3 collective-permute-done.18.refs_5_
  50.3 0.3 second_combine.1
  50.6 0.8 %broadcast_in_dim.2 = f32[32,16,128]{2,1,0:T(8,128)} broadcast(f32[16,128]{1,0:T(8,128)S(1)} %get-tuple-element.32), dimensions={1,2} | broadcast | bytes 270336 | tf_op jit(solution)/shard_map/broadcast_in_dim | solution.py:311
  51.4 3.1 %all-to-all-start = ((f32[32,16,128]{2,1,0:T(8,128)}), f32[32,16,128]{2,1,0:T(8,128)S(1)}, u32[]{:S(2)}, u32[]{:S(2)}) async-start(f32[32,16,128]{2,1,0:T(8,128)} %broadcast_in_dim.2), calls=%async_computation | async-start | bytes 524288 | tf_op jit(solution)/shard_map/all_to_all | solution.py:310
  54.5 0.3 collective-permute-start.22
  54.8 1.6 %collective-permute-start.23 = (f32[16,640]{1,0:T(8,128)S(1)}, f32[16,640]{1,0:T(8,128)S(1)}, u32[]{:S(2)}, u32[]{:S(2)}) collective-permute-start(f32[16,640]{1,0:T(8,128)S(1)} %get-tuple-element.33.refs_1_), channel_id=1, source_target_pairs={{0,2},{1,3},{2,0},{3,1},{4,6},{5,7},{6,4},{7,5},{8,10},{9,11},{10,... | collective-permute-start | bytes 122888 | tf_op jit(solution)/shard_map/ppermute | solution.py:29
  56.5 3.1 %collective-permute-done.23.refs_3_ = f32[16,640]{1,0:T(8,128)S(1)} collective-permute-done((f32[16,640]{1,0:T(8,128)S(1)}, f32[16,640]{1,0:T(8,128)S(1)}, u32[]{:S(2)}, u32[]{:S(2)}) %collective-permute-start.23) | collective-permute-done | bytes 40992 | tf_op jit(solution)/shard_map/ppermute | solution.py:29
  59.6 1.4 %collective-permute-done.24.refs_4_ = f32[16,640]{1,0:T(8,128)S(1)} collective-permute-done((f32[16,640]{1,0:T(8,128)S(1)}, f32[16,640]{1,0:T(8,128)S(1)}, u32[]{:S(2)}, u32[]{:S(2)}) %collective-permute-start.24) | collective-permute-done | bytes 40992 | tf_op jit(solution)/shard_map/ppermute | solution.py:29
  61.0 4.1 %all-to-all-done.refs_0_ = f32[32,16,128]{2,1,0:T(8,128)S(1)} async-done(((f32[32,16,128]{2,1,0:T(8,128)}), f32[32,16,128]{2,1,0:T(8,128)S(1)}, u32[]{:S(2)}, u32[]{:S(2)}) %all-to-all-start) | async-done | bytes 262176 | tf_op jit(solution)/shard_map/all_to_all | solution.py:310
  65.1 14.1 %finish.1 = (f32[16,512]{1,0:T(8,128)}, f32[16,512]{1,0:T(8,128)}) custom-call(f32[32,16,128]{2,1,0:T(8,128)S(1)} %all-to-all-done.refs_0_, f32[16,640]{1,0:T(8,128)S(1)} %get-tuple-element.33.refs_1_, f32[16,640]{1,0:T(8,128)S(1)} %collective-permute-done.22.refs_2_, f32[16,640]{1,0:T(8,128)S(1)} %collective-permute-done.23.refs_3_, ...), custom_call_target="tpu_custom_call" | custom-call | tf_op jit(solution)/shard_map/finish/pallas_call | solution.py:253
  (22 shorter events, 0.1 us)
Async XLA Ops:
  0.6 7.6 %collective-permute-start.4 = (f32[16,512]{1,0:T(8,128)}, f32[16,512]{1,0:T(8,128)S(1)}, u32[]{:S(2)}, u32[]{:S(2)}) collective-permute-start(f32[16,512]{1,0:T(8,128)} %refs_5_.1), channel_id=1, source_target_pairs={{0,1},{1,0},{2,3},{3,2},{4,5},{5,4},{6,7},{7,6},{8,9},{9,8},{10,11... | collective-permute-start | bytes 98312 | tf_op jit(solution)/shard_map/ppermute | solution.py:29
  1.2 7.0 %collective-permute-start.5 = (f32[16,512]{1,0:T(8,128)}, f32[16,512]{1,0:T(8,128)S(1)}, u32[]{:S(2)}, u32[]{:S(2)}) collective-permute-start(f32[16,512]{1,0:T(8,128)} %refs_5_.1), channel_id=1, source_target_pairs={{0,2},{1,3},{2,0},{3,1},{4,6},{5,7},{6,4},{7,5},{8,10},{9,11},{10,... | collective-permute-start | bytes 98312 | tf_op jit(solution)/shard_map/ppermute | solution.py:29
  3.7 6.9 %collective-permute-start.6 = (f32[16,512]{1,0:T(8,128)}, f32[16,512]{1,0:T(8,128)S(1)}, u32[]{:S(2)}, u32[]{:S(2)}) collective-permute-start(f32[16,512]{1,0:T(8,128)} %refs_5_.1), channel_id=1, source_target_pairs={{0,3},{1,2},{2,1},{3,0},{4,7},{5,6},{6,5},{7,4},{8,11},{9,10},{10,... | collective-permute-start | bytes 98312 | tf_op jit(solution)/shard_map/ppermute | solution.py:29
  3.8 6.8 %collective-permute-start = (f32[16,512]{1,0:T(8,128)}, f32[16,512]{1,0:T(8,128)S(1)}, u32[]{:S(2)}, u32[]{:S(2)}) collective-permute-start(f32[16,512]{1,0:T(8,128)} %refs_5_.1), channel_id=1, source_target_pairs={{0,8},{8,0},{16,24},{24,16},{1,9},{9,1},{17,25},{25,17},{2,10},{10... | collective-permute-start | bytes 98312 | tf_op jit(solution)/shard_map/ppermute | solution.py:29
  5.6 5.6 %collective-permute-start.1 = (f32[16,512]{1,0:T(8,128)}, f32[16,512]{1,0:T(8,128)S(1)}, u32[]{:S(2)}, u32[]{:S(2)}) collective-permute-start(f32[16,512]{1,0:T(8,128)} %refs_5_.1), channel_id=1, source_target_pairs={{0,16},{8,24},{16,0},{24,8},{1,17},{9,25},{17,1},{25,9},{2,18},{10... | collective-permute-start | bytes 98312 | tf_op jit(solution)/shard_map/ppermute | solution.py:29
  8.2 5.9 %collective-permute-start.2 = (f32[16,512]{1,0:T(8,128)}, f32[16,512]{1,0:T(8,128)S(1)}, u32[]{:S(2)}, u32[]{:S(2)}) collective-permute-start(f32[16,512]{1,0:T(8,128)} %refs_5_.1), channel_id=1, source_target_pairs={{0,24},{8,16},{16,8},{24,0},{1,25},{9,17},{17,9},{25,1},{2,26},{10... | collective-permute-start | bytes 98312 | tf_op jit(solution)/shard_map/ppermute | solution.py:29
  8.2 5.9 %collective-permute-start.3 = (f32[16,512]{1,0:T(8,128)}, f32[16,512]{1,0:T(8,128)S(1)}, u32[]{:S(2)}, u32[]{:S(2)}) collective-permute-start(f32[16,512]{1,0:T(8,128)} %refs_5_.1), channel_id=1, source_target_pairs={{0,4},{4,0},{1,5},{5,1},{2,6},{6,2},{3,7},{7,3},{8,12},{12,8},{9,1... | collective-permute-start | bytes 98312 | tf_op jit(solution)/shard_map/ppermute | solution.py:29
  14.1 2.2 %copy-start = (f32[1,1,16,256,256]{4,3,2,1,0:T(8,128)S(1)}, f32[1,1,16,256,256]{4,3,2,1,0:T(8,128)}, u32[]{:S(2)}) copy-start(f32[1,1,16,256,256]{4,3,2,1,0:T(8,128)} %param.6) | copy-start | bytes 12582916
  16.3 0.8 copy-start.2
  17.1 0.7 copy-start.4
  17.7 0.7 copy-start.5
  18.4 21.1 %copy-start.1 = (f32[1,1,16,256,256]{4,3,2,1,0:T(8,128)S(1)}, f32[1,1,16,256,256]{4,3,2,1,0:T(8,128)}, u32[]{:S(2)}) copy-start(f32[1,1,16,256,256]{4,3,2,1,0:T(8,128)} %param.6) | copy-start | bytes 12582916
  18.4 31.9 %copy-start.3 = (f32[16,512]{1,0:T(8,128)S(1)}, f32[16,512]{1,0:T(8,128)}, u32[]{:S(2)}) copy-start(f32[16,512]{1,0:T(8,128)} %refs_5_.1) | copy-start | bytes 98308
  20.8 8.5 %collective-permute-start.7 = (f32[16,640]{1,0:T(8,128)S(1)}, f32[16,640]{1,0:T(8,128)S(1)}, u32[]{:S(2)}, u32[]{:S(2)}) collective-permute-start(f32[16,640]{1,0:T(8,128)S(1)} %get-tuple-element.20), channel_id=1, source_target_pairs={{0,8},{8,0},{16,24},{24,16},{1,9},{9,1},{17,25},{25,17},{2,10},{10... | collective-permute-start | bytes 122888 | tf_op jit(solution)/shard_map/ppermute | solution.py:29
  20.9 8.4 %collective-permute-start.8 = (f32[16,640]{1,0:T(8,128)S(1)}, f32[16,640]{1,0:T(8,128)S(1)}, u32[]{:S(2)}, u32[]{:S(2)}) collective-permute-start(f32[16,640]{1,0:T(8,128)S(1)} %get-tuple-element.21), channel_id=1, source_target_pairs={{0,16},{8,24},{16,0},{24,8},{1,17},{9,25},{17,1},{25,9},{2,18},{10... | collective-permute-start | bytes 122888 | tf_op jit(solution)/shard_map/ppermute | solution.py:29
  23.5 5.9 %collective-permute-start.9 = (f32[16,640]{1,0:T(8,128)S(1)}, f32[16,640]{1,0:T(8,128)S(1)}, u32[]{:S(2)}, u32[]{:S(2)}) collective-permute-start(f32[16,640]{1,0:T(8,128)S(1)} %get-tuple-element.22), channel_id=1, source_target_pairs={{0,24},{8,16},{16,8},{24,0},{1,25},{9,17},{17,9},{25,1},{2,26},{10... | collective-permute-start | bytes 122888 | tf_op jit(solution)/shard_map/ppermute | solution.py:29
  25.3 4.1 %collective-permute-start.10 = (f32[16,512]{1,0:T(8,128)S(1)}, f32[16,512]{1,0:T(8,128)S(1)}, u32[]{:S(2)}, u32[]{:S(2)}) collective-permute-start(f32[16,512]{1,0:T(8,128)S(1)} %get-tuple-element.23), channel_id=1, source_target_pairs={{0,4},{4,0},{1,5},{5,1},{2,6},{6,2},{3,7},{7,3},{8,12},{12,8},{9,1... | collective-permute-start | bytes 98312 | tf_op jit(solution)/shard_map/ppermute | solution.py:29
  29.6 5.9 %collective-permute-start.11 = (f32[16,512]{1,0:T(8,128)S(1)}, f32[16,512]{1,0:T(8,128)S(1)}, u32[]{:S(2)}, u32[]{:S(2)}) collective-permute-start(f32[16,512]{1,0:T(8,128)S(1)} %get-tuple-element.25.refs_10_.refs_9_), channel_id=1, source_target_pairs={{0,8},{8,0},{16,24},{24,16},{1,9},{9,1},{17,25},{25,17},{2,10},{10... | collective-permute-start | bytes 98312 | tf_op jit(solution)/shard_map/ppermute | solution.py:29
  29.6 9.9 %collective-permute-start.14 = (f32[16,640]{1,0:T(8,128)S(1)}, f32[16,640]{1,0:T(8,128)S(1)}, u32[]{:S(2)}, u32[]{:S(2)}) collective-permute-start(f32[16,640]{1,0:T(8,128)S(1)} %get-tuple-element.24.refs_4_), channel_id=1, source_target_pairs={{0,4},{4,0},{1,5},{5,1},{2,6},{6,2},{3,7},{7,3},{8,12},{12,8},{9,1... | collective-permute-start | bytes 122888 | tf_op jit(solution)/shard_map/ppermute | solution.py:29
  31.2 5.9 %collective-permute-start.12 = (f32[16,512]{1,0:T(8,128)S(1)}, f32[16,512]{1,0:T(8,128)S(1)}, u32[]{:S(2)}, u32[]{:S(2)}) collective-permute-start(f32[16,512]{1,0:T(8,128)S(1)} %get-tuple-element.25.refs_10_.refs_9_), channel_id=1, source_target_pairs={{0,16},{8,24},{16,0},{24,8},{1,17},{9,25},{17,1},{25,9},{2,18},{10... | collective-permute-start | bytes 98312 | tf_op jit(solution)/shard_map/ppermute | solution.py:29
  33.8 5.7 %collective-permute-start.13 = (f32[16,512]{1,0:T(8,128)S(1)}, f32[16,512]{1,0:T(8,128)S(1)}, u32[]{:S(2)}, u32[]{:S(2)}) collective-permute-start(f32[16,512]{1,0:T(8,128)S(1)} %get-tuple-element.25.refs_10_.refs_9_), channel_id=1, source_target_pairs={{0,24},{8,16},{16,8},{24,0},{1,25},{9,17},{17,9},{25,1},{2,26},{10... | collective-permute-start | bytes 98312 | tf_op jit(solution)/shard_map/ppermute | solution.py:29
  35.6 10.7 %collective-permute-start.19 = (f32[16,512]{1,0:T(8,128)S(1)}, f32[16,512]{1,0:T(8,128)S(1)}, u32[]{:S(2)}, u32[]{:S(2)}) collective-permute-start(f32[16,512]{1,0:T(8,128)S(1)} %get-tuple-element.25.refs_10_.refs_9_), channel_id=1, source_target_pairs={{0,1},{1,0},{2,3},{3,2},{4,5},{5,4},{6,7},{7,6},{8,9},{9,8},{10,11... | collective-permute-start | bytes 98312 | tf_op jit(solution)/shard_map/ppermute | solution.py:29
  35.6 10.7 %collective-permute-start.20 = (f32[16,512]{1,0:T(8,128)S(1)}, f32[16,512]{1,0:T(8,128)S(1)}, u32[]{:S(2)}, u32[]{:S(2)}) collective-permute-start(f32[16,512]{1,0:T(8,128)S(1)} %get-tuple-element.25.refs_10_.refs_9_), channel_id=1, source_target_pairs={{0,2},{1,3},{2,0},{3,1},{4,6},{5,7},{6,4},{7,5},{8,10},{9,11},{10,... | collective-permute-start | bytes 98312 | tf_op jit(solution)/shard_map/ppermute | solution.py:29
  41.8 8.4 %collective-permute-start.15 = (f32[16,640]{1,0:T(8,128)S(1)}, f32[16,640]{1,0:T(8,128)S(1)}, u32[]{:S(2)}, u32[]{:S(2)}) collective-permute-start(f32[16,640]{1,0:T(8,128)S(1)} %get-tuple-element.28), channel_id=1, source_target_pairs={{0,8},{8,0},{16,24},{24,16},{1,9},{9,1},{17,25},{25,17},{2,10},{10... | collective-permute-start | bytes 122888 | tf_op jit(solution)/shard_map/ppermute | solution.py:29
  41.9 8.4 %collective-permute-start.16 = (f32[16,640]{1,0:T(8,128)S(1)}, f32[16,640]{1,0:T(8,128)S(1)}, u32[]{:S(2)}, u32[]{:S(2)}) collective-permute-start(f32[16,640]{1,0:T(8,128)S(1)} %get-tuple-element.29), channel_id=1, source_target_pairs={{0,16},{8,24},{16,0},{24,8},{1,17},{9,25},{17,1},{25,9},{2,18},{10... | collective-permute-start | bytes 122888 | tf_op jit(solution)/shard_map/ppermute | solution.py:29
  44.2 6.1 %collective-permute-start.17 = (f32[16,640]{1,0:T(8,128)S(1)}, f32[16,640]{1,0:T(8,128)S(1)}, u32[]{:S(2)}, u32[]{:S(2)}) collective-permute-start(f32[16,640]{1,0:T(8,128)S(1)} %get-tuple-element.30), channel_id=1, source_target_pairs={{0,24},{8,16},{16,8},{24,0},{1,25},{9,17},{17,9},{25,1},{2,26},{10... | collective-permute-start | bytes 122888 | tf_op jit(solution)/shard_map/ppermute | solution.py:29
  46.3 3.7 %collective-permute-start.21 = (f32[16,512]{1,0:T(8,128)S(1)}, f32[16,512]{1,0:T(8,128)S(1)}, u32[]{:S(2)}, u32[]{:S(2)}) collective-permute-start(f32[16,512]{1,0:T(8,128)S(1)} %get-tuple-element.25.refs_10_.refs_9_), channel_id=1, source_target_pairs={{0,3},{1,2},{2,1},{3,0},{4,7},{5,6},{6,5},{7,4},{8,11},{9,10},{10,... | collective-permute-start | bytes 98312 | tf_op jit(solution)/shard_map/ppermute | solution.py:29
  46.3 4.0 %collective-permute-start.18 = (f32[16,512]{1,0:T(8,128)S(1)}, f32[16,512]{1,0:T(8,128)S(1)}, u32[]{:S(2)}, u32[]{:S(2)}) collective-permute-start(f32[16,512]{1,0:T(8,128)S(1)} %get-tuple-element.31), channel_id=1, source_target_pairs={{0,4},{4,0},{1,5},{5,1},{2,6},{6,2},{3,7},{7,3},{8,12},{12,8},{9,1... | collective-permute-start | bytes 98312 | tf_op jit(solution)/shard_map/ppermute | solution.py:29
  51.4 13.7 %all-to-all-start = ((f32[32,16,128]{2,1,0:T(8,128)}), f32[32,16,128]{2,1,0:T(8,128)S(1)}, u32[]{:S(2)}, u32[]{:S(2)}) async-start(f32[32,16,128]{2,1,0:T(8,128)} %broadcast_in_dim.2), calls=%async_computation | async-start | bytes 524288 | tf_op jit(solution)/shard_map/all_to_all | solution.py:310
  54.5 2.0 %collective-permute-start.22 = (f32[16,640]{1,0:T(8,128)S(1)}, f32[16,640]{1,0:T(8,128)S(1)}, u32[]{:S(2)}, u32[]{:S(2)}) collective-permute-start(f32[16,640]{1,0:T(8,128)S(1)} %get-tuple-element.33.refs_1_), channel_id=1, source_target_pairs={{0,1},{1,0},{2,3},{3,2},{4,5},{5,4},{6,7},{7,6},{8,9},{9,8},{10,11... | collective-permute-start | bytes 122888 | tf_op jit(solution)/shard_map/ppermute | solution.py:29
  54.8 4.8 %collective-permute-start.23 = (f32[16,640]{1,0:T(8,128)S(1)}, f32[16,640]{1,0:T(8,128)S(1)}, u32[]{:S(2)}, u32[]{:S(2)}) collective-permute-start(f32[16,640]{1,0:T(8,128)S(1)} %get-tuple-element.33.refs_1_), channel_id=1, source_target_pairs={{0,2},{1,3},{2,0},{3,1},{4,6},{5,7},{6,4},{7,5},{8,10},{9,11},{10,... | collective-permute-start | bytes 122888 | tf_op jit(solution)/shard_map/ppermute | solution.py:29
  56.5 4.6 %collective-permute-start.24 = (f32[16,640]{1,0:T(8,128)S(1)}, f32[16,640]{1,0:T(8,128)S(1)}, u32[]{:S(2)}, u32[]{:S(2)}) collective-permute-start(f32[16,640]{1,0:T(8,128)S(1)} %get-tuple-element.33.refs_1_), channel_id=1, source_target_pairs={{0,3},{1,2},{2,1},{3,0},{4,7},{5,6},{6,5},{7,4},{8,11},{9,10},{10,... | collective-permute-start | bytes 122888 | tf_op jit(solution)/shard_map/ppermute | solution.py:29

commit v2 on v1

v2 whole, which is shorter than its diff:
```python
import functools

import jax
import jax.numpy as jnp
from jax import lax
from jax.experimental import pallas as pl
from jax.experimental.pallas import tpu as pltpu
from jax.sharding import PartitionSpec as P

BLK = 256
SEG = 2
HIGHEST = lax.Precision.HIGHEST
VMEM = pl.BlockSpec(memory_space=pltpu.VMEM)
SMEM = pl.BlockSpec(memory_space=pltpu.SMEM)
PARAMS = pltpu.CompilerParams(vmem_limit_bytes=40 << 20)


def partner(index, step, size):
    return index ^ step if size & (size - 1) == 0 else (index + step) % size


def source(index, step, size):
    return index ^ step if size & (size - 1) == 0 else (index + size - step) % size


def send_all(arrays, axis):
    size = lax.axis_size(axis)
    return [
        lax.ppermute(arrays[k - 1], axis, [(i, partner(i, k, size)) for i in range(size)])
        for k in range(1, size)
    ]


def source_of(axis, step):
    index, size = lax.axis_index(axis), lax.axis_size(axis)
    if size & (size - 1) == 0:
        return index ^ step
    return lax.rem(index + size - step, size)


def partner_of(axis, step):
    index, size = lax.axis_index(axis), lax.axis_size(axis)
    if size & (size - 1) == 0:
        return index ^ step
    return lax.rem(index + step, size)


def dot_nt(a, b):
    return lax.dot_general(a, b, (((1,), (1,)), ((), ())), precision=HIGHEST, preferred_element_type=jnp.float32)


def dot_tn(a, b):
    return lax.dot_general(a, b, (((0,), (0,)), ((), ())), precision=HIGHEST, preferred_element_type=jnp.float32)


def dot_nn(a, b):
    return lax.dot_general(a, b, (((1,), (0,)), ((), ())), precision=HIGHEST, preferred_element_type=jnp.float32)


def halves(x):
    high = x.astype(jnp.bfloat16)
    return high, (x - high.astype(jnp.float32)).astype(jnp.bfloat16)


def bf16_dot(a, b, contract):
    return lax.dot_general(a, b, (contract, ((), ())), preferred_element_type=jnp.float32)


def stack_fields(all_ref, own_ref, depth_refs):
    width, points = own_ref.shape[0], all_ref.shape[1]
    for step, ref in enumerate([own_ref] + depth_refs):
        place = source_of("depth", step)
        all_ref[pl.ds(pl.multiple_of(place * width, width), width), :] = ref[:, 0:points]


def prepare(
    count_ref, rows_ref, cols_ref, blocks_ref, fields_ref, high_out, low_out, fields_out, table_out,
    landed, rows_at, cols_at, sems,
):
    slots = blocks_ref.shape[2]
    copies = [pltpu.make_async_copy(blocks_ref.at[0, 0, s], landed.at[s], sems.at[s]) for s in range(slots)]
    copies.append(pltpu.make_async_copy(rows_ref, rows_at, sems.at[slots]))
    copies.append(pltpu.make_async_copy(cols_ref, cols_at, sems.at[slots + 1]))
    copies.append(pltpu.make_async_copy(fields_ref, fields_out, sems.at[slots + 2]))
    for copy in copies:
        copy.start()
    for slot in range(slots):
        copies[slot].wait()
        high_out[slot], low_out[slot] = halves(landed[slot])
    for copy in copies[slots:]:
        copy.wait()
    for slot in range(slots):
        table_out[0, slot] = rows_at[0, 0, slot]
        table_out[1, slot] = cols_at[0, 0, slot]
        table_out[2, slot] = count_ref[0, 0]


def products(
    n_row, n_col, table_ref, high_ref, low_ref, own_ref, z_refs, y_refs, own_out, z_outs, y_outs,
    col_in, row_in, col_acc, row_acc,
):
    width = own_ref.shape[0]
    row_at, col_at = lax.axis_index("row"), lax.axis_index("col")
    for axis, refs, held in (("row", [own_ref] + z_refs, col_in), ("col", [own_ref] + y_refs, row_in)):
        for step, ref in enumerate(refs):
            place = source_of(axis, step)
            for part in range(SEG):
                high, low = halves(ref[:, part * BLK : (part + 1) * BLK])
                held[place * SEG + part] = jnp.concatenate([high, low], axis=0)
    col_acc[...] = jnp.zeros_like(col_acc)
    row_acc[...] = jnp.zeros_like(row_acc)
    count = table_ref[2, 0]
    for slot in range(high_ref.shape[0]):
        high, low = high_ref[slot], low_ref[slot]
        row_place, col_place = table_ref[0, slot], table_ref[1, slot]
        live = slot < count
        for vec, acc, at_in, at_out, contract in (
            (col_in, row_acc, col_place, row_place, ((1,), (1,))),
            (row_in, col_acc, row_place, col_place, ((1,), (0,))),
        ):
            if slot < SEG and acc is col_acc:
                continue
            both = vec[at_in]
            wide = bf16_dot(both, high, contract)
            term = wide[:width] + wide[width:] + bf16_dot(both[:width], low, contract)
            acc[at_out] += jnp.where(live, term, 0.0)
    for part in range(SEG):
        lanes = slice(part * BLK, (part + 1) * BLK)
        own_out[:, lanes] = row_acc[col_at * SEG + part] + col_acc[row_at * SEG + part]
        for step, ref in enumerate(z_outs, 1):
            ref[:, lanes] = col_acc[partner_of("row", step) * SEG + part]
        for step, ref in enumerate(y_outs, 1):
            ref[:, lanes] = row_acc[partner_of("col", step) * SEG + part]


def split(refs, *sizes):
    out = []
    for size in sizes:
        out.append(list(refs[:size]))
        refs = refs[size:]
    return out


def first_products(n_row, n_col, *refs):
    (head, own, z_in, y_in, outs, z_outs, y_outs, scratch) = split(
        refs, 3, 1, n_row - 1, n_col - 1, 1, n_row - 1, n_col - 1, 4
    )
    products(n_row, n_col, *head, own[0], z_in, y_in, outs[0], z_outs, y_outs, *scratch)


def first_combine(n_row, n_col, n_depth, *refs):
    partial, z_in, y_in, field_refs, out, out_wide, fields = split(refs, 1, n_row - 1, n_col - 1, n_depth, 1, 1, 1)
    points = partial[0].shape[1]
    total = partial[0][...]
    for ref in z_in + y_in:
        total += ref[...]
    stack_fields(fields[0], field_refs[0], field_refs[1:])
    everything = fields[0][...]
    out[0][...] = total
    out_wide[0][:, :points] = total
    out_wide[0][:, points:] = jnp.concatenate(
        [dot_nt(field_refs[0][...], everything), dot_nt(total, everything)], axis=1
    )


def second_products(n_row, n_col, *refs):
    (head, own, z_in, y_in, outs, z_outs, y_outs, scratch) = split(
        refs, 3, 1, n_row - 1, n_col - 1, 2, n_row - 1, n_col - 1, 4
    )
    points = outs[0].shape[1]
    products(n_row, n_col, *head, own[0], z_in, y_in, outs[0], z_outs, y_outs, *scratch)
    grams = own[0][:, points:]
    for ref in y_in:
        grams += ref[:, points:]
    outs[1][...] = grams
    for ref in z_outs:
        ref[:, points:] = grams


def second_combine(n_row, n_col, n_depth, *refs):
    partial, gram, z_in, y_in, base_refs, image_refs, out_wide, out_gram, fields = split(
        refs, 1, 1, n_row - 1, n_col - 1, n_depth, n_depth, 1, 1, 1
    )
    points = partial[0].shape[1]
    total = partial[0][...]
    early = gram[0][...]
    for ref in z_in:
        total += ref[:, :points]
        early += ref[:, points:]
    for ref in y_in:
        total += ref[...]
    out_wide[0][:, :points] = total
    out_wide[0][:, points:] = early
    stack_fields(fields[0], base_refs[0], base_refs[1:])
    third = dot_nt(total, fields[0][...])
    stack_fields(fields[0], image_refs[0], image_refs[1:])
    fourth = dot_nt(total, fields[0][...])
    late = jnp.concatenate([third, fourth], axis=1)
    for i in range(out_gram[0].shape[0]):
        out_gram[0][i] = late


def eliminate(tables):
    size, wide = tables[0].shape
    sub = 8
    at_row = lax.broadcasted_iota(jnp.int32, (sub, wide), 0)
    tables = [[table[t : t + sub] for t in range(0, size, sub)] for table in tables]
    for k in range(0, size, 4):
        home, base = k // sub, k % sub
        for tiles in tables:
            spread = [[jnp.broadcast_to(tile[:, k + j : k + j + 1], (sub, wide)) for tile in tiles] for j in range(4)]
            row = [jnp.broadcast_to(tiles[home][base + i : base + i + 1], (sub, wide)) for i in range(4)]
            e = [
                [jnp.broadcast_to(spread[j][home][base + i : base + i + 1], (sub, wide)) if i <= j else None for j in range(4)]
                for i in range(4)
            ]
            scale = 1.0 / (e[0][0] * e[1][1] - e[0][1] * e[0][1])
            a00, a01, a11 = e[1][1] * scale, -e[0][1] * scale, e[0][0] * scale
            x00, x10 = a00 * e[0][2] + a01 * e[1][2], a01 * e[0][2] + a11 * e[1][2]
            x01, x11 = a00 * e[0][3] + a01 * e[1][3], a01 * e[0][3] + a11 * e[1][3]
            s00 = e[2][2] - (e[0][2] * x00 + e[1][2] * x10)
            s01 = e[2][3] - (e[0][2] * x01 + e[1][2] * x11)
            s11 = e[3][3] - (e[0][3] * x01 + e[1][3] * x11)
            scale = 1.0 / (s00 * s11 - s01 * s01)
            t2 = row[2] - (x00 * row[0] + x10 * row[1])
            t3 = row[3] - (x01 * row[0] + x11 * row[1])
            p2 = (s11 * t2 - s01 * t3) * scale
            p3 = (s00 * t3 - s01 * t2) * scale
            p0 = (a00 * row[0] + a01 * row[1]) - (x00 * p2 + x01 * p3)
            p1 = (a01 * row[0] + a11 * row[1]) - (x10 * p2 + x11 * p3)
            pivots = (p0, p1, p2, p3)
            for t, tile in enumerate(tiles):
                if t == home:
                    keep = tile - sum(spread[j][t] * pivots[j] for j in range(4))
                    for i in range(4):
                        keep = jnp.where(at_row == base + i, pivots[i], keep)
                    tiles[t] = keep
                else:
                    tiles[t] = tile - sum(spread[j][t] * pivots[j] for j in range(4))
    return [jnp.concatenate(tiles, axis=0) for tiles in tables]


def identity_of(size):
    shape = (size, size)
    same = lax.broadcasted_iota(jnp.int32, shape, 0) == lax.broadcasted_iota(jnp.int32, shape, 1)
    return same.astype(jnp.float32)


def early_solve(n_depth, points, *refs):
    wide_refs, outs, scratch = split(refs, n_depth, 4, 1)
    width = wide_refs[0].shape[0]
    for step, ref in enumerate(wide_refs):
        place = source_of("depth", step)
        scratch[0][pl.ds(pl.multiple_of(place * width, width), width), :] = ref[:, points:]
    early = scratch[0][...]
    size = n_depth * width
    gram0, gram1 = early[:, :size], early[:, size:]
    first, inverse = eliminate(
        [jnp.concatenate([gram1, gram0], axis=1), jnp.concatenate([gram0, identity_of(size)], axis=1)]
    )
    step1 = first[:, size:]
    coupling = dot_nn(gram1, step1)
    outs[0][...] = step1
    outs[1][...] = inverse[:, size:]
    outs[2][...] = gram0 - coupling - coupling.T
    outs[3][...] = gram1


def finish(n_depth, *refs):
    gathered, solved, wide_refs, base_refs, image_refs, outs, scratch = split(
        refs, 1, 4, n_depth, n_depth, n_depth, 2, 3
    )
    base, image, mapped = scratch
    solution_out, residual_out = outs
    width, points = solution_out.shape
    size = n_depth * width
    groups = gathered[0].shape[0] // n_depth
    stack_fields(base, base_refs[0], base_refs[1:])
    stack_fields(image, image_refs[0], image_refs[1:])
    stack_fields(mapped, wide_refs[0], wide_refs[1:])
    late = [sum(gathered[0][g * n_depth + d] for g in range(groups)) for d in range(n_depth)]
    late = jnp.concatenate(late, axis=0)
    gram2, gram3 = late[:, :size], late[:, size:]
    step1, inverse, rest, gram1 = (ref[...] for ref in solved)
    product = dot_nn(gram2, step1)
    renewed = rest + dot_tn(step1, product)
    blend = identity_of(size) + dot_nn(inverse, renewed)
    upper = dot_nn(gram1, blend) - product
    lower = dot_nn(gram2, blend) - dot_nn(gram3, step1)
    curvature = dot_tn(blend, upper) - dot_tn(step1, lower)
    (second,) = eliminate([jnp.concatenate([curvature, renewed], axis=1)])
    own = lax.axis_index("depth") * width
    pick = (
        lax.broadcasted_iota(jnp.int32, (size, width), 0) == lax.broadcasted_iota(jnp.int32, (size, width), 1) + own
    ).astype(jnp.float32)
    step2 = dot_nn(second[:, size:], pick)
    weight0 = dot_nn(step1, pick) + dot_nn(blend, step2)
    weight1 = -dot_nn(step1, step2)
    base_all, image_all = base[...], image[...]
    solution_out[...] = dot_tn(weight0, base_all) + dot_tn(weight1, image_all)
    residual_out[...] = base_refs[0][...] - dot_tn(weight0, image_all) - dot_tn(weight1, mapped[...])


def call(body, name, operands, in_specs, out_shapes, scratch, cost=None, out_specs=None):
    return pl.pallas_call(
        body,
        name=name,
        out_shape=[s if hasattr(s, "dtype") else jax.ShapeDtypeStruct(s, jnp.float32) for s in out_shapes],
        in_specs=list(in_specs) + [VMEM] * (len(operands) - len(in_specs)),
        out_specs=out_specs or [VMEM] * len(out_shapes),
        scratch_shapes=scratch,
        compiler_params=PARAMS,
        cost_estimate=cost,
    )(*operands)


def per_device(right_sides, blocks, block_rows, block_cols, block_count):
    n_row, n_col, n_depth = (lax.axis_size(a) for a in ("row", "col", "depth"))
    width, points = right_sides.shape
    size = n_depth * width
    slots = blocks.shape[2]
    f32, b16 = jnp.float32, jnp.bfloat16
    work = [
        pltpu.VMEM((n_row * SEG, 2 * width, BLK), b16),
        pltpu.VMEM((n_col * SEG, 2 * width, BLK), b16),
        pltpu.VMEM((n_row * SEG, width, BLK), f32),
        pltpu.VMEM((n_col * SEG, width, BLK), f32),
    ]
    fields = pltpu.VMEM((size, points), f32)
    narrow, wide, tail, square = (width, points), (width, points + 2 * size), (width, 2 * size), (size, size)

    y = send_all([right_sides] * (n_col - 1), "col")
    z = send_all([right_sides] * (n_row - 1), "row")
    half = jax.ShapeDtypeStruct(blocks.shape[2:], b16)
    high, low, fields_copy, table = call(
        prepare, "prepare",
        [block_count]
        + [pltpu.with_memory_space_constraint(x, pltpu.HBM) for x in (block_rows, block_cols, blocks, right_sides)],
        [SMEM] + [pl.BlockSpec(memory_space=pltpu.HBM)] * 4,
        [half, half, narrow, jax.ShapeDtypeStruct((3, slots), jnp.int32)],
        [pltpu.VMEM(blocks.shape[2:], f32)]
        + [pltpu.SMEM(block_rows.shape, jnp.int32)] * 2 + [pltpu.SemaphoreType.DMA((slots + 3,))],
        pl.CostEstimate(flops=4 * blocks.size, transcendentals=0, bytes_accessed=8 * blocks.size),
        [VMEM] * 3 + [SMEM],
    )
    head = [table, high, low]
    base = [right_sides] + send_all([fields_copy] * (n_depth - 1), "depth")
    partial, *rest = call(
        functools.partial(first_products, n_row, n_col), "first_products",
        head + [right_sides] + z + y, [SMEM], [narrow] * (n_row + n_col - 1), work,
    )
    y = send_all(rest[n_row - 1 :], "col")
    z = send_all(rest[: n_row - 1], "row")
    image, image_wide = call(
        functools.partial(first_combine, n_row, n_col, n_depth), "first_combine",
        [partial] + z + y + base, [], [narrow, wide], [fields],
    )
    y = send_all([image_wide] * (n_col - 1), "col")
    z = send_all([image] * (n_row - 1), "row")
    image = [image] + send_all([image] * (n_depth - 1), "depth")
    partial, gram, *rest = call(
        functools.partial(second_products, n_row, n_col), "second_products",
        head + [image_wide] + z + y, [SMEM],
        [narrow, tail] + [wide] * (n_row - 1) + [narrow] * (n_col - 1), work,
    )
    y = send_all(rest[n_row - 1 :], "col")
    z = send_all(rest[: n_row - 1], "row")
    n_all = n_row * n_col * n_depth
    mapped, late = call(
        functools.partial(second_combine, n_row, n_col, n_depth), "second_combine",
        [partial, gram] + z + y + base + image, [], [wide, (n_all,) + tail], [fields],
    )
    mapped = [mapped] + send_all([mapped] * (n_depth - 1), "depth")
    late = lax.all_to_all(late, ("row", "col", "depth"), 0, 0)
    solved = call(
        functools.partial(early_solve, n_depth, points), "early_solve", mapped, [], [square] * 4,
        [pltpu.VMEM((size, 2 * size), f32)],
        pl.CostEstimate(flops=4 * size**3, transcendentals=0, bytes_accessed=160 * size * size),
    )
    solution, residual = call(
        functools.partial(finish, n_depth), "finish",
        [late] + list(solved) + mapped + base + image, [], [narrow, narrow], [fields, fields, fields],
    )
    return solution, residual


def solution(mesh):
    return jax.shard_map(
        per_device,
        mesh=mesh,
        in_specs=(
            P("depth", ("row", "col")),
            P("row", "col", None, None, None),
            P("row", "col", None),
            P("row", "col", None),
            P("row", "col"),
        ),
        out_specs=(P("depth", ("row", "col")), P("depth", ("row", "col"))),
        check_vma=False,
    )
```

time: 79.5 us -> 67.6 us (0.85)
  waiting for transfers between devices: 20.5 us -> 14.9 us
  local copies, waits for them, and re-layouts: 5.07 us -> 0.01 us
  Pallas kernels: 19.4 us -> 18.2 us
    unnamed x12 -> x2, local copies, waits for them, and re-layouts: 4.26 us -> 0.01 us
    all_to_all x1, waiting for transfers between devices: 4.07 us -> 0.39 us  [per_device(): late = lax.all_to_all(late, ('row', 'col', 'depth'), 0, 0)]
    ppermute x25, waiting for transfers between devices: 16.5 us -> 14.5 us  [send_all(): lax.ppermute(arrays[k - 1], axis, [(i, partner(i, k, size)) for i in rang...]
    pallas_call x5 -> x7, Pallas kernels: 19.4 us -> 18.2 us  [call(): pl.pallas_call(body, name=name, out_shape=[s if hasattr(s, 'dtype') else...]
    all_to_all x1, starting transfers between devices: 3.07 us -> 4.05 us  [per_device(): late = lax.all_to_all(late, ('row', 'col', 'depth'), 0, 0)]
    ppermute x25, starting transfers between devices: 29.7 us -> 28.8 us  [send_all(): lax.ppermute(arrays[k - 1], axis, [(i, partner(i, k, size)) for i in rang...]
    broadcast_in_dim x1 -> x0, local copies, waits for them, and re-layouts: 0.8 us -> none  [per_device(): jnp.broadcast_to(late[None], (n_row * n_col * n_depth,) + late.shape)]
  transfers between devices with their start and end apart: 26 -> 26, of which waited for: 9 -> 8; matrix products, arithmetic and copies ran while one was open for 0% -> 0% of each run, Pallas kernels for 3% -> 17%
where the time goes in v2:
time: 67.6 us; the launch traced here: 67.4 us
  starting transfers between devices  32.9 us (49%)
  Pallas kernels  18.2 us (27%)
  waiting for transfers between devices  14.9 us (22%)
  between operations  1.39 us (2%)
    ppermute x25, starting transfers between devices, send_all(): lax.ppermute(arrays[k - 1], axis, [(i, partner(i, k, size)) for i in rang...  28.8 us
    pallas_call x7, Pallas kernels, call(): pl.pallas_call(body, name=name, out_shape=[s if hasattr(s, 'dtype') else...  18.2 us
    ppermute x25, waiting for transfers between devices, send_all(): lax.ppermute(arrays[k - 1], axis, [(i, partner(i, k, size)) for i in rang...  14.5 us
    all_to_all x1, starting transfers between devices, per_device(): late = lax.all_to_all(late, ('row', 'col', 'depth'), 0, 0)  4.05 us
  transfers between devices with their start and end apart: 26, of which 8 were waited for; matrix products, arithmetic and copies ran while one was open for 0% of the time, Pallas kernels for 17%

profile of v2, /device:TPU:0, one launch (start us, length us, event | category | flops | bytes accessed | tf_op | source)
XLA Modules:
  0.0 67.4 jit_solution(5152315575924743128)
XLA Ops:
  0.6 3.1 %collective-permute-start = (f32[16,512]{1,0:T(8,128)}, f32[16,512]{1,0:T(8,128)S(1)}, u32[]{:S(2)}, u32[]{:S(2)}) collective-permute-start(f32[16,512]{1,0:T(8,128)} %refs_9_.1), channel_id=1, source_target_pairs={{0,8},{8,0},{16,24},{24,16},{1,9},{9,1},{17,25},{25,17},{2,10},{10... | collective-permute-start | bytes 98312 | tf_op jit(solution)/shard_map/ppermute | solution.py:29
  3.7 2.6 %collective-permute-start.1 = (f32[16,512]{1,0:T(8,128)}, f32[16,512]{1,0:T(8,128)S(1)}, u32[]{:S(2)}, u32[]{:S(2)}) collective-permute-start(f32[16,512]{1,0:T(8,128)} %refs_9_.1), channel_id=1, source_target_pairs={{0,16},{8,24},{16,0},{24,8},{1,17},{9,25},{17,1},{25,9},{2,18},{10... | collective-permute-start | bytes 98312 | tf_op jit(solution)/shard_map/ppermute | solution.py:29
  6.3 0.0 collective-permute-start.2
  6.3 1.7 %collective-permute-start.3 = (f32[16,512]{1,0:T(8,128)}, f32[16,512]{1,0:T(8,128)S(1)}, u32[]{:S(2)}, u32[]{:S(2)}) collective-permute-start(f32[16,512]{1,0:T(8,128)} %refs_9_.1), channel_id=1, source_target_pairs={{0,4},{4,0},{1,5},{5,1},{2,6},{6,2},{3,7},{7,3},{8,12},{12,8},{9,1... | collective-permute-start | bytes 98312 | tf_op jit(solution)/shard_map/ppermute | solution.py:29
  8.7 3.0 %prepare.1 = (bf16[16,256,256]{2,1,0:T(8,128)(2,1)S(1)}, bf16[16,256,256]{2,1,0:T(8,128)(2,1)S(1)}, f32[16,512]{1,0:T(8,128)S(1)}, s32[3,16]{1,0:T(4,128)S(1)}) custom-call(s32[1,1]{1,0:T(1,128)S(6)} %copy.7.count_ref, s32[1,1,16]{2,1,0:T(1,128)} %rows_ref.1, s32[1,1,16]{2,1,0:T(1,128)} %cols_ref.1, f32[1,1,16,256,256]{4,3,2,1,0:T(8,128)} %blocks_ref.1, ...), custom_call_target="tpu_custom_call" | custom-call | flops 4194304 | bytes 8388608 | tf_op jit(solution)/shard_map/prepare/pallas_call | solution.py:305
  11.8 0.1 collective-permute-start.10
  11.8 0.0 collective-permute-done.refs_4_
  11.8 1.6 %collective-permute-start.8 = (f32[16,512]{1,0:T(8,128)S(1)}, f32[16,512]{1,0:T(8,128)S(1)}, u32[]{:S(2)}, u32[]{:S(2)}) collective-permute-start(f32[16,512]{1,0:T(8,128)S(1)} %get-tuple-element.33), channel_id=1, source_target_pairs={{0,1},{1,0},{2,3},{3,2},{4,5},{5,4},{6,7},{7,6},{8,9},{9,8},{10,11... | collective-permute-start | bytes 98312 | tf_op jit(solution)/shard_map/ppermute | solution.py:29
  13.4 0.5 collective-permute-start.9
  14.0 0.0 collective-permute-done.2.refs_6_
  14.0 2.3 %first_products.1 = (f32[16,512]{1,0:T(8,128)S(1)}, f32[16,512]{1,0:T(8,128)S(1)}, f32[16,512]{1,0:T(8,128)S(1)}, f32[16,512]{1,0:T(8,128)S(1)}, f32[16,512]{1,0:T(8,128)S(1)}) custom-call(s32[3,16]{1,0:T(4,128)S(1)} %get-tuple-element.25.refs_0_, bf16[16,256,256]{2,1,0:T(8,128)(2,1)S(1)} %get-tuple-element.26.refs_1_, ...), custom_call_target="tpu_custom_call" | custom-call | tf_op jit(solution)/shard_map/first_products/pallas_call | solution.py:305
  16.3 0.7 %collective-permute-start.4 = (f32[16,512]{1,0:T(8,128)S(1)}, f32[16,512]{1,0:T(8,128)S(1)}, u32[]{:S(2)}, u32[]{:S(2)}) collective-permute-start(f32[16,512]{1,0:T(8,128)S(1)} %get-tuple-element.29), channel_id=1, source_target_pairs={{0,8},{8,0},{16,24},{24,16},{1,9},{9,1},{17,25},{25,17},{2,10},{10... | collective-permute-start | bytes 98312 | tf_op jit(solution)/shard_map/ppermute | solution.py:29
  17.0 3.5 %collective-permute-start.5 = (f32[16,512]{1,0:T(8,128)S(1)}, f32[16,512]{1,0:T(8,128)S(1)}, u32[]{:S(2)}, u32[]{:S(2)}) collective-permute-start(f32[16,512]{1,0:T(8,128)S(1)} %get-tuple-element.30), channel_id=1, source_target_pairs={{0,16},{8,24},{16,0},{24,8},{1,17},{9,25},{17,1},{25,9},{2,18},{10... | collective-permute-start | bytes 98312 | tf_op jit(solution)/shard_map/ppermute | solution.py:29
  20.5 0.0 collective-permute-done.10.refs_8_.refs_9_.refs_12_
  20.5 0.2 collective-permute-start.6
  20.7 0.0 collective-permute-done.8.refs_6_.refs_7_.refs_10_
  20.7 0.4 collective-permute-start.7
  21.1 0.0 collective-permute-done.9.refs_7_.refs_8_.refs_11_
  21.1 1.9 %collective-permute-done.5.refs_2_ = f32[16,512]{1,0:T(8,128)S(1)} collective-permute-done((f32[16,512]{1,0:T(8,128)S(1)}, f32[16,512]{1,0:T(8,128)S(1)}, u32[]{:S(2)}, u32[]{:S(2)}) %collective-permute-start.5) | collective-permute-done | bytes 32800 | tf_op jit(solution)/shard_map/ppermute | solution.py:29
  23.0 3.2 %collective-permute-done.6.refs_3_ = f32[16,512]{1,0:T(8,128)S(1)} collective-permute-done((f32[16,512]{1,0:T(8,128)S(1)}, f32[16,512]{1,0:T(8,128)S(1)}, u32[]{:S(2)}, u32[]{:S(2)}) %collective-permute-start.6) | collective-permute-done | bytes 32800 | tf_op jit(solution)/shard_map/ppermute | solution.py:29
  26.2 0.4 first_combine.1
  26.6 0.0 collective-permute-start.11
  26.6 0.5 collective-permute-start.14
  27.2 2.6 %collective-permute-start.12 = (f32[16,512]{1,0:T(8,128)S(1)}, f32[16,512]{1,0:T(8,128)S(1)}, u32[]{:S(2)}, u32[]{:S(2)}) collective-permute-start(f32[16,512]{1,0:T(8,128)S(1)} %get-tuple-element.35.refs_10_.refs_13_), channel_id=1, source_target_pairs={{0,16},{8,24},{16,0},{24,8},{1,17},{9,25},{17,1},{25,9},{2,18},{10... | collective-permute-start | bytes 98312 | tf_op jit(solution)/shard_map/ppermute | solution.py:29
  29.7 1.8 %collective-permute-start.13 = (f32[16,512]{1,0:T(8,128)S(1)}, f32[16,512]{1,0:T(8,128)S(1)}, u32[]{:S(2)}, u32[]{:S(2)}) collective-permute-start(f32[16,512]{1,0:T(8,128)S(1)} %get-tuple-element.35.refs_10_.refs_13_), channel_id=1, source_target_pairs={{0,24},{8,16},{16,8},{24,0},{1,25},{9,17},{17,9},{25,1},{2,26},{10... | collective-permute-start | bytes 98312 | tf_op jit(solution)/shard_map/ppermute | solution.py:29
  31.5 0.0 collective-permute-start.19
  31.5 0.0 collective-permute-done.11.refs_4_
  31.5 1.5 %collective-permute-start.20 = (f32[16,512]{1,0:T(8,128)S(1)}, f32[16,512]{1,0:T(8,128)S(1)}, u32[]{:S(2)}, u32[]{:S(2)}) collective-permute-start(f32[16,512]{1,0:T(8,128)S(1)} %get-tuple-element.35.refs_10_.refs_13_), channel_id=1, source_target_pairs={{0,2},{1,3},{2,0},{3,1},{4,6},{5,7},{6,4},{7,5},{8,10},{9,11},{10,... | collective-permute-start | bytes 98312 | tf_op jit(solution)/shard_map/ppermute | solution.py:29
  33.0 0.0 collective-permute-done.12.refs_5_
  33.0 2.4 %collective-permute-done.13.refs_6_ = f32[16,512]{1,0:T(8,128)S(1)} collective-permute-done((f32[16,512]{1,0:T(8,128)S(1)}, f32[16,512]{1,0:T(8,128)S(1)}, u32[]{:S(2)}, u32[]{:S(2)}) %collective-permute-start.13) | collective-permute-done | bytes 32800 | tf_op jit(solution)/shard_map/ppermute | solution.py:29
  35.5 0.0 collective-permute-done.14.refs_7_
  35.5 2.3 %second_products.1 = (f32[16,512]{1,0:T(8,128)S(1)}, f32[16,128]{1,0:T(8,128)S(1)}, f32[16,640]{1,0:T(8,128)S(1)}, f32[16,640]{1,0:T(8,128)S(1)}, f32[16,640]{1,0:T(8,128)S(1)}, /*index=5*/f32[16,512]{1,0:T(8,128)S(1)}) custom-call(s32[3,16]{1,0:T(4,128)S(1)} %get-tuple-element.25.refs_0_, bf16[16,256,256]{2,1,0:T(8,128)(2,1)S(1)} %get-tuple-element.26.refs_1_, ...), custom_call_target="tpu_custom_call" | custom-call | tf_op jit(solution)/shard_map/second_products/pallas_call | solution.py:305
  37.8 0.1 collective-permute-start.15
  37.8 2.3 %collective-permute-start.16 = (f32[16,640]{1,0:T(8,128)S(1)}, f32[16,640]{1,0:T(8,128)S(1)}, u32[]{:S(2)}, u32[]{:S(2)}) collective-permute-start(f32[16,640]{1,0:T(8,128)S(1)} %get-tuple-element.39), channel_id=1, source_target_pairs={{0,16},{8,24},{16,0},{24,8},{1,17},{9,25},{17,1},{25,9},{2,18},{10... | collective-permute-start | bytes 122888 | tf_op jit(solution)/shard_map/ppermute | solution.py:29
  40.2 2.0 %collective-permute-start.17 = (f32[16,640]{1,0:T(8,128)S(1)}, f32[16,640]{1,0:T(8,128)S(1)}, u32[]{:S(2)}, u32[]{:S(2)}) collective-permute-start(f32[16,640]{1,0:T(8,128)S(1)} %get-tuple-element.40), channel_id=1, source_target_pairs={{0,24},{8,16},{16,8},{24,0},{1,25},{9,17},{17,9},{25,1},{2,26},{10... | collective-permute-start | bytes 122888 | tf_op jit(solution)/shard_map/ppermute | solution.py:29
  42.2 0.0 collective-permute-start.21
  42.2 1.6 %collective-permute-start.18 = (f32[16,512]{1,0:T(8,128)S(1)}, f32[16,512]{1,0:T(8,128)S(1)}, u32[]{:S(2)}, u32[]{:S(2)}) collective-permute-start(f32[16,512]{1,0:T(8,128)S(1)} %get-tuple-element.41), channel_id=1, source_target_pairs={{0,4},{4,0},{1,5},{5,1},{2,6},{6,2},{3,7},{7,3},{8,12},{12,8},{9,1... | collective-permute-start | bytes 98312 | tf_op jit(solution)/shard_map/ppermute | solution.py:29
  43.8 2.0 %collective-permute-done.21.refs_13_.refs_16_ = f32[16,512]{1,0:T(8,128)S(1)} collective-permute-done((f32[16,512]{1,0:T(8,128)S(1)}, f32[16,512]{1,0:T(8,128)S(1)}, u32[]{:S(2)}, u32[]{:S(2)}) %collective-permute-start.21) | collective-permute-done | bytes 32800 | tf_op jit(solution)/shard_map/ppermute | solution.py:29
  45.9 0.3 collective-permute-done.18.refs_5_
  46.2 1.1 %second_combine.1 = (f32[16,640]{1,0:T(8,128)S(1)}, f32[32,16,128]{2,1,0:T(8,128)}) custom-call(f32[16,512]{1,0:T(8,128)S(1)} %get-tuple-element.36.refs_0_, f32[16,128]{1,0:T(8,128)S(1)} %get-tuple-element.37.refs_1_, f32[16,640]{1,0:T(8,128)S(1)} %collective-permute-done.15.refs_2_, f32[16,640]{1,0:T(8,128)S(1)} %collective-permute-done.16.refs_3_, ...), custom_call_target="tpu_custom_call" | custom-call | tf_op jit(solution)/shard_map/second_combine/pallas_call | solution.py:305
  47.4 4.0 %all-to-all-start = ((f32[32,16,128]{2,1,0:T(8,128)}), f32[32,16,128]{2,1,0:T(8,128)S(1)}, u32[]{:S(2)}, u32[]{:S(2)}) async-start(f32[32,16,128]{2,1,0:T(8,128)} %get-tuple-element.42), calls=%async_computation | async-start | bytes 524288 | tf_op jit(solution)/shard_map/all_to_all | solution.py:374
  51.4 0.3 collective-permute-start.22
  51.7 1.6 %collective-permute-start.23 = (f32[16,640]{1,0:T(8,128)S(1)}, f32[16,640]{1,0:T(8,128)S(1)}, u32[]{:S(2)}, u32[]{:S(2)}) collective-permute-start(f32[16,640]{1,0:T(8,128)S(1)} %get-tuple-element.43.refs_0_.refs_5_), channel_id=1, source_target_pairs={{0,2},{1,3},{2,0},{3,1},{4,6},{5,7},{6,4},{7,5},{8,10},{9,11},{10,... | collective-permute-start | bytes 122888 | tf_op jit(solution)/shard_map/ppermute | solution.py:29
  53.4 3.1 %collective-permute-done.23.refs_2_.refs_7_ = f32[16,640]{1,0:T(8,128)S(1)} collective-permute-done((f32[16,640]{1,0:T(8,128)S(1)}, f32[16,640]{1,0:T(8,128)S(1)}, u32[]{:S(2)}, u32[]{:S(2)}) %collective-permute-start.23) | collective-permute-done | bytes 40992 | tf_op jit(solution)/shard_map/ppermute | solution.py:29
  56.5 1.4 %collective-permute-done.24.refs_3_.refs_8_ = f32[16,640]{1,0:T(8,128)S(1)} collective-permute-done((f32[16,640]{1,0:T(8,128)S(1)}, f32[16,640]{1,0:T(8,128)S(1)}, u32[]{:S(2)}, u32[]{:S(2)}) %collective-permute-start.24) | collective-permute-done | bytes 40992 | tf_op jit(solution)/shard_map/ppermute | solution.py:29
  57.9 3.7 %early_solve.1 = (f32[64,64]{1,0:T(8,128)S(1)}, f32[64,64]{1,0:T(8,128)S(1)}, f32[64,64]{1,0:T(8,128)S(1)}, f32[64,64]{1,0:T(8,128)S(1)}) custom-call(f32[16,640]{1,0:T(8,128)S(1)} %get-tuple-element.43.refs_0_.refs_5_, f32[16,640]{1,0:T(8,128)S(1)} %collective-permute-done.22.refs_1_.refs_6_, f32[16,640]{1,0:T(8,128)S(1)} %collective-permute-done.23.refs_2_.refs_7_, ...), custom_call_target="tpu_custom_call" | custom-call | flops 1048576 | bytes 655360 | tf_op jit(solution)/shard_map/early_solve/pallas_call | solution.py:305
  61.6 0.4 all-to-all-done.refs_0_
  62.0 5.4 %finish.1 = (f32[16,512]{1,0:T(8,128)}, f32[16,512]{1,0:T(8,128)}) custom-call(f32[32,16,128]{2,1,0:T(8,128)S(1)} %all-to-all-done.refs_0_, f32[64,64]{1,0:T(8,128)S(1)} %get-tuple-element.44.refs_1_, f32[64,64]{1,0:T(8,128)S(1)} %get-tuple-element.45.refs_2_, f32[64,64]{1,0:T(8,128)S(1)} %get-tuple-element.46.refs_3_, ...), custom_call_target="tpu_custom_call" | custom-call | tf_op jit(solution)/shard_map/finish/pallas_call | solution.py:305
  (13 shorter events, 0.0 us)
Async XLA Ops:
  0.6 11.2 %collective-permute-start = (f32[16,512]{1,0:T(8,128)}, f32[16,512]{1,0:T(8,128)S(1)}, u32[]{:S(2)}, u32[]{:S(2)}) collective-permute-start(f32[16,512]{1,0:T(8,128)} %refs_9_.1), channel_id=1, source_target_pairs={{0,8},{8,0},{16,24},{24,16},{1,9},{9,1},{17,25},{25,17},{2,10},{10... | collective-permute-start | bytes 98312 | tf_op jit(solution)/shard_map/ppermute | solution.py:29
  3.7 9.7 %collective-permute-start.1 = (f32[16,512]{1,0:T(8,128)}, f32[16,512]{1,0:T(8,128)S(1)}, u32[]{:S(2)}, u32[]{:S(2)}) collective-permute-start(f32[16,512]{1,0:T(8,128)} %refs_9_.1), channel_id=1, source_target_pairs={{0,16},{8,24},{16,0},{24,8},{1,17},{9,25},{17,1},{25,9},{2,18},{10... | collective-permute-start | bytes 98312 | tf_op jit(solution)/shard_map/ppermute | solution.py:29
  6.3 7.6 %collective-permute-start.2 = (f32[16,512]{1,0:T(8,128)}, f32[16,512]{1,0:T(8,128)S(1)}, u32[]{:S(2)}, u32[]{:S(2)}) collective-permute-start(f32[16,512]{1,0:T(8,128)} %refs_9_.1), channel_id=1, source_target_pairs={{0,24},{8,16},{16,8},{24,0},{1,25},{9,17},{17,9},{25,1},{2,26},{10... | collective-permute-start | bytes 98312 | tf_op jit(solution)/shard_map/ppermute | solution.py:29
  6.3 7.6 %collective-permute-start.3 = (f32[16,512]{1,0:T(8,128)}, f32[16,512]{1,0:T(8,128)S(1)}, u32[]{:S(2)}, u32[]{:S(2)}) collective-permute-start(f32[16,512]{1,0:T(8,128)} %refs_9_.1), channel_id=1, source_target_pairs={{0,4},{4,0},{1,5},{5,1},{2,6},{6,2},{3,7},{7,3},{8,12},{12,8},{9,1... | collective-permute-start | bytes 98312 | tf_op jit(solution)/shard_map/ppermute | solution.py:29
  8.7 5.2 %copy-start = (f32[16,512]{1,0:T(8,128)S(1)}, f32[16,512]{1,0:T(8,128)}, u32[]{:S(2)}) copy-start(f32[16,512]{1,0:T(8,128)} %refs_9_.1) | copy-start | bytes 98308
  11.8 8.8 %collective-permute-start.10 = (f32[16,512]{1,0:T(8,128)S(1)}, f32[16,512]{1,0:T(8,128)S(1)}, u32[]{:S(2)}, u32[]{:S(2)}) collective-permute-start(f32[16,512]{1,0:T(8,128)S(1)} %get-tuple-element.33), channel_id=1, source_target_pairs={{0,3},{1,2},{2,1},{3,0},{4,7},{5,6},{6,5},{7,4},{8,11},{9,10},{10,... | collective-permute-start | bytes 98312 | tf_op jit(solution)/shard_map/ppermute | solution.py:29
  11.8 8.9 %collective-permute-start.8 = (f32[16,512]{1,0:T(8,128)S(1)}, f32[16,512]{1,0:T(8,128)S(1)}, u32[]{:S(2)}, u32[]{:S(2)}) collective-permute-start(f32[16,512]{1,0:T(8,128)S(1)} %get-tuple-element.33), channel_id=1, source_target_pairs={{0,1},{1,0},{2,3},{3,2},{4,5},{5,4},{6,7},{7,6},{8,9},{9,8},{10,11... | collective-permute-start | bytes 98312 | tf_op jit(solution)/shard_map/ppermute | solution.py:29
  13.4 7.7 %collective-permute-start.9 = (f32[16,512]{1,0:T(8,128)S(1)}, f32[16,512]{1,0:T(8,128)S(1)}, u32[]{:S(2)}, u32[]{:S(2)}) collective-permute-start(f32[16,512]{1,0:T(8,128)S(1)} %get-tuple-element.33), channel_id=1, source_target_pairs={{0,2},{1,3},{2,0},{3,1},{4,6},{5,7},{6,4},{7,5},{8,10},{9,11},{10,... | collective-permute-start | bytes 98312 | tf_op jit(solution)/shard_map/ppermute | solution.py:29
  16.3 4.8 %collective-permute-start.4 = (f32[16,512]{1,0:T(8,128)S(1)}, f32[16,512]{1,0:T(8,128)S(1)}, u32[]{:S(2)}, u32[]{:S(2)}) collective-permute-start(f32[16,512]{1,0:T(8,128)S(1)} %get-tuple-element.29), channel_id=1, source_target_pairs={{0,8},{8,0},{16,24},{24,16},{1,9},{9,1},{17,25},{25,17},{2,10},{10... | collective-permute-start | bytes 98312 | tf_op jit(solution)/shard_map/ppermute | solution.py:29
  17.0 6.0 %collective-permute-start.5 = (f32[16,512]{1,0:T(8,128)S(1)}, f32[16,512]{1,0:T(8,128)S(1)}, u32[]{:S(2)}, u32[]{:S(2)}) collective-permute-start(f32[16,512]{1,0:T(8,128)S(1)} %get-tuple-element.30), channel_id=1, source_target_pairs={{0,16},{8,24},{16,0},{24,8},{1,17},{9,25},{17,1},{25,9},{2,18},{10... | collective-permute-start | bytes 98312 | tf_op jit(solution)/shard_map/ppermute | solution.py:29
  20.5 5.7 %collective-permute-start.6 = (f32[16,512]{1,0:T(8,128)S(1)}, f32[16,512]{1,0:T(8,128)S(1)}, u32[]{:S(2)}, u32[]{:S(2)}) collective-permute-start(f32[16,512]{1,0:T(8,128)S(1)} %get-tuple-element.31), channel_id=1, source_target_pairs={{0,24},{8,16},{16,8},{24,0},{1,25},{9,17},{17,9},{25,1},{2,26},{10... | collective-permute-start | bytes 98312 | tf_op jit(solution)/shard_map/ppermute | solution.py:29
  20.7 5.5 %collective-permute-start.7 = (f32[16,512]{1,0:T(8,128)S(1)}, f32[16,512]{1,0:T(8,128)S(1)}, u32[]{:S(2)}, u32[]{:S(2)}) collective-permute-start(f32[16,512]{1,0:T(8,128)S(1)} %get-tuple-element.32), channel_id=1, source_target_pairs={{0,4},{4,0},{1,5},{5,1},{2,6},{6,2},{3,7},{7,3},{8,12},{12,8},{9,1... | collective-permute-start | bytes 98312 | tf_op jit(solution)/shard_map/ppermute | solution.py:29
  26.6 4.9 %collective-permute-start.11 = (f32[16,512]{1,0:T(8,128)S(1)}, f32[16,512]{1,0:T(8,128)S(1)}, u32[]{:S(2)}, u32[]{:S(2)}) collective-permute-start(f32[16,512]{1,0:T(8,128)S(1)} %get-tuple-element.35.refs_10_.refs_13_), channel_id=1, source_target_pairs={{0,8},{8,0},{16,24},{24,16},{1,9},{9,1},{17,25},{25,17},{2,10},{10... | collective-permute-start | bytes 98312 | tf_op jit(solution)/shard_map/ppermute | solution.py:29
  26.6 8.8 %collective-permute-start.14 = (f32[16,640]{1,0:T(8,128)S(1)}, f32[16,640]{1,0:T(8,128)S(1)}, u32[]{:S(2)}, u32[]{:S(2)}) collective-permute-start(f32[16,640]{1,0:T(8,128)S(1)} %get-tuple-element.34.refs_3_), channel_id=1, source_target_pairs={{0,4},{4,0},{1,5},{5,1},{2,6},{6,2},{3,7},{7,3},{8,12},{12,8},{9,1... | collective-permute-start | bytes 122888 | tf_op jit(solution)/shard_map/ppermute | solution.py:29
  27.2 5.9 %collective-permute-start.12 = (f32[16,512]{1,0:T(8,128)S(1)}, f32[16,512]{1,0:T(8,128)S(1)}, u32[]{:S(2)}, u32[]{:S(2)}) collective-permute-start(f32[16,512]{1,0:T(8,128)S(1)} %get-tuple-element.35.refs_10_.refs_13_), channel_id=1, source_target_pairs={{0,16},{8,24},{16,0},{24,8},{1,17},{9,25},{17,1},{25,9},{2,18},{10... | collective-permute-start | bytes 98312 | tf_op jit(solution)/shard_map/ppermute | solution.py:29
  29.7 5.7 %collective-permute-start.13 = (f32[16,512]{1,0:T(8,128)S(1)}, f32[16,512]{1,0:T(8,128)S(1)}, u32[]{:S(2)}, u32[]{:S(2)}) collective-permute-start(f32[16,512]{1,0:T(8,128)S(1)} %get-tuple-element.35.refs_10_.refs_13_), channel_id=1, source_target_pairs={{0,24},{8,16},{16,8},{24,0},{1,25},{9,17},{17,9},{25,1},{2,26},{10... | collective-permute-start | bytes 98312 | tf_op jit(solution)/shard_map/ppermute | solution.py:29
  31.5 10.7 %collective-permute-start.19 = (f32[16,512]{1,0:T(8,128)S(1)}, f32[16,512]{1,0:T(8,128)S(1)}, u32[]{:S(2)}, u32[]{:S(2)}) collective-permute-start(f32[16,512]{1,0:T(8,128)S(1)} %get-tuple-element.35.refs_10_.refs_13_), channel_id=1, source_target_pairs={{0,1},{1,0},{2,3},{3,2},{4,5},{5,4},{6,7},{7,6},{8,9},{9,8},{10,11... | collective-permute-start | bytes 98312 | tf_op jit(solution)/shard_map/ppermute | solution.py:29
  31.5 10.7 %collective-permute-start.20 = (f32[16,512]{1,0:T(8,128)S(1)}, f32[16,512]{1,0:T(8,128)S(1)}, u32[]{:S(2)}, u32[]{:S(2)}) collective-permute-start(f32[16,512]{1,0:T(8,128)S(1)} %get-tuple-element.35.refs_10_.refs_13_), channel_id=1, source_target_pairs={{0,2},{1,3},{2,0},{3,1},{4,6},{5,7},{6,4},{7,5},{8,10},{9,11},{10,... | collective-permute-start | bytes 98312 | tf_op jit(solution)/shard_map/ppermute | solution.py:29
  37.8 8.4 %collective-permute-start.15 = (f32[16,640]{1,0:T(8,128)S(1)}, f32[16,640]{1,0:T(8,128)S(1)}, u32[]{:S(2)}, u32[]{:S(2)}) collective-permute-start(f32[16,640]{1,0:T(8,128)S(1)} %get-tuple-element.38), channel_id=1, source_target_pairs={{0,8},{8,0},{16,24},{24,16},{1,9},{9,1},{17,25},{25,17},{2,10},{10... | collective-permute-start | bytes 122888 | tf_op jit(solution)/shard_map/ppermute | solution.py:29
  37.8 8.4 %collective-permute-start.16 = (f32[16,640]{1,0:T(8,128)S(1)}, f32[16,640]{1,0:T(8,128)S(1)}, u32[]{:S(2)}, u32[]{:S(2)}) collective-permute-start(f32[16,640]{1,0:T(8,128)S(1)} %get-tuple-element.39), channel_id=1, source_target_pairs={{0,16},{8,24},{16,0},{24,8},{1,17},{9,25},{17,1},{25,9},{2,18},{10... | collective-permute-start | bytes 122888 | tf_op jit(solution)/shard_map/ppermute | solution.py:29
  40.2 6.0 %collective-permute-start.17 = (f32[16,640]{1,0:T(8,128)S(1)}, f32[16,640]{1,0:T(8,128)S(1)}, u32[]{:S(2)}, u32[]{:S(2)}) collective-permute-start(f32[16,640]{1,0:T(8,128)S(1)} %get-tuple-element.40), channel_id=1, source_target_pairs={{0,24},{8,16},{16,8},{24,0},{1,25},{9,17},{17,9},{25,1},{2,26},{10... | collective-permute-start | bytes 122888 | tf_op jit(solution)/shard_map/ppermute | solution.py:29
  42.2 3.6 %collective-permute-start.21 = (f32[16,512]{1,0:T(8,128)S(1)}, f32[16,512]{1,0:T(8,128)S(1)}, u32[]{:S(2)}, u32[]{:S(2)}) collective-permute-start(f32[16,512]{1,0:T(8,128)S(1)} %get-tuple-element.35.refs_10_.refs_13_), channel_id=1, source_target_pairs={{0,3},{1,2},{2,1},{3,0},{4,7},{5,6},{6,5},{7,4},{8,11},{9,10},{10,... | collective-permute-start | bytes 98312 | tf_op jit(solution)/shard_map/ppermute | solution.py:29
  42.2 4.0 %collective-permute-start.18 = (f32[16,512]{1,0:T(8,128)S(1)}, f32[16,512]{1,0:T(8,128)S(1)}, u32[]{:S(2)}, u32[]{:S(2)}) collective-permute-start(f32[16,512]{1,0:T(8,128)S(1)} %get-tuple-element.41), channel_id=1, source_target_pairs={{0,4},{4,0},{1,5},{5,1},{2,6},{6,2},{3,7},{7,3},{8,12},{12,8},{9,1... | collective-permute-start | bytes 98312 | tf_op jit(solution)/shard_map/ppermute | solution.py:29
  47.4 14.6 %all-to-all-start = ((f32[32,16,128]{2,1,0:T(8,128)}), f32[32,16,128]{2,1,0:T(8,128)S(1)}, u32[]{:S(2)}, u32[]{:S(2)}) async-start(f32[32,16,128]{2,1,0:T(8,128)} %get-tuple-element.42), calls=%async_computation | async-start | bytes 524288 | tf_op jit(solution)/shard_map/all_to_all | solution.py:374
  51.4 2.0 %collective-permute-start.22 = (f32[16,640]{1,0:T(8,128)S(1)}, f32[16,640]{1,0:T(8,128)S(1)}, u32[]{:S(2)}, u32[]{:S(2)}) collective-permute-start(f32[16,640]{1,0:T(8,128)S(1)} %get-tuple-element.43.refs_0_.refs_5_), channel_id=1, source_target_pairs={{0,1},{1,0},{2,3},{3,2},{4,5},{5,4},{6,7},{7,6},{8,9},{9,8},{10,11... | collective-permute-start | bytes 122888 | tf_op jit(solution)/shard_map/ppermute | solution.py:29
  51.7 4.8 %collective-permute-start.23 = (f32[16,640]{1,0:T(8,128)S(1)}, f32[16,640]{1,0:T(8,128)S(1)}, u32[]{:S(2)}, u32[]{:S(2)}) collective-permute-start(f32[16,640]{1,0:T(8,128)S(1)} %get-tuple-element.43.refs_0_.refs_5_), channel_id=1, source_target_pairs={{0,2},{1,3},{2,0},{3,1},{4,6},{5,7},{6,4},{7,5},{8,10},{9,11},{10,... | collective-permute-start | bytes 122888 | tf_op jit(solution)/shard_map/ppermute | solution.py:29
  53.4 4.6 %collective-permute-start.24 = (f32[16,640]{1,0:T(8,128)S(1)}, f32[16,640]{1,0:T(8,128)S(1)}, u32[]{:S(2)}, u32[]{:S(2)}) collective-permute-start(f32[16,640]{1,0:T(8,128)S(1)} %get-tuple-element.43.refs_0_.refs_5_), channel_id=1, source_target_pairs={{0,3},{1,2},{2,1},{3,0},{4,7},{5,6},{6,5},{7,4},{8,11},{9,10},{10,... | collective-permute-start | bytes 122888 | tf_op jit(solution)/shard_map/ppermute | solution.py:29

commit v3 on v2

--- a/solution.py
+++ b/solution.py
@@ -7,6 +7,7 @@
 from jax.experimental.pallas import tpu as pltpu
 from jax.sharding import PartitionSpec as P
 
+
 BLK = 256
 SEG = 2
 HIGHEST = lax.Precision.HIGHEST
@@ -19,16 +20,29 @@
     return index ^ step if size & (size - 1) == 0 else (index + step) % size
 
 
-def source(index, step, size):
-    return index ^ step if size & (size - 1) == 0 else (index + size - step) % size
+def power_of_two(n):
+    return n & (n - 1) == 0
 
 
 def send_all(arrays, axis):
     size = lax.axis_size(axis)
-    return [
-        lax.ppermute(arrays[k - 1], axis, [(i, partner(i, k, size)) for i in range(size)])
-        for k in range(1, size)
-    ]
+    return [send(arrays[k - 1], axis, k) for k in range(1, size)]
+
+
+def send(x, axis, step):
+    size = lax.axis_size(axis)
+    return lax.ppermute(x, axis, [(i, partner(i, step, size)) for i in range(size)])
+
+
+def collect(x, axis):
+    size = lax.axis_size(axis)
+    if not power_of_two(size):
+        return send_all([x] * (size - 1), axis)
+    held = {0: x}
+    for k in sorted(range(1, size), key=lambda k: (k.bit_count(), -k)):
+        low = k & -k
+        held[k] = send(held[k - low], axis, low)
+    return [held[k] for k in range(1, size)]
 
 
 def source_of(axis, step):
@@ -73,30 +87,27 @@
         all_ref[pl.ds(pl.multiple_of(place * width, width), width), :] = ref[:, 0:points]
 
 
-def prepare(
-    count_ref, rows_ref, cols_ref, blocks_ref, fields_ref, high_out, low_out, fields_out, table_out,
-    landed, rows_at, cols_at, sems,
-):
+def prepare(count_ref, rows_ref, cols_ref, blocks_ref, blocks_out, table_out, rows_at, cols_at, sems):
     slots = blocks_ref.shape[2]
-    copies = [pltpu.make_async_copy(blocks_ref.at[0, 0, s], landed.at[s], sems.at[s]) for s in range(slots)]
-    copies.append(pltpu.make_async_copy(rows_ref, rows_at, sems.at[slots]))
-    copies.append(pltpu.make_async_copy(cols_ref, cols_at, sems.at[slots + 1]))
-    copies.append(pltpu.make_async_copy(fields_ref, fields_out, sems.at[slots + 2]))
-    for copy in copies:
+    copies = [pltpu.make_async_copy(blocks_ref.at[0, 0, s], blocks_out.at[s], sems.at[s]) for s in range(slots)]
+    small = [
+        pltpu.make_async_copy(rows_ref, rows_at, sems.at[slots]),
+        pltpu.make_async_copy(cols_ref, cols_at, sems.at[slots + 1]),
+    ]
+    for copy in small + copies:
         copy.start()
-    for slot in range(slots):
-        copies[slot].wait()
-        high_out[slot], low_out[slot] = halves(landed[slot])
-    for copy in copies[slots:]:
+    for copy in small:
         copy.wait()
     for slot in range(slots):
         table_out[0, slot] = rows_at[0, 0, slot]
         table_out[1, slot] = cols_at[0, 0, slot]
         table_out[2, slot] = count_ref[0, 0]
+    for copy in copies:
+        copy.wait()
 
 
 def products(
-    n_row, n_col, table_ref, high_ref, low_ref, own_ref, z_refs, y_refs, own_out, z_outs, y_outs,
+    table_ref, blocks_ref, own_ref, z_refs, y_refs, own_out, z_outs, y_outs,
     col_in, row_in, col_acc, row_acc,
 ):
     width = own_ref.shape[0]
@@ -110,8 +121,8 @@
     col_acc[...] = jnp.zeros_like(col_acc)
     row_acc[...] = jnp.zeros_like(row_acc)
     count = table_ref[2, 0]
-    for slot in range(high_ref.shape[0]):
-        high, low = high_ref[slot], low_ref[slot]
+    for slot in range(blocks_ref.shape[0]):
+        high, low = halves(blocks_ref[slot])
         row_place, col_place = table_ref[0, slot], table_ref[1, slot]
         live = slot < count
         for vec, acc, at_in, at_out, contract in (
@@ -143,32 +154,38 @@
 
 def first_products(n_row, n_col, *refs):
     (head, own, z_in, y_in, outs, z_outs, y_outs, scratch) = split(
-        refs, 3, 1, n_row - 1, n_col - 1, 1, n_row - 1, n_col - 1, 4
-    )
-    products(n_row, n_col, *head, own[0], z_in, y_in, outs[0], z_outs, y_outs, *scratch)
-
-
-def first_combine(n_row, n_col, n_depth, *refs):
-    partial, z_in, y_in, field_refs, out, out_wide, fields = split(refs, 1, n_row - 1, n_col - 1, n_depth, 1, 1, 1)
-    points = partial[0].shape[1]
+        refs, 2, 1, n_row - 1, n_col - 1, 2, n_row - 1, n_col - 1, 4
+    )
+    outs[1][...] = own[0][...]
+    products(*head, own[0], z_in, y_in, outs[0], z_outs, y_outs, *scratch)
+
+
+def first_combine(n_row, n_col, *refs):
+    partial, received, out = split(refs, 1, n_row + n_col - 2, 1)
     total = partial[0][...]
-    for ref in z_in + y_in:
+    for ref in received:
         total += ref[...]
+    out[0][...] = total
+
+
+def first_grams(n_depth, *refs):
+    image, field_refs, out, fields = split(refs, 1, n_depth, 1, 1)
+    total = image[0][...]
+    points = total.shape[1]
     stack_fields(fields[0], field_refs[0], field_refs[1:])
     everything = fields[0][...]
-    out[0][...] = total
-    out_wide[0][:, :points] = total
-    out_wide[0][:, points:] = jnp.concatenate(
+    out[0][:, :points] = total
+    out[0][:, points:] = jnp.concatenate(
         [dot_nt(field_refs[0][...], everything), dot_nt(total, everything)], axis=1
     )
 
 
 def second_products(n_row, n_col, *refs):
     (head, own, z_in, y_in, outs, z_outs, y_outs, scratch) = split(
-        refs, 3, 1, n_row - 1, n_col - 1, 2, n_row - 1, n_col - 1, 4
+        refs, 2, 1, n_row - 1, n_col - 1, 2, n_row - 1, n_col - 1, 4
     )
     points = outs[0].shape[1]
-    products(n_row, n_col, *head, own[0], z_in, y_in, outs[0], z_outs, y_outs, *scratch)
+    products(*head, own[0], z_in, y_in, outs[0], z_outs, y_outs, *scratch)
     grams = own[0][:, points:]
     for ref in y_in:
         grams += ref[:, points:]
@@ -247,32 +264,27 @@
 
 
 def early_solve(n_depth, points, *refs):
-    wide_refs, outs, scratch = split(refs, n_depth, 4, 1)
+    wide_refs, outs, scratch = split(refs, n_depth, 3, 1)
     width = wide_refs[0].shape[0]
+    size = n_depth * width
     for step, ref in enumerate(wide_refs):
         place = source_of("depth", step)
-        scratch[0][pl.ds(pl.multiple_of(place * width, width), width), :] = ref[:, points:]
-    early = scratch[0][...]
-    size = n_depth * width
-    gram0, gram1 = early[:, :size], early[:, size:]
-    first, inverse = eliminate(
-        [jnp.concatenate([gram1, gram0], axis=1), jnp.concatenate([gram0, identity_of(size)], axis=1)]
-    )
-    step1 = first[:, size:]
-    coupling = dot_nn(gram1, step1)
-    outs[0][...] = step1
-    outs[1][...] = inverse[:, size:]
-    outs[2][...] = gram0 - coupling - coupling.T
-    outs[3][...] = gram1
+        scratch[0][pl.ds(pl.multiple_of(place * width, width), width), :] = ref[:, points + size : points + 2 * size]
+    gram1 = scratch[0][...]
+    (first,) = eliminate([jnp.concatenate([gram1, identity_of(size)], axis=1)])
+    inverse = first[:, size:]
+    outs[0][...] = inverse
+    outs[1][...] = dot_nt(inverse, wide_refs[0][:, points : points + size])
+    outs[2][...] = dot_nt(identity_of(size), wide_refs[0][:, points + size : points + 2 * size])
 
 
 def finish(n_depth, *refs):
     gathered, solved, wide_refs, base_refs, image_refs, outs, scratch = split(
-        refs, 1, 4, n_depth, n_depth, n_depth, 2, 3
+        refs, 1, 3, n_depth, n_depth, n_depth, 2, 3
     )
     base, image, mapped = scratch
     solution_out, residual_out = outs
-    width, points = solution_out.shape
+    width, _ = solution_out.shape
     size = n_depth * width
     groups = gathered[0].shape[0] // n_depth
     stack_fields(base, base_refs[0], base_refs[1:])
@@ -281,30 +293,22 @@
     late = [sum(gathered[0][g * n_depth + d] for g in range(groups)) for d in range(n_depth)]
     late = jnp.concatenate(late, axis=0)
     gram2, gram3 = late[:, :size], late[:, size:]
-    step1, inverse, rest, gram1 = (ref[...] for ref in solved)
-    product = dot_nn(gram2, step1)
-    renewed = rest + dot_tn(step1, product)
-    blend = identity_of(size) + dot_nn(inverse, renewed)
-    upper = dot_nn(gram1, blend) - product
-    lower = dot_nn(gram2, blend) - dot_nn(gram3, step1)
-    curvature = dot_tn(blend, upper) - dot_tn(step1, lower)
-    (second,) = eliminate([jnp.concatenate([curvature, renewed], axis=1)])
-    own = lax.axis_index("depth") * width
-    pick = (
-        lax.broadcasted_iota(jnp.int32, (size, width), 0) == lax.broadcasted_iota(jnp.int32, (size, width), 1) + own
-    ).astype(jnp.float32)
-    step2 = dot_nn(second[:, size:], pick)
-    weight0 = dot_nn(step1, pick) + dot_nn(blend, step2)
-    weight1 = -dot_nn(step1, step2)
+    inverse, start, gram1_own = (ref[...] for ref in solved)
+    carry = dot_nn(inverse, gram2)
+    schur = gram3 - dot_nn(gram2, carry)
+    right = gram1_own - dot_nn(gram2, start)
+    fill = jnp.zeros((size, size - width), jnp.float32)
+    (second,) = eliminate([jnp.concatenate([schur, right, fill], axis=1)])
+    weight1 = second[:, size : size + width]
+    weight0 = start - dot_nn(carry, weight1)
     base_all, image_all = base[...], image[...]
     solution_out[...] = dot_tn(weight0, base_all) + dot_tn(weight1, image_all)
     residual_out[...] = base_refs[0][...] - dot_tn(weight0, image_all) - dot_tn(weight1, mapped[...])
 
 
-def call(body, name, operands, in_specs, out_shapes, scratch, cost=None, out_specs=None):
+def call(body, operands, in_specs, out_shapes, scratch, cost=None, out_specs=None):
     return pl.pallas_call(
         body,
-        name=name,
         out_shape=[s if hasattr(s, "dtype") else jax.ShapeDtypeStruct(s, jnp.float32) for s in out_shapes],
         in_specs=list(in_specs) + [VMEM] * (len(operands) - len(in_specs)),
         out_specs=out_specs or [VMEM] * len(out_shapes),
@@ -331,35 +335,30 @@
 
     y = send_all([right_sides] * (n_col - 1), "col")
     z = send_all([right_sides] * (n_row - 1), "row")
-    half = jax.ShapeDtypeStruct(blocks.shape[2:], b16)
-    high, low, fields_copy, table = call(
-        prepare, "prepare",
-        [block_count]
-        + [pltpu.with_memory_space_constraint(x, pltpu.HBM) for x in (block_rows, block_cols, blocks, right_sides)],
-        [SMEM] + [pl.BlockSpec(memory_space=pltpu.HBM)] * 4,
-        [half, half, narrow, jax.ShapeDtypeStruct((3, slots), jnp.int32)],
-        [pltpu.VMEM(blocks.shape[2:], f32)]
-        + [pltpu.SMEM(block_rows.shape, jnp.int32)] * 2 + [pltpu.SemaphoreType.DMA((slots + 3,))],
-        pl.CostEstimate(flops=4 * blocks.size, transcendentals=0, bytes_accessed=8 * blocks.size),
-        [VMEM] * 3 + [SMEM],
-    )
-    head = [table, high, low]
-    base = [right_sides] + send_all([fields_copy] * (n_depth - 1), "depth")
-    partial, *rest = call(
-        functools.partial(first_products, n_row, n_col), "first_products",
-        head + [right_sides] + z + y, [SMEM], [narrow] * (n_row + n_col - 1), work,
+    near, table = call(
+        prepare,
+        [block_count] + [pltpu.with_memory_space_constraint(x, pltpu.HBM) for x in (block_rows, block_cols, blocks)],
+        [SMEM] + [pl.BlockSpec(memory_space=pltpu.HBM)] * 3,
+        [blocks.shape[2:], jax.ShapeDtypeStruct((3, slots), jnp.int32)],
+        [pltpu.SMEM(block_rows.shape, jnp.int32)] * 2 + [pltpu.SemaphoreType.DMA((slots + 2,))],
+        pl.CostEstimate(flops=0, transcendentals=0, bytes_accessed=8 * blocks.size),
+        [VMEM, SMEM],
+    )
+    head = [table, near]
+    partial, copied, *rest = call(
+        functools.partial(first_products, n_row, n_col),
+        head + [right_sides] + z + y, [SMEM], [narrow] * (n_row + n_col), work,
     )
     y = send_all(rest[n_row - 1 :], "col")
     z = send_all(rest[: n_row - 1], "row")
-    image, image_wide = call(
-        functools.partial(first_combine, n_row, n_col, n_depth), "first_combine",
-        [partial] + z + y + base, [], [narrow, wide], [fields],
-    )
+    base = [right_sides] + collect(copied, "depth")
+    (image,) = call(functools.partial(first_combine, n_row, n_col), [partial] + z + y, [], [narrow], [])
+    z = send_all([image] * (n_row - 1), "row")
+    (image_wide,) = call(functools.partial(first_grams, n_depth), [image] + base, [], [wide], [fields])
     y = send_all([image_wide] * (n_col - 1), "col")
-    z = send_all([image] * (n_row - 1), "row")
-    image = [image] + send_all([image] * (n_depth - 1), "depth")
+    image = [image] + collect(image, "depth")
     partial, gram, *rest = call(
-        functools.partial(second_products, n_row, n_col), "second_products",
+        functools.partial(second_products, n_row, n_col),
         head + [image_wide] + z + y, [SMEM],
         [narrow, tail] + [wide] * (n_row - 1) + [narrow] * (n_col - 1), work,
     )
@@ -367,18 +366,18 @@
     z = send_all(rest[: n_row - 1], "row")
     n_all = n_row * n_col * n_depth
     mapped, late = call(
-        functools.partial(second_combine, n_row, n_col, n_depth), "second_combine",
+        functools.partial(second_combine, n_row, n_col, n_depth),
         [partial, gram] + z + y + base + image, [], [wide, (n_all,) + tail], [fields],
     )
-    mapped = [mapped] + send_all([mapped] * (n_depth - 1), "depth")
+    mapped = [mapped] + collect(mapped, "depth")
     late = lax.all_to_all(late, ("row", "col", "depth"), 0, 0)
     solved = call(
-        functools.partial(early_solve, n_depth, points), "early_solve", mapped, [], [square] * 4,
-        [pltpu.VMEM((size, 2 * size), f32)],
+        functools.partial(early_solve, n_depth, points), mapped, [],
+        [square, (size, width), (size, width)], [pltpu.VMEM(square, f32)],
         pl.CostEstimate(flops=4 * size**3, transcendentals=0, bytes_accessed=160 * size * size),
     )
     solution, residual = call(
-        functools.partial(finish, n_depth), "finish",
+        functools.partial(finish, n_depth),
         [late] + list(solved) + mapped + base + image, [], [narrow, narrow], [fields, fields, fields],
     )
     return solution, residual

time: 67.6 us -> 65.4 us (0.967)
  Pallas kernels: 18.2 us -> 17.2 us
  starting transfers between devices: 32.9 us -> 31.9 us
    pallas_call x7 -> x8, Pallas kernels: 18.2 us -> 17.2 us  [call(): pl.pallas_call(body, out_shape=[s if hasattr(s, 'dtype') else jax.ShapeDt...]
    all_to_all x1, starting transfers between devices: 4.05 us -> 3.13 us  [per_device(): late = lax.all_to_all(late, ('row', 'col', 'depth'), 0, 0)]
    ppermute x25, waiting for transfers between devices: 14.5 us -> 13.7 us  [send(): lax.ppermute(x, axis, [(i, partner(i, step, size)) for i in range(size)])]
  transfers between devices with their start and end apart: 26 -> 26, of which waited for: 8 -> 8; matrix products, arithmetic and copies ran while one was open for 0% -> 0% of each run, Pallas kernels for 17% -> 14%
where the time goes in v3:
time: 65.4 us; the launch traced here: 65.2 us
  starting transfers between devices  31.9 us (49%)
  Pallas kernels  17.2 us (26%)
  waiting for transfers between devices  14.7 us (22%)
  between operations  1.41 us (2%)
    ppermute x25, starting transfers between devices, send(): lax.ppermute(x, axis, [(i, partner(i, step, size)) for i in range(size)])  28.8 us
    pallas_call x8, Pallas kernels, call(): pl.pallas_call(body, out_shape=[s if hasattr(s, 'dtype') else jax.ShapeDt...  17.2 us
    ppermute x25, waiting for transfers between devices, send(): lax.ppermute(x, axis, [(i, partner(i, step, size)) for i in range(size)])  13.7 us
    all_to_all x1, starting transfers between devices, per_device(): late = lax.all_to_all(late, ('row', 'col', 'depth'), 0, 0)  3.13 us
  transfers between devices with their start and end apart: 26, of which 8 were waited for; matrix products, arithmetic and copies ran while one was open for 0% of the time, Pallas kernels for 14%

profile of v3, /device:TPU:0, one launch (start us, length us, event | category | flops | bytes accessed | tf_op | source)
XLA Modules:
  0.0 65.2 jit_solution(15461873383866406513)
XLA Ops:
  0.6 3.1 %collective-permute-start = (f32[16,512]{1,0:T(8,128)}, f32[16,512]{1,0:T(8,128)S(1)}, u32[]{:S(2)}, u32[]{:S(2)}) collective-permute-start(f32[16,512]{1,0:T(8,128)} %refs_8_.1), channel_id=1, source_target_pairs={{0,8},{8,0},{16,24},{24,16},{1,9},{9,1},{17,25},{25,17},{2,10},{10... | collective-permute-start | bytes 98312 | tf_op jit(solution)/shard_map/ppermute | solution.py:34
  3.8 2.6 %collective-permute-start.1 = (f32[16,512]{1,0:T(8,128)}, f32[16,512]{1,0:T(8,128)S(1)}, u32[]{:S(2)}, u32[]{:S(2)}) collective-permute-start(f32[16,512]{1,0:T(8,128)} %refs_8_.1), channel_id=1, source_target_pairs={{0,16},{8,24},{16,0},{24,8},{1,17},{9,25},{17,1},{25,9},{2,18},{10... | collective-permute-start | bytes 98312 | tf_op jit(solution)/shard_map/ppermute | solution.py:34
  6.4 1.7 %collective-permute-start.3 = (f32[16,512]{1,0:T(8,128)}, f32[16,512]{1,0:T(8,128)S(1)}, u32[]{:S(2)}, u32[]{:S(2)}) collective-permute-start(f32[16,512]{1,0:T(8,128)} %refs_8_.1), channel_id=1, source_target_pairs={{0,4},{4,0},{1,5},{5,1},{2,6},{6,2},{3,7},{7,3},{8,12},{12,8},{9,1... | collective-permute-start | bytes 98312 | tf_op jit(solution)/shard_map/ppermute | solution.py:34
  8.7 2.9 %shard_map.68 = (f32[16,256,256]{2,1,0:T(8,128)S(1)}, s32[3,16]{1,0:T(4,128)S(1)}) custom-call(s32[1,1]{1,0:T(1,128)S(6)} %copy.7.count_ref, s32[1,1,16]{2,1,0:T(1,128)} %rows_ref.1, s32[1,1,16]{2,1,0:T(1,128)} %cols_ref.1, f32[1,1,16,256,256]{4,3,2,1,0:T(8,128)} %blocks_ref.1), custom_call_target="tpu_custom_call" | custom-call | bytes 8388608 | tf_op jit(solution)/shard_map/pallas_call | solution.py:310
  11.7 0.0 collective-permute-done.refs_3_
  11.7 0.0 collective-permute-done.1.refs_4_
  11.7 0.6 collective-permute-done.2.refs_5_
  12.3 0.0 collective-permute-done.3.refs_6_
  12.3 2.3 %shard_map.69 = (f32[16,512]{1,0:T(8,128)S(1)}, f32[16,512]{1,0:T(8,128)S(1)}, f32[16,512]{1,0:T(8,128)S(1)}, f32[16,512]{1,0:T(8,128)S(1)}, f32[16,512]{1,0:T(8,128)S(1)}, /*index=5*/f32[16,512]{1,0:T(8,128)S(1)}) custom-call(s32[3,16]{1,0:T(4,128)S(1)} %get-tuple-element.21.refs_0_, f32[16,256,256]{2,1,0:T(8,128)S(1)} %get-tuple-element.22.refs_1_, ...), custom_call_target="tpu_custom_call" | custom-call | tf_op jit(solution)/shard_map/pallas_call | solution.py:310
  14.6 0.2 collective-permute-start.4
  14.8 1.5 %collective-permute-start.9 = (f32[16,512]{1,0:T(8,128)S(1)}, f32[16,512]{1,0:T(8,128)S(1)}, u32[]{:S(2)}, u32[]{:S(2)}) collective-permute-start(f32[16,512]{1,0:T(8,128)S(1)} %get-tuple-element.28), channel_id=1, source_target_pairs={{0,2},{1,3},{2,0},{3,1},{4,6},{5,7},{6,4},{7,5},{8,10},{9,11},{10,... | collective-permute-start | bytes 98312 | tf_op jit(solution)/shard_map/ppermute | solution.py:34
  16.3 3.5 %collective-permute-start.5 = (f32[16,512]{1,0:T(8,128)S(1)}, f32[16,512]{1,0:T(8,128)S(1)}, u32[]{:S(2)}, u32[]{:S(2)}) collective-permute-start(f32[16,512]{1,0:T(8,128)S(1)} %get-tuple-element.25), channel_id=1, source_target_pairs={{0,16},{8,24},{16,0},{24,8},{1,17},{9,25},{17,1},{25,9},{2,18},{10... | collective-permute-start | bytes 98312 | tf_op jit(solution)/shard_map/ppermute | solution.py:34
  19.7 0.8 %collective-permute-start.6 = (f32[16,512]{1,0:T(8,128)S(1)}, f32[16,512]{1,0:T(8,128)S(1)}, u32[]{:S(2)}, u32[]{:S(2)}) collective-permute-start(f32[16,512]{1,0:T(8,128)S(1)} %get-tuple-element.26), channel_id=1, source_target_pairs={{0,24},{8,16},{16,8},{24,0},{1,25},{9,17},{17,9},{25,1},{2,26},{10... | collective-permute-start | bytes 98312 | tf_op jit(solution)/shard_map/ppermute | solution.py:34
  20.5 1.5 %collective-permute-start.7 = (f32[16,512]{1,0:T(8,128)S(1)}, f32[16,512]{1,0:T(8,128)S(1)}, u32[]{:S(2)}, u32[]{:S(2)}) collective-permute-start(f32[16,512]{1,0:T(8,128)S(1)} %get-tuple-element.27), channel_id=1, source_target_pairs={{0,4},{4,0},{1,5},{5,1},{2,6},{6,2},{3,7},{7,3},{8,12},{12,8},{9,1... | collective-permute-start | bytes 98312 | tf_op jit(solution)/shard_map/ppermute | solution.py:34
  22.1 0.0 collective-permute-done.4.refs_1_
  22.1 0.0 collective-permute-start.8
  22.1 0.0 collective-permute-done.9.refs_3_.refs_8_.refs_10_
  22.1 0.5 collective-permute-start.10
  22.6 0.0 collective-permute-done.5.refs_2_
  22.6 2.9 %collective-permute-done.6.refs_3_ = f32[16,512]{1,0:T(8,128)S(1)} collective-permute-done((f32[16,512]{1,0:T(8,128)S(1)}, f32[16,512]{1,0:T(8,128)S(1)}, u32[]{:S(2)}, u32[]{:S(2)}) %collective-permute-start.6) | collective-permute-done | bytes 32800 | tf_op jit(solution)/shard_map/ppermute | solution.py:34
  25.5 0.0 collective-permute-done.7.refs_4_
  25.5 0.1 collective-permute-start.11
  25.6 0.0 collective-permute-done.10.refs_4_.refs_9_.refs_11_
  25.6 0.4 shard_map.71.refs_2_
  26.0 0.5 collective-permute-start.14
  26.5 2.5 %collective-permute-start.12 = (f32[16,512]{1,0:T(8,128)S(1)}, f32[16,512]{1,0:T(8,128)S(1)}, u32[]{:S(2)}, u32[]{:S(2)}) collective-permute-start(f32[16,512]{1,0:T(8,128)S(1)} %shard_map.70.refs_0_.refs_10_.refs_12_), channel_id=1, source_target_pairs={{0,16},{8,24},{16,0},{24,8},{1,17},{9,25},{17,1},{25,9},{2,18},{10... | collective-permute-start | bytes 98312 | tf_op jit(solution)/shard_map/ppermute | solution.py:34
  29.1 1.8 %collective-permute-start.13 = (f32[16,512]{1,0:T(8,128)S(1)}, f32[16,512]{1,0:T(8,128)S(1)}, u32[]{:S(2)}, u32[]{:S(2)}) collective-permute-start(f32[16,512]{1,0:T(8,128)S(1)} %shard_map.70.refs_0_.refs_10_.refs_12_), channel_id=1, source_target_pairs={{0,24},{8,16},{16,8},{24,0},{1,25},{9,17},{17,9},{25,1},{2,26},{10... | collective-permute-start | bytes 98312 | tf_op jit(solution)/shard_map/ppermute | solution.py:34
  30.9 0.5 collective-permute-start.20
  31.4 0.0 collective-permute-done.11.refs_3_
  31.4 0.0 collective-permute-start.19
  31.4 0.1 collective-permute-done.12.refs_4_
  31.5 3.2 %collective-permute-done.13.refs_5_ = f32[16,512]{1,0:T(8,128)S(1)} collective-permute-done((f32[16,512]{1,0:T(8,128)S(1)}, f32[16,512]{1,0:T(8,128)S(1)}, u32[]{:S(2)}, u32[]{:S(2)}) %collective-permute-start.13) | collective-permute-done | bytes 32800 | tf_op jit(solution)/shard_map/ppermute | solution.py:34
  34.8 2.3 %shard_map.72 = (f32[16,512]{1,0:T(8,128)S(1)}, f32[16,128]{1,0:T(8,128)S(1)}, f32[16,640]{1,0:T(8,128)S(1)}, f32[16,640]{1,0:T(8,128)S(1)}, f32[16,640]{1,0:T(8,128)S(1)}, /*index=5*/f32[16,512]{1,0:T(8,128)S(1)}) custom-call(s32[3,16]{1,0:T(4,128)S(1)} %get-tuple-element.21.refs_0_, f32[16,256,256]{2,1,0:T(8,128)S(1)} %get-tuple-element.22.refs_1_, ...), custom_call_target="tpu_custom_call" | custom-call | tf_op jit(solution)/shard_map/pallas_call | solution.py:310
  37.1 0.1 collective-permute-start.15
  37.2 2.4 %collective-permute-start.16 = (f32[16,640]{1,0:T(8,128)S(1)}, f32[16,640]{1,0:T(8,128)S(1)}, u32[]{:S(2)}, u32[]{:S(2)}) collective-permute-start(f32[16,640]{1,0:T(8,128)S(1)} %get-tuple-element.32), channel_id=1, source_target_pairs={{0,16},{8,24},{16,0},{24,8},{1,17},{9,25},{17,1},{25,9},{2,18},{10... | collective-permute-start | bytes 122888 | tf_op jit(solution)/shard_map/ppermute | solution.py:34
  39.5 2.0 %collective-permute-start.17 = (f32[16,640]{1,0:T(8,128)S(1)}, f32[16,640]{1,0:T(8,128)S(1)}, u32[]{:S(2)}, u32[]{:S(2)}) collective-permute-start(f32[16,640]{1,0:T(8,128)S(1)} %get-tuple-element.33), channel_id=1, source_target_pairs={{0,24},{8,16},{16,8},{24,0},{1,25},{9,17},{17,9},{25,1},{2,26},{10... | collective-permute-start | bytes 122888 | tf_op jit(solution)/shard_map/ppermute | solution.py:34
  41.5 0.0 collective-permute-done.20.refs_12_.refs_14_
  41.5 0.0 collective-permute-start.21
  41.5 1.6 %collective-permute-start.18 = (f32[16,512]{1,0:T(8,128)S(1)}, f32[16,512]{1,0:T(8,128)S(1)}, u32[]{:S(2)}, u32[]{:S(2)}) collective-permute-start(f32[16,512]{1,0:T(8,128)S(1)} %get-tuple-element.34), channel_id=1, source_target_pairs={{0,4},{4,0},{1,5},{5,1},{2,6},{6,2},{3,7},{7,3},{8,12},{12,8},{9,1... | collective-permute-start | bytes 98312 | tf_op jit(solution)/shard_map/ppermute | solution.py:34
  43.1 2.4 %collective-permute-done.18.refs_5_ = f32[16,512]{1,0:T(8,128)S(1)} collective-permute-done((f32[16,512]{1,0:T(8,128)S(1)}, f32[16,512]{1,0:T(8,128)S(1)}, u32[]{:S(2)}, u32[]{:S(2)}) %collective-permute-start.18) | collective-permute-done | bytes 32800 | tf_op jit(solution)/shard_map/ppermute | solution.py:34
  45.5 1.2 %shard_map.73 = (f32[16,640]{1,0:T(8,128)S(1)}, f32[32,16,128]{2,1,0:T(8,128)}) custom-call(f32[16,512]{1,0:T(8,128)S(1)} %get-tuple-element.29.refs_0_, f32[16,128]{1,0:T(8,128)S(1)} %get-tuple-element.30.refs_1_, f32[16,640]{1,0:T(8,128)S(1)} %collective-permute-done.15.refs_2_, f32[16,640]{1,0:T(8,128)S(1)} %collective-permute-done.16.refs_3_, ...), custom_call_target="tpu_custom_call" | custom-call | tf_op jit(solution)/shard_map/pallas_call | solution.py:310
  46.7 3.1 %all-to-all-start = ((f32[32,16,128]{2,1,0:T(8,128)}), f32[32,16,128]{2,1,0:T(8,128)S(1)}, u32[]{:S(2)}, u32[]{:S(2)}) async-start(f32[32,16,128]{2,1,0:T(8,128)} %get-tuple-element.35), calls=%async_computation | async-start | bytes 524288 | tf_op jit(solution)/shard_map/all_to_all | solution.py:373
  49.8 1.8 %collective-permute-start.23 = (f32[16,640]{1,0:T(8,128)S(1)}, f32[16,640]{1,0:T(8,128)S(1)}, u32[]{:S(2)}, u32[]{:S(2)}) collective-permute-start(f32[16,640]{1,0:T(8,128)S(1)} %get-tuple-element.36.refs_0_.refs_4_), channel_id=1, source_target_pairs={{0,2},{1,3},{2,0},{3,1},{4,6},{5,7},{6,4},{7,5},{8,10},{9,11},{10,... | collective-permute-start | bytes 122888 | tf_op jit(solution)/shard_map/ppermute | solution.py:34
  51.7 3.2 %collective-permute-done.23.refs_2_.refs_6_ = f32[16,640]{1,0:T(8,128)S(1)} collective-permute-done((f32[16,640]{1,0:T(8,128)S(1)}, f32[16,640]{1,0:T(8,128)S(1)}, u32[]{:S(2)}, u32[]{:S(2)}) %collective-permute-start.23) | collective-permute-done | bytes 40992 | tf_op jit(solution)/shard_map/ppermute | solution.py:34
  54.9 1.2 %collective-permute-done.24.refs_3_.refs_7_ = f32[16,640]{1,0:T(8,128)S(1)} collective-permute-done((f32[16,640]{1,0:T(8,128)S(1)}, f32[16,640]{1,0:T(8,128)S(1)}, u32[]{:S(2)}, u32[]{:S(2)}) %collective-permute-start.24) | collective-permute-done | bytes 40992 | tf_op jit(solution)/shard_map/ppermute | solution.py:34
  56.1 3.3 %shard_map.74 = (f32[64,64]{1,0:T(8,128)S(1)}, f32[64,16]{1,0:T(8,128)S(1)}, f32[64,16]{1,0:T(8,128)S(1)}) custom-call(f32[16,640]{1,0:T(8,128)S(1)} %get-tuple-element.36.refs_0_.refs_4_, f32[16,640]{1,0:T(8,128)S(1)} %collective-permute-done.22.refs_1_.refs_5_, f32[16,640]{1,0:T(8,128)S(1)} %collective-permute-done.23.refs_2_.refs_6_, ...), custom_call_target="tpu_custom_call" | custom-call | flops 1048576 | bytes 655360 | tf_op jit(solution)/shard_map/pallas_call | solution.py:310
  59.4 1.0 %all-to-all-done.refs_0_ = f32[32,16,128]{2,1,0:T(8,128)S(1)} async-done(((f32[32,16,128]{2,1,0:T(8,128)}), f32[32,16,128]{2,1,0:T(8,128)S(1)}, u32[]{:S(2)}, u32[]{:S(2)}) %all-to-all-start) | async-done | bytes 262176 | tf_op jit(solution)/shard_map/all_to_all | solution.py:373
  60.4 4.8 %shard_map.75 = (f32[16,512]{1,0:T(8,128)}, f32[16,512]{1,0:T(8,128)}) custom-call(f32[32,16,128]{2,1,0:T(8,128)S(1)} %all-to-all-done.refs_0_, f32[64,64]{1,0:T(8,128)S(1)} %get-tuple-element.37.refs_1_, f32[64,16]{1,0:T(8,128)S(1)} %get-tuple-element.38.refs_2_, f32[64,16]{1,0:T(8,128)S(1)} %get-tuple-element.39.refs_3_, ...), custom_call_target="tpu_custom_call" | custom-call | tf_op jit(solution)/shard_map/pallas_call | solution.py:310
  (14 shorter events, 0.0 us)
Async XLA Ops:
  0.6 11.6 %copy-start = (f32[16,512]{1,0:T(8,128)S(1)}, f32[16,512]{1,0:T(8,128)}, u32[]{:S(2)}) copy-start(f32[16,512]{1,0:T(8,128)} %refs_8_.1) | copy-start | bytes 98308
  0.6 11.0 %collective-permute-start = (f32[16,512]{1,0:T(8,128)}, f32[16,512]{1,0:T(8,128)S(1)}, u32[]{:S(2)}, u32[]{:S(2)}) collective-permute-start(f32[16,512]{1,0:T(8,128)} %refs_8_.1), channel_id=1, source_target_pairs={{0,8},{8,0},{16,24},{24,16},{1,9},{9,1},{17,25},{25,17},{2,10},{10... | collective-permute-start | bytes 98312 | tf_op jit(solution)/shard_map/ppermute | solution.py:34
  3.8 7.9 %collective-permute-start.1 = (f32[16,512]{1,0:T(8,128)}, f32[16,512]{1,0:T(8,128)S(1)}, u32[]{:S(2)}, u32[]{:S(2)}) collective-permute-start(f32[16,512]{1,0:T(8,128)} %refs_8_.1), channel_id=1, source_target_pairs={{0,16},{8,24},{16,0},{24,8},{1,17},{9,25},{17,1},{25,9},{2,18},{10... | collective-permute-start | bytes 98312 | tf_op jit(solution)/shard_map/ppermute | solution.py:34
  6.3 5.9 %collective-permute-start.2 = (f32[16,512]{1,0:T(8,128)}, f32[16,512]{1,0:T(8,128)S(1)}, u32[]{:S(2)}, u32[]{:S(2)}) collective-permute-start(f32[16,512]{1,0:T(8,128)} %refs_8_.1), channel_id=1, source_target_pairs={{0,24},{8,16},{16,8},{24,0},{1,25},{9,17},{17,9},{25,1},{2,26},{10... | collective-permute-start | bytes 98312 | tf_op jit(solution)/shard_map/ppermute | solution.py:34
  6.4 5.9 %collective-permute-start.3 = (f32[16,512]{1,0:T(8,128)}, f32[16,512]{1,0:T(8,128)S(1)}, u32[]{:S(2)}, u32[]{:S(2)}) collective-permute-start(f32[16,512]{1,0:T(8,128)} %refs_8_.1), channel_id=1, source_target_pairs={{0,4},{4,0},{1,5},{5,1},{2,6},{6,2},{3,7},{7,3},{8,12},{12,8},{9,1... | collective-permute-start | bytes 98312 | tf_op jit(solution)/shard_map/ppermute | solution.py:34
  14.6 7.5 %collective-permute-start.4 = (f32[16,512]{1,0:T(8,128)S(1)}, f32[16,512]{1,0:T(8,128)S(1)}, u32[]{:S(2)}, u32[]{:S(2)}) collective-permute-start(f32[16,512]{1,0:T(8,128)S(1)} %get-tuple-element.24), channel_id=1, source_target_pairs={{0,8},{8,0},{16,24},{24,16},{1,9},{9,1},{17,25},{25,17},{2,10},{10... | collective-permute-start | bytes 98312 | tf_op jit(solution)/shard_map/ppermute | solution.py:34
  14.8 7.3 %collective-permute-start.9 = (f32[16,512]{1,0:T(8,128)S(1)}, f32[16,512]{1,0:T(8,128)S(1)}, u32[]{:S(2)}, u32[]{:S(2)}) collective-permute-start(f32[16,512]{1,0:T(8,128)S(1)} %get-tuple-element.28), channel_id=1, source_target_pairs={{0,2},{1,3},{2,0},{3,1},{4,6},{5,7},{6,4},{7,5},{8,10},{9,11},{10,... | collective-permute-start | bytes 98312 | tf_op jit(solution)/shard_map/ppermute | solution.py:34
  16.3 6.3 %collective-permute-start.5 = (f32[16,512]{1,0:T(8,128)S(1)}, f32[16,512]{1,0:T(8,128)S(1)}, u32[]{:S(2)}, u32[]{:S(2)}) collective-permute-start(f32[16,512]{1,0:T(8,128)S(1)} %get-tuple-element.25), channel_id=1, source_target_pairs={{0,16},{8,24},{16,0},{24,8},{1,17},{9,25},{17,1},{25,9},{2,18},{10... | collective-permute-start | bytes 98312 | tf_op jit(solution)/shard_map/ppermute | solution.py:34
  19.7 5.7 %collective-permute-start.6 = (f32[16,512]{1,0:T(8,128)S(1)}, f32[16,512]{1,0:T(8,128)S(1)}, u32[]{:S(2)}, u32[]{:S(2)}) collective-permute-start(f32[16,512]{1,0:T(8,128)S(1)} %get-tuple-element.26), channel_id=1, source_target_pairs={{0,24},{8,16},{16,8},{24,0},{1,25},{9,17},{17,9},{25,1},{2,26},{10... | collective-permute-start | bytes 98312 | tf_op jit(solution)/shard_map/ppermute | solution.py:34
  20.5 4.9 %collective-permute-start.7 = (f32[16,512]{1,0:T(8,128)S(1)}, f32[16,512]{1,0:T(8,128)S(1)}, u32[]{:S(2)}, u32[]{:S(2)}) collective-permute-start(f32[16,512]{1,0:T(8,128)S(1)} %get-tuple-element.27), channel_id=1, source_target_pairs={{0,4},{4,0},{1,5},{5,1},{2,6},{6,2},{3,7},{7,3},{8,12},{12,8},{9,1... | collective-permute-start | bytes 98312 | tf_op jit(solution)/shard_map/ppermute | solution.py:34
  22.1 3.5 %collective-permute-start.8 = (f32[16,512]{1,0:T(8,128)S(1)}, f32[16,512]{1,0:T(8,128)S(1)}, u32[]{:S(2)}, u32[]{:S(2)}) collective-permute-start(f32[16,512]{1,0:T(8,128)S(1)} %get-tuple-element.28), channel_id=1, source_target_pairs={{0,1},{1,0},{2,3},{3,2},{4,5},{5,4},{6,7},{7,6},{8,9},{9,8},{10,11... | collective-permute-start | bytes 98312 | tf_op jit(solution)/shard_map/ppermute | solution.py:34
  22.1 3.5 %collective-permute-start.10 = (f32[16,512]{1,0:T(8,128)S(1)}, f32[16,512]{1,0:T(8,128)S(1)}, u32[]{:S(2)}, u32[]{:S(2)}) collective-permute-start(f32[16,512]{1,0:T(8,128)S(1)} %collective-permute-done.9.refs_3_.refs_8_.refs_10_), channel_id=1, source_target_pairs={{0,1},{1,0},{2,3},{3,2},{4,5},{5,4},{6,7},{7,6},{8,9},{9,8},{10,11... | collective-permute-start | bytes 98312 | tf_op jit(solution)/shard_map/ppermute | solution.py:34
  25.5 5.9 %collective-permute-start.11 = (f32[16,512]{1,0:T(8,128)S(1)}, f32[16,512]{1,0:T(8,128)S(1)}, u32[]{:S(2)}, u32[]{:S(2)}) collective-permute-start(f32[16,512]{1,0:T(8,128)S(1)} %shard_map.70.refs_0_.refs_10_.refs_12_), channel_id=1, source_target_pairs={{0,8},{8,0},{16,24},{24,16},{1,9},{9,1},{17,25},{25,17},{2,10},{10... | collective-permute-start | bytes 98312 | tf_op jit(solution)/shard_map/ppermute | solution.py:34
  26.0 8.8 %collective-permute-start.14 = (f32[16,640]{1,0:T(8,128)S(1)}, f32[16,640]{1,0:T(8,128)S(1)}, u32[]{:S(2)}, u32[]{:S(2)}) collective-permute-start(f32[16,640]{1,0:T(8,128)S(1)} %shard_map.71.refs_2_), channel_id=1, source_target_pairs={{0,4},{4,0},{1,5},{5,1},{2,6},{6,2},{3,7},{7,3},{8,12},{12,8},{9,1... | collective-permute-start | bytes 122888 | tf_op jit(solution)/shard_map/ppermute | solution.py:34
  26.5 5.0 %collective-permute-start.12 = (f32[16,512]{1,0:T(8,128)S(1)}, f32[16,512]{1,0:T(8,128)S(1)}, u32[]{:S(2)}, u32[]{:S(2)}) collective-permute-start(f32[16,512]{1,0:T(8,128)S(1)} %shard_map.70.refs_0_.refs_10_.refs_12_), channel_id=1, source_target_pairs={{0,16},{8,24},{16,0},{24,8},{1,17},{9,25},{17,1},{25,9},{2,18},{10... | collective-permute-start | bytes 98312 | tf_op jit(solution)/shard_map/ppermute | solution.py:34
  29.1 5.7 %collective-permute-start.13 = (f32[16,512]{1,0:T(8,128)S(1)}, f32[16,512]{1,0:T(8,128)S(1)}, u32[]{:S(2)}, u32[]{:S(2)}) collective-permute-start(f32[16,512]{1,0:T(8,128)S(1)} %shard_map.70.refs_0_.refs_10_.refs_12_), channel_id=1, source_target_pairs={{0,24},{8,16},{16,8},{24,0},{1,25},{9,17},{17,9},{25,1},{2,26},{10... | collective-permute-start | bytes 98312 | tf_op jit(solution)/shard_map/ppermute | solution.py:34
  30.9 10.7 %collective-permute-start.20 = (f32[16,512]{1,0:T(8,128)S(1)}, f32[16,512]{1,0:T(8,128)S(1)}, u32[]{:S(2)}, u32[]{:S(2)}) collective-permute-start(f32[16,512]{1,0:T(8,128)S(1)} %shard_map.70.refs_0_.refs_10_.refs_12_), channel_id=1, source_target_pairs={{0,2},{1,3},{2,0},{3,1},{4,6},{5,7},{6,4},{7,5},{8,10},{9,11},{10,... | collective-permute-start | bytes 98312 | tf_op jit(solution)/shard_map/ppermute | solution.py:34
  31.4 10.1 %collective-permute-start.19 = (f32[16,512]{1,0:T(8,128)S(1)}, f32[16,512]{1,0:T(8,128)S(1)}, u32[]{:S(2)}, u32[]{:S(2)}) collective-permute-start(f32[16,512]{1,0:T(8,128)S(1)} %shard_map.70.refs_0_.refs_10_.refs_12_), channel_id=1, source_target_pairs={{0,1},{1,0},{2,3},{3,2},{4,5},{5,4},{6,7},{7,6},{8,9},{9,8},{10,11... | collective-permute-start | bytes 98312 | tf_op jit(solution)/shard_map/ppermute | solution.py:34
  37.1 8.4 %collective-permute-start.15 = (f32[16,640]{1,0:T(8,128)S(1)}, f32[16,640]{1,0:T(8,128)S(1)}, u32[]{:S(2)}, u32[]{:S(2)}) collective-permute-start(f32[16,640]{1,0:T(8,128)S(1)} %get-tuple-element.31), channel_id=1, source_target_pairs={{0,8},{8,0},{16,24},{24,16},{1,9},{9,1},{17,25},{25,17},{2,10},{10... | collective-permute-start | bytes 122888 | tf_op jit(solution)/shard_map/ppermute | solution.py:34
  37.2 8.4 %collective-permute-start.16 = (f32[16,640]{1,0:T(8,128)S(1)}, f32[16,640]{1,0:T(8,128)S(1)}, u32[]{:S(2)}, u32[]{:S(2)}) collective-permute-start(f32[16,640]{1,0:T(8,128)S(1)} %get-tuple-element.32), channel_id=1, source_target_pairs={{0,16},{8,24},{16,0},{24,8},{1,17},{9,25},{17,1},{25,9},{2,18},{10... | collective-permute-start | bytes 122888 | tf_op jit(solution)/shard_map/ppermute | solution.py:34
  39.5 6.0 %collective-permute-start.17 = (f32[16,640]{1,0:T(8,128)S(1)}, f32[16,640]{1,0:T(8,128)S(1)}, u32[]{:S(2)}, u32[]{:S(2)}) collective-permute-start(f32[16,640]{1,0:T(8,128)S(1)} %get-tuple-element.33), channel_id=1, source_target_pairs={{0,24},{8,16},{16,8},{24,0},{1,25},{9,17},{17,9},{25,1},{2,26},{10... | collective-permute-start | bytes 122888 | tf_op jit(solution)/shard_map/ppermute | solution.py:34
  41.5 1.6 %collective-permute-start.21 = (f32[16,512]{1,0:T(8,128)S(1)}, f32[16,512]{1,0:T(8,128)S(1)}, u32[]{:S(2)}, u32[]{:S(2)}) collective-permute-start(f32[16,512]{1,0:T(8,128)S(1)} %collective-permute-done.20.refs_12_.refs_14_), channel_id=1, source_target_pairs={{0,1},{1,0},{2,3},{3,2},{4,5},{5,4},{6,7},{7,6},{8,9},{9,8},{10,11... | collective-permute-start | bytes 98312 | tf_op jit(solution)/shard_map/ppermute | solution.py:34
  41.5 4.0 %collective-permute-start.18 = (f32[16,512]{1,0:T(8,128)S(1)}, f32[16,512]{1,0:T(8,128)S(1)}, u32[]{:S(2)}, u32[]{:S(2)}) collective-permute-start(f32[16,512]{1,0:T(8,128)S(1)} %get-tuple-element.34), channel_id=1, source_target_pairs={{0,4},{4,0},{1,5},{5,1},{2,6},{6,2},{3,7},{7,3},{8,12},{12,8},{9,1... | collective-permute-start | bytes 98312 | tf_op jit(solution)/shard_map/ppermute | solution.py:34
  46.7 13.7 %all-to-all-start = ((f32[32,16,128]{2,1,0:T(8,128)}), f32[32,16,128]{2,1,0:T(8,128)S(1)}, u32[]{:S(2)}, u32[]{:S(2)}) async-start(f32[32,16,128]{2,1,0:T(8,128)} %get-tuple-element.35), calls=%async_computation | async-start | bytes 524288 | tf_op jit(solution)/shard_map/all_to_all | solution.py:373
  49.8 5.0 %collective-permute-start.23 = (f32[16,640]{1,0:T(8,128)S(1)}, f32[16,640]{1,0:T(8,128)S(1)}, u32[]{:S(2)}, u32[]{:S(2)}) collective-permute-start(f32[16,640]{1,0:T(8,128)S(1)} %get-tuple-element.36.refs_0_.refs_4_), channel_id=1, source_target_pairs={{0,2},{1,3},{2,0},{3,1},{4,6},{5,7},{6,4},{7,5},{8,10},{9,11},{10,... | collective-permute-start | bytes 122888 | tf_op jit(solution)/shard_map/ppermute | solution.py:34
  51.7 3.2 %collective-permute-start.22 = (f32[16,640]{1,0:T(8,128)S(1)}, f32[16,640]{1,0:T(8,128)S(1)}, u32[]{:S(2)}, u32[]{:S(2)}) collective-permute-start(f32[16,640]{1,0:T(8,128)S(1)} %get-tuple-element.36.refs_0_.refs_4_), channel_id=1, source_target_pairs={{0,1},{1,0},{2,3},{3,2},{4,5},{5,4},{6,7},{7,6},{8,9},{9,8},{10,11... | collective-permute-start | bytes 122888 | tf_op jit(solution)/shard_map/ppermute | solution.py:34
  54.9 1.2 %collective-permute-start.24 = (f32[16,640]{1,0:T(8,128)S(1)}, f32[16,640]{1,0:T(8,128)S(1)}, u32[]{:S(2)}, u32[]{:S(2)}) collective-permute-start(f32[16,640]{1,0:T(8,128)S(1)} %collective-permute-done.23.refs_2_.refs_6_), channel_id=1, source_target_pairs={{0,1},{1,0},{2,3},{3,2},{4,5},{5,4},{6,7},{7,6},{8,9},{9,8},{10,11... | collective-permute-start | bytes 122888 | tf_op jit(solution)/shard_map/ppermute | solution.py:34

commit v4 on v3

--- a/solution.py
+++ b/solution.py
@@ -10,6 +10,7 @@
 
 BLK = 256
 SEG = 2
+PIVOT = 4
 HIGHEST = lax.Precision.HIGHEST
 VMEM = pl.BlockSpec(memory_space=pltpu.VMEM)
 SMEM = pl.BlockSpec(memory_space=pltpu.SMEM)
@@ -217,43 +218,62 @@
         out_gram[0][i] = late
 
 
-def eliminate(tables):
+def factor_two(e):
+    a, b, d = e(0, 0), e(0, 1), e(1, 1)
+    scale = 1.0 / (a * d - b * b)
+    a, b, d = a * scale, b * scale, d * scale
+    return lambda q: [d * q[0] - b * q[1], a * q[1] - b * q[0]]
+
+
+def factor(e, size):
+    if size == 2:
+        return factor_two(e)
+    half = size // 2
+    top = factor(e, half)
+    columns = [top([e(i, half + j) for i in range(half)]) for j in range(half)]
+
+    def schur(i, j):
+        return e(half + i, half + j) - sum(e(a, half + i) * columns[j][a] for a in range(half))
+
+    entries = {(i, j): schur(i, j) for i in range(half) for j in range(i, half)}
+    bottom = factor(lambda i, j: entries[i, j], half)
+
+    def solve(q):
+        upper = top(q[:half])
+        lower = bottom([q[half + i] - sum(columns[i][a] * q[a] for a in range(half)) for i in range(half)])
+        return [upper[a] - sum(columns[i][a] * lower[i] for i in range(half)) for a in range(half)] + lower
+
+    return solve
+
+
+def eliminate(tables, pivot):
     size, wide = tables[0].shape
     sub = 8
     at_row = lax.broadcasted_iota(jnp.int32, (sub, wide), 0)
+    one = tables[0][:sub] * 0.0 + 1.0
     tables = [[table[t : t + sub] for t in range(0, size, sub)] for table in tables]
-    for k in range(0, size, 4):
+    for k in range(0, size, pivot):
         home, base = k // sub, k % sub
         for tiles in tables:
-            spread = [[jnp.broadcast_to(tile[:, k + j : k + j + 1], (sub, wide)) for tile in tiles] for j in range(4)]
-            row = [jnp.broadcast_to(tiles[home][base + i : base + i + 1], (sub, wide)) for i in range(4)]
-            e = [
-                [jnp.broadcast_to(spread[j][home][base + i : base + i + 1], (sub, wide)) if i <= j else None for j in range(4)]
-                for i in range(4)
+            spread = [
+                [jnp.broadcast_to(tile[:, k + j : k + j + 1], (sub, wide)) for tile in tiles] for j in range(pivot)
             ]
-            scale = 1.0 / (e[0][0] * e[1][1] - e[0][1] * e[0][1])
-            a00, a01, a11 = e[1][1] * scale, -e[0][1] * scale, e[0][0] * scale
-            x00, x10 = a00 * e[0][2] + a01 * e[1][2], a01 * e[0][2] + a11 * e[1][2]
-            x01, x11 = a00 * e[0][3] + a01 * e[1][3], a01 * e[0][3] + a11 * e[1][3]
-            s00 = e[2][2] - (e[0][2] * x00 + e[1][2] * x10)
-            s01 = e[2][3] - (e[0][2] * x01 + e[1][2] * x11)
-            s11 = e[3][3] - (e[0][3] * x01 + e[1][3] * x11)
-            scale = 1.0 / (s00 * s11 - s01 * s01)
-            t2 = row[2] - (x00 * row[0] + x10 * row[1])
-            t3 = row[3] - (x01 * row[0] + x11 * row[1])
-            p2 = (s11 * t2 - s01 * t3) * scale
-            p3 = (s00 * t3 - s01 * t2) * scale
-            p0 = (a00 * row[0] + a01 * row[1]) - (x00 * p2 + x01 * p3)
-            p1 = (a01 * row[0] + a11 * row[1]) - (x10 * p2 + x11 * p3)
-            pivots = (p0, p1, p2, p3)
+            row = [jnp.broadcast_to(tiles[home][base + i : base + i + 1], (sub, wide)) for i in range(pivot)]
+            near = [spread[j][home] * one for j in range(pivot)]
+            entries = {
+                (i, j): jnp.broadcast_to(near[j][base + i : base + i + 1], (sub, wide))
+                for j in range(pivot)
+                for i in range(j + 1)
+            }
+            solved = factor(lambda i, j: entries[i, j], pivot)(row)
             for t, tile in enumerate(tiles):
+                if t == home and pivot == sub:
+                    tiles[t] = solved[0]
+                else:
+                    tiles[t] = tile - sum(spread[j][t] * solved[j] for j in range(pivot))
                 if t == home:
-                    keep = tile - sum(spread[j][t] * pivots[j] for j in range(4))
-                    for i in range(4):
-                        keep = jnp.where(at_row == base + i, pivots[i], keep)
-                    tiles[t] = keep
-                else:
-                    tiles[t] = tile - sum(spread[j][t] * pivots[j] for j in range(4))
+                    for i in range(pivot):
+                        tiles[t] = jnp.where(at_row == base + i, solved[i], tiles[t])
     return [jnp.concatenate(tiles, axis=0) for tiles in tables]
 
 
@@ -271,7 +291,7 @@
         place = source_of("depth", step)
         scratch[0][pl.ds(pl.multiple_of(place * width, width), width), :] = ref[:, points + size : points + 2 * size]
     gram1 = scratch[0][...]
-    (first,) = eliminate([jnp.concatenate([gram1, identity_of(size)], axis=1)])
+    (first,) = eliminate([jnp.concatenate([gram1, identity_of(size)], axis=1)], PIVOT)
     inverse = first[:, size:]
     outs[0][...] = inverse
     outs[1][...] = dot_nt(inverse, wide_refs[0][:, points : points + size])
@@ -298,7 +318,7 @@
     schur = gram3 - dot_nn(gram2, carry)
     right = gram1_own - dot_nn(gram2, start)
     fill = jnp.zeros((size, size - width), jnp.float32)
-    (second,) = eliminate([jnp.concatenate([schur, right, fill], axis=1)])
+    (second,) = eliminate([jnp.concatenate([schur, right, fill], axis=1)], PIVOT)
     weight1 = second[:, size : size + width]
     weight0 = start - dot_nn(carry, weight1)
     base_all, image_all = base[...], image[...]

time: 65.4 us -> 64.6 us (0.988)
  Pallas kernels: 17.2 us -> 15.6 us
  waiting for transfers between devices: 14.7 us -> 15.5 us
    pallas_call x8, Pallas kernels: 17.2 us -> 15.6 us  [call(): pl.pallas_call(body, out_shape=[s if hasattr(s, 'dtype') else jax.ShapeDt...]
    all_to_all x1, waiting for transfers between devices: 1.01 us -> 1.77 us  [per_device(): late = lax.all_to_all(late, ('row', 'col', 'depth'), 0, 0)]
  transfers between devices with their start and end apart: 26 -> 26, of which waited for: 8 -> 8; matrix products, arithmetic and copies ran while one was open for 0% -> 0% of each run, Pallas kernels for 14% -> 13%
where the time goes in v4:
time: 64.6 us; the launch traced here: 64.4 us
  starting transfers between devices  31.9 us (49%)
  Pallas kernels  15.6 us (24%)
  waiting for transfers between devices  15.5 us (24%)
  between operations  1.41 us (2%)
    ppermute x25, starting transfers between devices, send(): lax.ppermute(x, axis, [(i, partner(i, step, size)) for i in range(size)])  28.8 us
    pallas_call x8, Pallas kernels, call(): pl.pallas_call(body, out_shape=[s if hasattr(s, 'dtype') else jax.ShapeDt...  15.6 us
    ppermute x25, waiting for transfers between devices, send(): lax.ppermute(x, axis, [(i, partner(i, step, size)) for i in range(size)])  13.7 us
    all_to_all x1, starting transfers between devices, per_device(): late = lax.all_to_all(late, ('row', 'col', 'depth'), 0, 0)  3.13 us
    all_to_all x1, waiting for transfers between devices, per_device(): late = lax.all_to_all(late, ('row', 'col', 'depth'), 0, 0)  1.77 us
  transfers between devices with their start and end apart: 26, of which 8 were waited for; matrix products, arithmetic and copies ran while one was open for 0% of the time, Pallas kernels for 13%

profile of v4, /device:TPU:0, one launch (start us, length us, event | category | flops | bytes accessed | tf_op | source)
XLA Modules:
  0.0 64.4 jit_solution(12726043340100817880)
XLA Ops:
  0.6 3.1 %collective-permute-start = (f32[16,512]{1,0:T(8,128)}, f32[16,512]{1,0:T(8,128)S(1)}, u32[]{:S(2)}, u32[]{:S(2)}) collective-permute-start(f32[16,512]{1,0:T(8,128)} %refs_8_.1), channel_id=1, source_target_pairs={{0,8},{8,0},{16,24},{24,16},{1,9},{9,1},{17,25},{25,17},{2,10},{10... | collective-permute-start | bytes 98312 | tf_op jit(solution)/shard_map/ppermute | solution.py:35
  3.8 2.6 %collective-permute-start.1 = (f32[16,512]{1,0:T(8,128)}, f32[16,512]{1,0:T(8,128)S(1)}, u32[]{:S(2)}, u32[]{:S(2)}) collective-permute-start(f32[16,512]{1,0:T(8,128)} %refs_8_.1), channel_id=1, source_target_pairs={{0,16},{8,24},{16,0},{24,8},{1,17},{9,25},{17,1},{25,9},{2,18},{10... | collective-permute-start | bytes 98312 | tf_op jit(solution)/shard_map/ppermute | solution.py:35
  6.4 1.7 %collective-permute-start.3 = (f32[16,512]{1,0:T(8,128)}, f32[16,512]{1,0:T(8,128)S(1)}, u32[]{:S(2)}, u32[]{:S(2)}) collective-permute-start(f32[16,512]{1,0:T(8,128)} %refs_8_.1), channel_id=1, source_target_pairs={{0,4},{4,0},{1,5},{5,1},{2,6},{6,2},{3,7},{7,3},{8,12},{12,8},{9,1... | collective-permute-start | bytes 98312 | tf_op jit(solution)/shard_map/ppermute | solution.py:35
  8.7 2.9 %shard_map.68 = (f32[16,256,256]{2,1,0:T(8,128)S(1)}, s32[3,16]{1,0:T(4,128)S(1)}) custom-call(s32[1,1]{1,0:T(1,128)S(6)} %copy.7.count_ref, s32[1,1,16]{2,1,0:T(1,128)} %rows_ref.1, s32[1,1,16]{2,1,0:T(1,128)} %cols_ref.1, f32[1,1,16,256,256]{4,3,2,1,0:T(8,128)} %blocks_ref.1), custom_call_target="tpu_custom_call" | custom-call | bytes 8388608 | tf_op jit(solution)/shard_map/pallas_call | solution.py:330
  11.7 0.0 collective-permute-done.refs_3_
  11.7 0.0 collective-permute-done.1.refs_4_
  11.7 0.6 collective-permute-done.2.refs_5_
  12.3 0.0 collective-permute-done.3.refs_6_
  12.3 2.3 %shard_map.69 = (f32[16,512]{1,0:T(8,128)S(1)}, f32[16,512]{1,0:T(8,128)S(1)}, f32[16,512]{1,0:T(8,128)S(1)}, f32[16,512]{1,0:T(8,128)S(1)}, f32[16,512]{1,0:T(8,128)S(1)}, /*index=5*/f32[16,512]{1,0:T(8,128)S(1)}) custom-call(s32[3,16]{1,0:T(4,128)S(1)} %get-tuple-element.21.refs_0_, f32[16,256,256]{2,1,0:T(8,128)S(1)} %get-tuple-element.22.refs_1_, ...), custom_call_target="tpu_custom_call" | custom-call | tf_op jit(solution)/shard_map/pallas_call | solution.py:330
  14.6 0.2 collective-permute-start.4
  14.8 1.5 %collective-permute-start.9 = (f32[16,512]{1,0:T(8,128)S(1)}, f32[16,512]{1,0:T(8,128)S(1)}, u32[]{:S(2)}, u32[]{:S(2)}) collective-permute-start(f32[16,512]{1,0:T(8,128)S(1)} %get-tuple-element.28), channel_id=1, source_target_pairs={{0,2},{1,3},{2,0},{3,1},{4,6},{5,7},{6,4},{7,5},{8,10},{9,11},{10,... | collective-permute-start | bytes 98312 | tf_op jit(solution)/shard_map/ppermute | solution.py:35
  16.3 3.5 %collective-permute-start.5 = (f32[16,512]{1,0:T(8,128)S(1)}, f32[16,512]{1,0:T(8,128)S(1)}, u32[]{:S(2)}, u32[]{:S(2)}) collective-permute-start(f32[16,512]{1,0:T(8,128)S(1)} %get-tuple-element.25), channel_id=1, source_target_pairs={{0,16},{8,24},{16,0},{24,8},{1,17},{9,25},{17,1},{25,9},{2,18},{10... | collective-permute-start | bytes 98312 | tf_op jit(solution)/shard_map/ppermute | solution.py:35
  19.7 0.8 %collective-permute-start.6 = (f32[16,512]{1,0:T(8,128)S(1)}, f32[16,512]{1,0:T(8,128)S(1)}, u32[]{:S(2)}, u32[]{:S(2)}) collective-permute-start(f32[16,512]{1,0:T(8,128)S(1)} %get-tuple-element.26), channel_id=1, source_target_pairs={{0,24},{8,16},{16,8},{24,0},{1,25},{9,17},{17,9},{25,1},{2,26},{10... | collective-permute-start | bytes 98312 | tf_op jit(solution)/shard_map/ppermute | solution.py:35
  20.5 1.5 %collective-permute-start.7 = (f32[16,512]{1,0:T(8,128)S(1)}, f32[16,512]{1,0:T(8,128)S(1)}, u32[]{:S(2)}, u32[]{:S(2)}) collective-permute-start(f32[16,512]{1,0:T(8,128)S(1)} %get-tuple-element.27), channel_id=1, source_target_pairs={{0,4},{4,0},{1,5},{5,1},{2,6},{6,2},{3,7},{7,3},{8,12},{12,8},{9,1... | collective-permute-start | bytes 98312 | tf_op jit(solution)/shard_map/ppermute | solution.py:35
  22.1 0.0 collective-permute-done.4.refs_1_
  22.1 0.0 collective-permute-start.8
  22.1 0.0 collective-permute-done.9.refs_3_.refs_8_.refs_10_
  22.1 0.5 collective-permute-start.10
  22.6 0.0 collective-permute-done.5.refs_2_
  22.6 2.9 %collective-permute-done.6.refs_3_ = f32[16,512]{1,0:T(8,128)S(1)} collective-permute-done((f32[16,512]{1,0:T(8,128)S(1)}, f32[16,512]{1,0:T(8,128)S(1)}, u32[]{:S(2)}, u32[]{:S(2)}) %collective-permute-start.6) | collective-permute-done | bytes 32800 | tf_op jit(solution)/shard_map/ppermute | solution.py:35
  25.5 0.0 collective-permute-done.7.refs_4_
  25.5 0.1 collective-permute-start.11
  25.6 0.0 collective-permute-done.10.refs_4_.refs_9_.refs_11_
  25.6 0.4 shard_map.71.refs_2_
  26.0 0.5 collective-permute-start.14
  26.5 2.5 %collective-permute-start.12 = (f32[16,512]{1,0:T(8,128)S(1)}, f32[16,512]{1,0:T(8,128)S(1)}, u32[]{:S(2)}, u32[]{:S(2)}) collective-permute-start(f32[16,512]{1,0:T(8,128)S(1)} %shard_map.70.refs_0_.refs_10_.refs_12_), channel_id=1, source_target_pairs={{0,16},{8,24},{16,0},{24,8},{1,17},{9,25},{17,1},{25,9},{2,18},{10... | collective-permute-start | bytes 98312 | tf_op jit(solution)/shard_map/ppermute | solution.py:35
  29.1 1.8 %collective-permute-start.13 = (f32[16,512]{1,0:T(8,128)S(1)}, f32[16,512]{1,0:T(8,128)S(1)}, u32[]{:S(2)}, u32[]{:S(2)}) collective-permute-start(f32[16,512]{1,0:T(8,128)S(1)} %shard_map.70.refs_0_.refs_10_.refs_12_), channel_id=1, source_target_pairs={{0,24},{8,16},{16,8},{24,0},{1,25},{9,17},{17,9},{25,1},{2,26},{10... | collective-permute-start | bytes 98312 | tf_op jit(solution)/shard_map/ppermute | solution.py:35
  30.9 0.5 collective-permute-start.20
  31.4 0.0 collective-permute-done.11.refs_3_
  31.4 0.0 collective-permute-start.19
  31.4 0.1 collective-permute-done.12.refs_4_
  31.5 3.2 %collective-permute-done.13.refs_5_ = f32[16,512]{1,0:T(8,128)S(1)} collective-permute-done((f32[16,512]{1,0:T(8,128)S(1)}, f32[16,512]{1,0:T(8,128)S(1)}, u32[]{:S(2)}, u32[]{:S(2)}) %collective-permute-start.13) | collective-permute-done | bytes 32800 | tf_op jit(solution)/shard_map/ppermute | solution.py:35
  34.8 2.3 %shard_map.72 = (f32[16,512]{1,0:T(8,128)S(1)}, f32[16,128]{1,0:T(8,128)S(1)}, f32[16,640]{1,0:T(8,128)S(1)}, f32[16,640]{1,0:T(8,128)S(1)}, f32[16,640]{1,0:T(8,128)S(1)}, /*index=5*/f32[16,512]{1,0:T(8,128)S(1)}) custom-call(s32[3,16]{1,0:T(4,128)S(1)} %get-tuple-element.21.refs_0_, f32[16,256,256]{2,1,0:T(8,128)S(1)} %get-tuple-element.22.refs_1_, ...), custom_call_target="tpu_custom_call" | custom-call | tf_op jit(solution)/shard_map/pallas_call | solution.py:330
  37.1 0.1 collective-permute-start.15
  37.2 2.4 %collective-permute-start.16 = (f32[16,640]{1,0:T(8,128)S(1)}, f32[16,640]{1,0:T(8,128)S(1)}, u32[]{:S(2)}, u32[]{:S(2)}) collective-permute-start(f32[16,640]{1,0:T(8,128)S(1)} %get-tuple-element.32), channel_id=1, source_target_pairs={{0,16},{8,24},{16,0},{24,8},{1,17},{9,25},{17,1},{25,9},{2,18},{10... | collective-permute-start | bytes 122888 | tf_op jit(solution)/shard_map/ppermute | solution.py:35
  39.5 2.0 %collective-permute-start.17 = (f32[16,640]{1,0:T(8,128)S(1)}, f32[16,640]{1,0:T(8,128)S(1)}, u32[]{:S(2)}, u32[]{:S(2)}) collective-permute-start(f32[16,640]{1,0:T(8,128)S(1)} %get-tuple-element.33), channel_id=1, source_target_pairs={{0,24},{8,16},{16,8},{24,0},{1,25},{9,17},{17,9},{25,1},{2,26},{10... | collective-permute-start | bytes 122888 | tf_op jit(solution)/shard_map/ppermute | solution.py:35
  41.5 0.0 collective-permute-done.20.refs_12_.refs_14_
  41.5 0.0 collective-permute-start.21
  41.5 1.6 %collective-permute-start.18 = (f32[16,512]{1,0:T(8,128)S(1)}, f32[16,512]{1,0:T(8,128)S(1)}, u32[]{:S(2)}, u32[]{:S(2)}) collective-permute-start(f32[16,512]{1,0:T(8,128)S(1)} %get-tuple-element.34), channel_id=1, source_target_pairs={{0,4},{4,0},{1,5},{5,1},{2,6},{6,2},{3,7},{7,3},{8,12},{12,8},{9,1... | collective-permute-start | bytes 98312 | tf_op jit(solution)/shard_map/ppermute | solution.py:35
  43.1 2.4 %collective-permute-done.18.refs_5_ = f32[16,512]{1,0:T(8,128)S(1)} collective-permute-done((f32[16,512]{1,0:T(8,128)S(1)}, f32[16,512]{1,0:T(8,128)S(1)}, u32[]{:S(2)}, u32[]{:S(2)}) %collective-permute-start.18) | collective-permute-done | bytes 32800 | tf_op jit(solution)/shard_map/ppermute | solution.py:35
  45.5 1.2 %shard_map.73 = (f32[16,640]{1,0:T(8,128)S(1)}, f32[32,16,128]{2,1,0:T(8,128)}) custom-call(f32[16,512]{1,0:T(8,128)S(1)} %get-tuple-element.29.refs_0_, f32[16,128]{1,0:T(8,128)S(1)} %get-tuple-element.30.refs_1_, f32[16,640]{1,0:T(8,128)S(1)} %collective-permute-done.15.refs_2_, f32[16,640]{1,0:T(8,128)S(1)} %collective-permute-done.16.refs_3_, ...), custom_call_target="tpu_custom_call" | custom-call | tf_op jit(solution)/shard_map/pallas_call | solution.py:330
  46.7 3.1 %all-to-all-start = ((f32[32,16,128]{2,1,0:T(8,128)}), f32[32,16,128]{2,1,0:T(8,128)S(1)}, u32[]{:S(2)}, u32[]{:S(2)}) async-start(f32[32,16,128]{2,1,0:T(8,128)} %get-tuple-element.35), calls=%async_computation | async-start | bytes 524288 | tf_op jit(solution)/shard_map/all_to_all | solution.py:393
  49.8 1.8 %collective-permute-start.23 = (f32[16,640]{1,0:T(8,128)S(1)}, f32[16,640]{1,0:T(8,128)S(1)}, u32[]{:S(2)}, u32[]{:S(2)}) collective-permute-start(f32[16,640]{1,0:T(8,128)S(1)} %get-tuple-element.36.refs_0_.refs_4_), channel_id=1, source_target_pairs={{0,2},{1,3},{2,0},{3,1},{4,6},{5,7},{6,4},{7,5},{8,10},{9,11},{10,... | collective-permute-start | bytes 122888 | tf_op jit(solution)/shard_map/ppermute | solution.py:35
  51.7 3.2 %collective-permute-done.23.refs_2_.refs_6_ = f32[16,640]{1,0:T(8,128)S(1)} collective-permute-done((f32[16,640]{1,0:T(8,128)S(1)}, f32[16,640]{1,0:T(8,128)S(1)}, u32[]{:S(2)}, u32[]{:S(2)}) %collective-permute-start.23) | collective-permute-done | bytes 40992 | tf_op jit(solution)/shard_map/ppermute | solution.py:35
  54.9 1.2 %collective-permute-done.24.refs_3_.refs_7_ = f32[16,640]{1,0:T(8,128)S(1)} collective-permute-done((f32[16,640]{1,0:T(8,128)S(1)}, f32[16,640]{1,0:T(8,128)S(1)}, u32[]{:S(2)}, u32[]{:S(2)}) %collective-permute-start.24) | collective-permute-done | bytes 40992 | tf_op jit(solution)/shard_map/ppermute | solution.py:35
  56.1 2.6 %shard_map.74 = (f32[64,64]{1,0:T(8,128)S(1)}, f32[64,16]{1,0:T(8,128)S(1)}, f32[64,16]{1,0:T(8,128)S(1)}) custom-call(f32[16,640]{1,0:T(8,128)S(1)} %get-tuple-element.36.refs_0_.refs_4_, f32[16,640]{1,0:T(8,128)S(1)} %collective-permute-done.22.refs_1_.refs_5_, f32[16,640]{1,0:T(8,128)S(1)} %collective-permute-done.23.refs_2_.refs_6_, ...), custom_call_target="tpu_custom_call" | custom-call | flops 1048576 | bytes 655360 | tf_op jit(solution)/shard_map/pallas_call | solution.py:330
  58.6 1.8 %all-to-all-done.refs_0_ = f32[32,16,128]{2,1,0:T(8,128)S(1)} async-done(((f32[32,16,128]{2,1,0:T(8,128)}), f32[32,16,128]{2,1,0:T(8,128)S(1)}, u32[]{:S(2)}, u32[]{:S(2)}) %all-to-all-start) | async-done | bytes 262176 | tf_op jit(solution)/shard_map/all_to_all | solution.py:393
  60.4 4.0 %shard_map.75 = (f32[16,512]{1,0:T(8,128)}, f32[16,512]{1,0:T(8,128)}) custom-call(f32[32,16,128]{2,1,0:T(8,128)S(1)} %all-to-all-done.refs_0_, f32[64,64]{1,0:T(8,128)S(1)} %get-tuple-element.37.refs_1_, f32[64,16]{1,0:T(8,128)S(1)} %get-tuple-element.38.refs_2_, f32[64,16]{1,0:T(8,128)S(1)} %get-tuple-element.39.refs_3_, ...), custom_call_target="tpu_custom_call" | custom-call | tf_op jit(solution)/shard_map/pallas_call | solution.py:330
  (14 shorter events, 0.0 us)
Async XLA Ops:
  0.6 11.6 %copy-start = (f32[16,512]{1,0:T(8,128)S(1)}, f32[16,512]{1,0:T(8,128)}, u32[]{:S(2)}) copy-start(f32[16,512]{1,0:T(8,128)} %refs_8_.1) | copy-start | bytes 98308
  0.6 11.0 %collective-permute-start = (f32[16,512]{1,0:T(8,128)}, f32[16,512]{1,0:T(8,128)S(1)}, u32[]{:S(2)}, u32[]{:S(2)}) collective-permute-start(f32[16,512]{1,0:T(8,128)} %refs_8_.1), channel_id=1, source_target_pairs={{0,8},{8,0},{16,24},{24,16},{1,9},{9,1},{17,25},{25,17},{2,10},{10... | collective-permute-start | bytes 98312 | tf_op jit(solution)/shard_map/ppermute | solution.py:35
  3.8 7.9 %collective-permute-start.1 = (f32[16,512]{1,0:T(8,128)}, f32[16,512]{1,0:T(8,128)S(1)}, u32[]{:S(2)}, u32[]{:S(2)}) collective-permute-start(f32[16,512]{1,0:T(8,128)} %refs_8_.1), channel_id=1, source_target_pairs={{0,16},{8,24},{16,0},{24,8},{1,17},{9,25},{17,1},{25,9},{2,18},{10... | collective-permute-start | bytes 98312 | tf_op jit(solution)/shard_map/ppermute | solution.py:35
  6.3 5.9 %collective-permute-start.2 = (f32[16,512]{1,0:T(8,128)}, f32[16,512]{1,0:T(8,128)S(1)}, u32[]{:S(2)}, u32[]{:S(2)}) collective-permute-start(f32[16,512]{1,0:T(8,128)} %refs_8_.1), channel_id=1, source_target_pairs={{0,24},{8,16},{16,8},{24,0},{1,25},{9,17},{17,9},{25,1},{2,26},{10... | collective-permute-start | bytes 98312 | tf_op jit(solution)/shard_map/ppermute | solution.py:35
  6.4 5.9 %collective-permute-start.3 = (f32[16,512]{1,0:T(8,128)}, f32[16,512]{1,0:T(8,128)S(1)}, u32[]{:S(2)}, u32[]{:S(2)}) collective-permute-start(f32[16,512]{1,0:T(8,128)} %refs_8_.1), channel_id=1, source_target_pairs={{0,4},{4,0},{1,5},{5,1},{2,6},{6,2},{3,7},{7,3},{8,12},{12,8},{9,1... | collective-permute-start | bytes 98312 | tf_op jit(solution)/shard_map/ppermute | solution.py:35
  14.6 7.5 %collective-permute-start.4 = (f32[16,512]{1,0:T(8,128)S(1)}, f32[16,512]{1,0:T(8,128)S(1)}, u32[]{:S(2)}, u32[]{:S(2)}) collective-permute-start(f32[16,512]{1,0:T(8,128)S(1)} %get-tuple-element.24), channel_id=1, source_target_pairs={{0,8},{8,0},{16,24},{24,16},{1,9},{9,1},{17,25},{25,17},{2,10},{10... | collective-permute-start | bytes 98312 | tf_op jit(solution)/shard_map/ppermute | solution.py:35
  14.8 7.3 %collective-permute-start.9 = (f32[16,512]{1,0:T(8,128)S(1)}, f32[16,512]{1,0:T(8,128)S(1)}, u32[]{:S(2)}, u32[]{:S(2)}) collective-permute-start(f32[16,512]{1,0:T(8,128)S(1)} %get-tuple-element.28), channel_id=1, source_target_pairs={{0,2},{1,3},{2,0},{3,1},{4,6},{5,7},{6,4},{7,5},{8,10},{9,11},{10,... | collective-permute-start | bytes 98312 | tf_op jit(solution)/shard_map/ppermute | solution.py:35
  16.3 6.3 %collective-permute-start.5 = (f32[16,512]{1,0:T(8,128)S(1)}, f32[16,512]{1,0:T(8,128)S(1)}, u32[]{:S(2)}, u32[]{:S(2)}) collective-permute-start(f32[16,512]{1,0:T(8,128)S(1)} %get-tuple-element.25), channel_id=1, source_target_pairs={{0,16},{8,24},{16,0},{24,8},{1,17},{9,25},{17,1},{25,9},{2,18},{10... | collective-permute-start | bytes 98312 | tf_op jit(solution)/shard_map/ppermute | solution.py:35
  19.7 5.7 %collective-permute-start.6 = (f32[16,512]{1,0:T(8,128)S(1)}, f32[16,512]{1,0:T(8,128)S(1)}, u32[]{:S(2)}, u32[]{:S(2)}) collective-permute-start(f32[16,512]{1,0:T(8,128)S(1)} %get-tuple-element.26), channel_id=1, source_target_pairs={{0,24},{8,16},{16,8},{24,0},{1,25},{9,17},{17,9},{25,1},{2,26},{10... | collective-permute-start | bytes 98312 | tf_op jit(solution)/shard_map/ppermute | solution.py:35
  20.5 4.9 %collective-permute-start.7 = (f32[16,512]{1,0:T(8,128)S(1)}, f32[16,512]{1,0:T(8,128)S(1)}, u32[]{:S(2)}, u32[]{:S(2)}) collective-permute-start(f32[16,512]{1,0:T(8,128)S(1)} %get-tuple-element.27), channel_id=1, source_target_pairs={{0,4},{4,0},{1,5},{5,1},{2,6},{6,2},{3,7},{7,3},{8,12},{12,8},{9,1... | collective-permute-start | bytes 98312 | tf_op jit(solution)/shard_map/ppermute | solution.py:35
  22.1 3.5 %collective-permute-start.8 = (f32[16,512]{1,0:T(8,128)S(1)}, f32[16,512]{1,0:T(8,128)S(1)}, u32[]{:S(2)}, u32[]{:S(2)}) collective-permute-start(f32[16,512]{1,0:T(8,128)S(1)} %get-tuple-element.28), channel_id=1, source_target_pairs={{0,1},{1,0},{2,3},{3,2},{4,5},{5,4},{6,7},{7,6},{8,9},{9,8},{10,11... | collective-permute-start | bytes 98312 | tf_op jit(solution)/shard_map/ppermute | solution.py:35
  22.1 3.5 %collective-permute-start.10 = (f32[16,512]{1,0:T(8,128)S(1)}, f32[16,512]{1,0:T(8,128)S(1)}, u32[]{:S(2)}, u32[]{:S(2)}) collective-permute-start(f32[16,512]{1,0:T(8,128)S(1)} %collective-permute-done.9.refs_3_.refs_8_.refs_10_), channel_id=1, source_target_pairs={{0,1},{1,0},{2,3},{3,2},{4,5},{5,4},{6,7},{7,6},{8,9},{9,8},{10,11... | collective-permute-start | bytes 98312 | tf_op jit(solution)/shard_map/ppermute | solution.py:35
  25.5 5.9 %collective-permute-start.11 = (f32[16,512]{1,0:T(8,128)S(1)}, f32[16,512]{1,0:T(8,128)S(1)}, u32[]{:S(2)}, u32[]{:S(2)}) collective-permute-start(f32[16,512]{1,0:T(8,128)S(1)} %shard_map.70.refs_0_.refs_10_.refs_12_), channel_id=1, source_target_pairs={{0,8},{8,0},{16,24},{24,16},{1,9},{9,1},{17,25},{25,17},{2,10},{10... | collective-permute-start | bytes 98312 | tf_op jit(solution)/shard_map/ppermute | solution.py:35
  26.0 8.8 %collective-permute-start.14 = (f32[16,640]{1,0:T(8,128)S(1)}, f32[16,640]{1,0:T(8,128)S(1)}, u32[]{:S(2)}, u32[]{:S(2)}) collective-permute-start(f32[16,640]{1,0:T(8,128)S(1)} %shard_map.71.refs_2_), channel_id=1, source_target_pairs={{0,4},{4,0},{1,5},{5,1},{2,6},{6,2},{3,7},{7,3},{8,12},{12,8},{9,1... | collective-permute-start | bytes 122888 | tf_op jit(solution)/shard_map/ppermute | solution.py:35
  26.5 5.0 %collective-permute-start.12 = (f32[16,512]{1,0:T(8,128)S(1)}, f32[16,512]{1,0:T(8,128)S(1)}, u32[]{:S(2)}, u32[]{:S(2)}) collective-permute-start(f32[16,512]{1,0:T(8,128)S(1)} %shard_map.70.refs_0_.refs_10_.refs_12_), channel_id=1, source_target_pairs={{0,16},{8,24},{16,0},{24,8},{1,17},{9,25},{17,1},{25,9},{2,18},{10... | collective-permute-start | bytes 98312 | tf_op jit(solution)/shard_map/ppermute | solution.py:35
  29.1 5.7 %collective-permute-start.13 = (f32[16,512]{1,0:T(8,128)S(1)}, f32[16,512]{1,0:T(8,128)S(1)}, u32[]{:S(2)}, u32[]{:S(2)}) collective-permute-start(f32[16,512]{1,0:T(8,128)S(1)} %shard_map.70.refs_0_.refs_10_.refs_12_), channel_id=1, source_target_pairs={{0,24},{8,16},{16,8},{24,0},{1,25},{9,17},{17,9},{25,1},{2,26},{10... | collective-permute-start | bytes 98312 | tf_op jit(solution)/shard_map/ppermute | solution.py:35
  30.9 10.7 %collective-permute-start.20 = (f32[16,512]{1,0:T(8,128)S(1)}, f32[16,512]{1,0:T(8,128)S(1)}, u32[]{:S(2)}, u32[]{:S(2)}) collective-permute-start(f32[16,512]{1,0:T(8,128)S(1)} %shard_map.70.refs_0_.refs_10_.refs_12_), channel_id=1, source_target_pairs={{0,2},{1,3},{2,0},{3,1},{4,6},{5,7},{6,4},{7,5},{8,10},{9,11},{10,... | collective-permute-start | bytes 98312 | tf_op jit(solution)/shard_map/ppermute | solution.py:35
  31.4 10.1 %collective-permute-start.19 = (f32[16,512]{1,0:T(8,128)S(1)}, f32[16,512]{1,0:T(8,128)S(1)}, u32[]{:S(2)}, u32[]{:S(2)}) collective-permute-start(f32[16,512]{1,0:T(8,128)S(1)} %shard_map.70.refs_0_.refs_10_.refs_12_), channel_id=1, source_target_pairs={{0,1},{1,0},{2,3},{3,2},{4,5},{5,4},{6,7},{7,6},{8,9},{9,8},{10,11... | collective-permute-start | bytes 98312 | tf_op jit(solution)/shard_map/ppermute | solution.py:35
  37.1 8.4 %collective-permute-start.15 = (f32[16,640]{1,0:T(8,128)S(1)}, f32[16,640]{1,0:T(8,128)S(1)}, u32[]{:S(2)}, u32[]{:S(2)}) collective-permute-start(f32[16,640]{1,0:T(8,128)S(1)} %get-tuple-element.31), channel_id=1, source_target_pairs={{0,8},{8,0},{16,24},{24,16},{1,9},{9,1},{17,25},{25,17},{2,10},{10... | collective-permute-start | bytes 122888 | tf_op jit(solution)/shard_map/ppermute | solution.py:35
  37.2 8.4 %collective-permute-start.16 = (f32[16,640]{1,0:T(8,128)S(1)}, f32[16,640]{1,0:T(8,128)S(1)}, u32[]{:S(2)}, u32[]{:S(2)}) collective-permute-start(f32[16,640]{1,0:T(8,128)S(1)} %get-tuple-element.32), channel_id=1, source_target_pairs={{0,16},{8,24},{16,0},{24,8},{1,17},{9,25},{17,1},{25,9},{2,18},{10... | collective-permute-start | bytes 122888 | tf_op jit(solution)/shard_map/ppermute | solution.py:35
  39.5 6.0 %collective-permute-start.17 = (f32[16,640]{1,0:T(8,128)S(1)}, f32[16,640]{1,0:T(8,128)S(1)}, u32[]{:S(2)}, u32[]{:S(2)}) collective-permute-start(f32[16,640]{1,0:T(8,128)S(1)} %get-tuple-element.33), channel_id=1, source_target_pairs={{0,24},{8,16},{16,8},{24,0},{1,25},{9,17},{17,9},{25,1},{2,26},{10... | collective-permute-start | bytes 122888 | tf_op jit(solution)/shard_map/ppermute | solution.py:35
  41.5 1.6 %collective-permute-start.21 = (f32[16,512]{1,0:T(8,128)S(1)}, f32[16,512]{1,0:T(8,128)S(1)}, u32[]{:S(2)}, u32[]{:S(2)}) collective-permute-start(f32[16,512]{1,0:T(8,128)S(1)} %collective-permute-done.20.refs_12_.refs_14_), channel_id=1, source_target_pairs={{0,1},{1,0},{2,3},{3,2},{4,5},{5,4},{6,7},{7,6},{8,9},{9,8},{10,11... | collective-permute-start | bytes 98312 | tf_op jit(solution)/shard_map/ppermute | solution.py:35
  41.5 4.0 %collective-permute-start.18 = (f32[16,512]{1,0:T(8,128)S(1)}, f32[16,512]{1,0:T(8,128)S(1)}, u32[]{:S(2)}, u32[]{:S(2)}) collective-permute-start(f32[16,512]{1,0:T(8,128)S(1)} %get-tuple-element.34), channel_id=1, source_target_pairs={{0,4},{4,0},{1,5},{5,1},{2,6},{6,2},{3,7},{7,3},{8,12},{12,8},{9,1... | collective-permute-start | bytes 98312 | tf_op jit(solution)/shard_map/ppermute | solution.py:35
  46.7 13.7 %all-to-all-start = ((f32[32,16,128]{2,1,0:T(8,128)}), f32[32,16,128]{2,1,0:T(8,128)S(1)}, u32[]{:S(2)}, u32[]{:S(2)}) async-start(f32[32,16,128]{2,1,0:T(8,128)} %get-tuple-element.35), calls=%async_computation | async-start | bytes 524288 | tf_op jit(solution)/shard_map/all_to_all | solution.py:393
  49.8 5.0 %collective-permute-start.23 = (f32[16,640]{1,0:T(8,128)S(1)}, f32[16,640]{1,0:T(8,128)S(1)}, u32[]{:S(2)}, u32[]{:S(2)}) collective-permute-start(f32[16,640]{1,0:T(8,128)S(1)} %get-tuple-element.36.refs_0_.refs_4_), channel_id=1, source_target_pairs={{0,2},{1,3},{2,0},{3,1},{4,6},{5,7},{6,4},{7,5},{8,10},{9,11},{10,... | collective-permute-start | bytes 122888 | tf_op jit(solution)/shard_map/ppermute | solution.py:35
  51.7 3.2 %collective-permute-start.22 = (f32[16,640]{1,0:T(8,128)S(1)}, f32[16,640]{1,0:T(8,128)S(1)}, u32[]{:S(2)}, u32[]{:S(2)}) collective-permute-start(f32[16,640]{1,0:T(8,128)S(1)} %get-tuple-element.36.refs_0_.refs_4_), channel_id=1, source_target_pairs={{0,1},{1,0},{2,3},{3,2},{4,5},{5,4},{6,7},{7,6},{8,9},{9,8},{10,11... | collective-permute-start | bytes 122888 | tf_op jit(solution)/shard_map/ppermute | solution.py:35
  54.9 1.2 %collective-permute-start.24 = (f32[16,640]{1,0:T(8,128)S(1)}, f32[16,640]{1,0:T(8,128)S(1)}, u32[]{:S(2)}, u32[]{:S(2)}) collective-permute-start(f32[16,640]{1,0:T(8,128)S(1)} %collective-permute-done.23.refs_2_.refs_6_), channel_id=1, source_target_pairs={{0,1},{1,0},{2,3},{3,2},{4,5},{5,4},{6,7},{7,6},{8,9},{9,8},{10,11... | collective-permute-start | bytes 122888 | tf_op jit(solution)/shard_map/ppermute | solution.py:35

commit v5 on v4

--- a/solution.py
+++ b/solution.py
@@ -213,9 +213,10 @@
     third = dot_nt(total, fields[0][...])
     stack_fields(fields[0], image_refs[0], image_refs[1:])
     fourth = dot_nt(total, fields[0][...])
-    late = jnp.concatenate([third, fourth], axis=1)
+    width = total.shape[0]
+    packed = [jnp.concatenate([g[: width // 2], g[width // 2 :]], axis=1) for g in (third, fourth)]
     for i in range(out_gram[0].shape[0]):
-        out_gram[0][i] = late
+        out_gram[0][i] = packed[i % n_depth % 2]
 
 
 def factor_two(e):
@@ -298,21 +299,36 @@
     outs[2][...] = dot_nt(identity_of(size), wide_refs[0][:, points + size : points + 2 * size])
 
 
+def late_total(n_depth, gathered_ref, out_ref):
+    rows = gathered_ref.shape[1]
+    groups = gathered_ref.shape[0] // n_depth
+    for d in range(n_depth):
+        out_ref[d * rows : (d + 1) * rows, :] = sum(gathered_ref[g * n_depth + d] for g in range(groups))
+
+
+def unpacked(packed, rows):
+    size = packed.shape[1] // 2
+    parts = []
+    for at in range(0, packed.shape[0], rows):
+        part = packed[at : at + rows]
+        parts += [part[:, :size], part[:, size:]]
+    return jnp.concatenate(parts, axis=0)
+
+
 def finish(n_depth, *refs):
-    gathered, solved, wide_refs, base_refs, image_refs, outs, scratch = split(
-        refs, 1, 3, n_depth, n_depth, n_depth, 2, 3
+    late, solved, wide_refs, base_refs, image_refs, outs, scratch = split(
+        refs, 2, 3, n_depth, n_depth, n_depth, 2, 3
     )
     base, image, mapped = scratch
     solution_out, residual_out = outs
     width, _ = solution_out.shape
     size = n_depth * width
-    groups = gathered[0].shape[0] // n_depth
     stack_fields(base, base_refs[0], base_refs[1:])
     stack_fields(image, image_refs[0], image_refs[1:])
     stack_fields(mapped, wide_refs[0], wide_refs[1:])
-    late = [sum(gathered[0][g * n_depth + d] for g in range(groups)) for d in range(n_depth)]
-    late = jnp.concatenate(late, axis=0)
-    gram2, gram3 = late[:, :size], late[:, size:]
+    mine, other = (unpacked(ref[...], width // 2) for ref in late)
+    even = lax.axis_index("depth") % 2 == 0
+    gram2, gram3 = jnp.where(even, mine, other), jnp.where(even, other, mine)
     inverse, start, gram1_own = (ref[...] for ref in solved)
     carry = dot_nn(inverse, gram2)
     schur = gram3 - dot_nn(gram2, carry)
@@ -387,7 +403,7 @@
     n_all = n_row * n_col * n_depth
     mapped, late = call(
         functools.partial(second_combine, n_row, n_col, n_depth),
-        [partial, gram] + z + y + base + image, [], [wide, (n_all,) + tail], [fields],
+        [partial, gram] + z + y + base + image, [], [wide, (n_all, width // 2, 2 * size)], [fields],
     )
     mapped = [mapped] + collect(mapped, "depth")
     late = lax.all_to_all(late, ("row", "col", "depth"), 0, 0)
@@ -396,9 +412,11 @@
         [square, (size, width), (size, width)], [pltpu.VMEM(square, f32)],
         pl.CostEstimate(flops=4 * size**3, transcendentals=0, bytes_accessed=160 * size * size),
     )
+    (late,) = call(functools.partial(late_total, n_depth), [late], [], [(size // 2, 2 * size)], [])
+    other = lax.ppermute(late, "depth", [(i, i ^ 1) for i in range(n_depth)])
     solution, residual = call(
         functools.partial(finish, n_depth),
-        [late] + list(solved) + mapped + base + image, [], [narrow, narrow], [fields, fields, fields],
+        [late, other] + list(solved) + mapped + base + image, [], [narrow, narrow], [fields, fields, fields],
     )
     return solution, residual
 

time: 64.6 us -> 65 us (level)
    all_to_all x1, waiting for transfers between devices: 1.77 us -> 3.96 us  [per_device(): late = lax.all_to_all(late, ('row', 'col', 'depth'), 0, 0)]
    ppermute x25, waiting for transfers between devices: 13.7 us -> 11.7 us  [send(): lax.ppermute(x, axis, [(i, partner(i, step, size)) for i in range(size)])]
    pallas_call x8 -> x9, Pallas kernels: 15.6 us -> 15.5 us  [call(): pl.pallas_call(body, out_shape=[s if hasattr(s, 'dtype') else jax.ShapeDt...]
  transfers between devices with their start and end apart: 26 -> 27, of which waited for: 8 -> 7; matrix products, arithmetic and copies ran while one was open for 0% -> 0% of each run, Pallas kernels for 13% -> 13%
where the time goes in v5:
time: 65 us; the launch traced here: 64.7 us
  starting transfers between devices  32.2 us (50%)
  waiting for transfers between devices  15.7 us (24%)
  Pallas kernels  15.5 us (24%)
  between operations  1.42 us (2%)
    ppermute x25, starting transfers between devices, send(): lax.ppermute(x, axis, [(i, partner(i, step, size)) for i in range(size)])  28.8 us
    pallas_call x9, Pallas kernels, call(): pl.pallas_call(body, out_shape=[s if hasattr(s, 'dtype') else jax.ShapeDt...  15.5 us
    ppermute x25, waiting for transfers between devices, send(): lax.ppermute(x, axis, [(i, partner(i, step, size)) for i in range(size)])  11.7 us
    all_to_all x1, waiting for transfers between devices, per_device(): late = lax.all_to_all(late, ('row', 'col', 'depth'), 0, 0)  3.96 us
    all_to_all x1, starting transfers between devices, per_device(): late = lax.all_to_all(late, ('row', 'col', 'depth'), 0, 0)  3.13 us
  transfers between devices with their start and end apart: 27, of which 7 were waited for; matrix products, arithmetic and copies ran while one was open for 0% of the time, Pallas kernels for 13%

profile of v5, /device:TPU:0, one launch (start us, length us, event | category | flops | bytes accessed | tf_op | source)
XLA Modules:
  0.0 64.7 jit_solution(11484784232836422581)
XLA Ops:
  0.6 3.1 %collective-permute-start = (f32[16,512]{1,0:T(8,128)}, f32[16,512]{1,0:T(8,128)S(1)}, u32[]{:S(2)}, u32[]{:S(2)}) collective-permute-start(f32[16,512]{1,0:T(8,128)} %refs_9_.1), channel_id=1, source_target_pairs={{0,8},{8,0},{16,24},{24,16},{1,9},{9,1},{17,25},{25,17},{2,10},{10... | collective-permute-start | bytes 98312 | tf_op jit(solution)/shard_map/ppermute | solution.py:35
  3.8 2.6 %collective-permute-start.1 = (f32[16,512]{1,0:T(8,128)}, f32[16,512]{1,0:T(8,128)S(1)}, u32[]{:S(2)}, u32[]{:S(2)}) collective-permute-start(f32[16,512]{1,0:T(8,128)} %refs_9_.1), channel_id=1, source_target_pairs={{0,16},{8,24},{16,0},{24,8},{1,17},{9,25},{17,1},{25,9},{2,18},{10... | collective-permute-start | bytes 98312 | tf_op jit(solution)/shard_map/ppermute | solution.py:35
  6.4 1.7 %collective-permute-start.3 = (f32[16,512]{1,0:T(8,128)}, f32[16,512]{1,0:T(8,128)S(1)}, u32[]{:S(2)}, u32[]{:S(2)}) collective-permute-start(f32[16,512]{1,0:T(8,128)} %refs_9_.1), channel_id=1, source_target_pairs={{0,4},{4,0},{1,5},{5,1},{2,6},{6,2},{3,7},{7,3},{8,12},{12,8},{9,1... | collective-permute-start | bytes 98312 | tf_op jit(solution)/shard_map/ppermute | solution.py:35
  8.7 2.9 %shard_map.68 = (f32[16,256,256]{2,1,0:T(8,128)S(1)}, s32[3,16]{1,0:T(4,128)S(1)}) custom-call(s32[1,1]{1,0:T(1,128)S(6)} %copy.7.count_ref, s32[1,1,16]{2,1,0:T(1,128)} %rows_ref.1, s32[1,1,16]{2,1,0:T(1,128)} %cols_ref.1, f32[1,1,16,256,256]{4,3,2,1,0:T(8,128)} %blocks_ref.1), custom_call_target="tpu_custom_call" | custom-call | bytes 8388608 | tf_op jit(solution)/shard_map/pallas_call | solution.py:346
  11.7 0.0 collective-permute-done.refs_3_
  11.7 0.0 collective-permute-done.1.refs_4_
  11.7 0.6 collective-permute-done.2.refs_5_
  12.3 0.0 collective-permute-done.3.refs_6_
  12.3 2.3 %shard_map.69 = (f32[16,512]{1,0:T(8,128)S(1)}, f32[16,512]{1,0:T(8,128)S(1)}, f32[16,512]{1,0:T(8,128)S(1)}, f32[16,512]{1,0:T(8,128)S(1)}, f32[16,512]{1,0:T(8,128)S(1)}, /*index=5*/f32[16,512]{1,0:T(8,128)S(1)}) custom-call(s32[3,16]{1,0:T(4,128)S(1)} %get-tuple-element.21.refs_0_, f32[16,256,256]{2,1,0:T(8,128)S(1)} %get-tuple-element.22.refs_1_, ...), custom_call_target="tpu_custom_call" | custom-call | tf_op jit(solution)/shard_map/pallas_call | solution.py:346
  14.6 0.2 collective-permute-start.4
  14.8 1.5 %collective-permute-start.9 = (f32[16,512]{1,0:T(8,128)S(1)}, f32[16,512]{1,0:T(8,128)S(1)}, u32[]{:S(2)}, u32[]{:S(2)}) collective-permute-start(f32[16,512]{1,0:T(8,128)S(1)} %get-tuple-element.28), channel_id=1, source_target_pairs={{0,2},{1,3},{2,0},{3,1},{4,6},{5,7},{6,4},{7,5},{8,10},{9,11},{10,... | collective-permute-start | bytes 98312 | tf_op jit(solution)/shard_map/ppermute | solution.py:35
  16.3 3.5 %collective-permute-start.5 = (f32[16,512]{1,0:T(8,128)S(1)}, f32[16,512]{1,0:T(8,128)S(1)}, u32[]{:S(2)}, u32[]{:S(2)}) collective-permute-start(f32[16,512]{1,0:T(8,128)S(1)} %get-tuple-element.25), channel_id=1, source_target_pairs={{0,16},{8,24},{16,0},{24,8},{1,17},{9,25},{17,1},{25,9},{2,18},{10... | collective-permute-start | bytes 98312 | tf_op jit(solution)/shard_map/ppermute | solution.py:35
  19.7 0.8 %collective-permute-start.6 = (f32[16,512]{1,0:T(8,128)S(1)}, f32[16,512]{1,0:T(8,128)S(1)}, u32[]{:S(2)}, u32[]{:S(2)}) collective-permute-start(f32[16,512]{1,0:T(8,128)S(1)} %get-tuple-element.26), channel_id=1, source_target_pairs={{0,24},{8,16},{16,8},{24,0},{1,25},{9,17},{17,9},{25,1},{2,26},{10... | collective-permute-start | bytes 98312 | tf_op jit(solution)/shard_map/ppermute | solution.py:35
  20.5 1.5 %collective-permute-start.7 = (f32[16,512]{1,0:T(8,128)S(1)}, f32[16,512]{1,0:T(8,128)S(1)}, u32[]{:S(2)}, u32[]{:S(2)}) collective-permute-start(f32[16,512]{1,0:T(8,128)S(1)} %get-tuple-element.27), channel_id=1, source_target_pairs={{0,4},{4,0},{1,5},{5,1},{2,6},{6,2},{3,7},{7,3},{8,12},{12,8},{9,1... | collective-permute-start | bytes 98312 | tf_op jit(solution)/shard_map/ppermute | solution.py:35
  22.1 0.0 collective-permute-done.4.refs_1_
  22.1 0.0 collective-permute-start.8
  22.1 0.0 collective-permute-done.9.refs_3_.refs_8_.refs_11_
  22.1 0.5 collective-permute-start.10
  22.6 0.0 collective-permute-done.5.refs_2_
  22.6 2.9 %collective-permute-done.6.refs_3_ = f32[16,512]{1,0:T(8,128)S(1)} collective-permute-done((f32[16,512]{1,0:T(8,128)S(1)}, f32[16,512]{1,0:T(8,128)S(1)}, u32[]{:S(2)}, u32[]{:S(2)}) %collective-permute-start.6) | collective-permute-done | bytes 32800 | tf_op jit(solution)/shard_map/ppermute | solution.py:35
  25.5 0.0 collective-permute-done.7.refs_4_
  25.5 0.1 collective-permute-start.11
  25.6 0.0 collective-permute-done.10.refs_4_.refs_9_.refs_12_
  25.6 0.4 shard_map.71.refs_2_
  26.0 0.5 collective-permute-start.14
  26.5 2.5 %collective-permute-start.12 = (f32[16,512]{1,0:T(8,128)S(1)}, f32[16,512]{1,0:T(8,128)S(1)}, u32[]{:S(2)}, u32[]{:S(2)}) collective-permute-start(f32[16,512]{1,0:T(8,128)S(1)} %shard_map.70.refs_0_.refs_10_.refs_13_), channel_id=1, source_target_pairs={{0,16},{8,24},{16,0},{24,8},{1,17},{9,25},{17,1},{25,9},{2,18},{10... | collective-permute-start | bytes 98312 | tf_op jit(solution)/shard_map/ppermute | solution.py:35
  29.1 1.8 %collective-permute-start.13 = (f32[16,512]{1,0:T(8,128)S(1)}, f32[16,512]{1,0:T(8,128)S(1)}, u32[]{:S(2)}, u32[]{:S(2)}) collective-permute-start(f32[16,512]{1,0:T(8,128)S(1)} %shard_map.70.refs_0_.refs_10_.refs_13_), channel_id=1, source_target_pairs={{0,24},{8,16},{16,8},{24,0},{1,25},{9,17},{17,9},{25,1},{2,26},{10... | collective-permute-start | bytes 98312 | tf_op jit(solution)/shard_map/ppermute | solution.py:35
  30.9 0.5 collective-permute-start.20
  31.4 0.0 collective-permute-done.11.refs_3_
  31.4 0.0 collective-permute-start.19
  31.4 0.1 collective-permute-done.12.refs_4_
  31.5 3.2 %collective-permute-done.13.refs_5_ = f32[16,512]{1,0:T(8,128)S(1)} collective-permute-done((f32[16,512]{1,0:T(8,128)S(1)}, f32[16,512]{1,0:T(8,128)S(1)}, u32[]{:S(2)}, u32[]{:S(2)}) %collective-permute-start.13) | collective-permute-done | bytes 32800 | tf_op jit(solution)/shard_map/ppermute | solution.py:35
  34.8 2.3 %shard_map.72 = (f32[16,512]{1,0:T(8,128)S(1)}, f32[16,128]{1,0:T(8,128)S(1)}, f32[16,640]{1,0:T(8,128)S(1)}, f32[16,640]{1,0:T(8,128)S(1)}, f32[16,640]{1,0:T(8,128)S(1)}, /*index=5*/f32[16,512]{1,0:T(8,128)S(1)}) custom-call(s32[3,16]{1,0:T(4,128)S(1)} %get-tuple-element.21.refs_0_, f32[16,256,256]{2,1,0:T(8,128)S(1)} %get-tuple-element.22.refs_1_, ...), custom_call_target="tpu_custom_call" | custom-call | tf_op jit(solution)/shard_map/pallas_call | solution.py:346
  37.1 0.1 collective-permute-start.15
  37.2 2.4 %collective-permute-start.16 = (f32[16,640]{1,0:T(8,128)S(1)}, f32[16,640]{1,0:T(8,128)S(1)}, u32[]{:S(2)}, u32[]{:S(2)}) collective-permute-start(f32[16,640]{1,0:T(8,128)S(1)} %get-tuple-element.32), channel_id=1, source_target_pairs={{0,16},{8,24},{16,0},{24,8},{1,17},{9,25},{17,1},{25,9},{2,18},{10... | collective-permute-start | bytes 122888 | tf_op jit(solution)/shard_map/ppermute | solution.py:35
  39.5 2.0 %collective-permute-start.17 = (f32[16,640]{1,0:T(8,128)S(1)}, f32[16,640]{1,0:T(8,128)S(1)}, u32[]{:S(2)}, u32[]{:S(2)}) collective-permute-start(f32[16,640]{1,0:T(8,128)S(1)} %get-tuple-element.33), channel_id=1, source_target_pairs={{0,24},{8,16},{16,8},{24,0},{1,25},{9,17},{17,9},{25,1},{2,26},{10... | collective-permute-start | bytes 122888 | tf_op jit(solution)/shard_map/ppermute | solution.py:35
  41.5 0.0 collective-permute-done.20.refs_12_.refs_15_
  41.5 0.0 collective-permute-start.21
  41.5 1.6 %collective-permute-start.18 = (f32[16,512]{1,0:T(8,128)S(1)}, f32[16,512]{1,0:T(8,128)S(1)}, u32[]{:S(2)}, u32[]{:S(2)}) collective-permute-start(f32[16,512]{1,0:T(8,128)S(1)} %get-tuple-element.34), channel_id=1, source_target_pairs={{0,4},{4,0},{1,5},{5,1},{2,6},{6,2},{3,7},{7,3},{8,12},{12,8},{9,1... | collective-permute-start | bytes 98312 | tf_op jit(solution)/shard_map/ppermute | solution.py:35
  43.1 2.4 %collective-permute-done.18.refs_5_ = f32[16,512]{1,0:T(8,128)S(1)} collective-permute-done((f32[16,512]{1,0:T(8,128)S(1)}, f32[16,512]{1,0:T(8,128)S(1)}, u32[]{:S(2)}, u32[]{:S(2)}) %collective-permute-start.18) | collective-permute-done | bytes 32800 | tf_op jit(solution)/shard_map/ppermute | solution.py:35
  45.5 1.1 %shard_map.73 = (f32[16,640]{1,0:T(8,128)S(1)}, f32[32,8,128]{2,1,0:T(8,128)}) custom-call(f32[16,512]{1,0:T(8,128)S(1)} %get-tuple-element.29.refs_0_, f32[16,128]{1,0:T(8,128)S(1)} %get-tuple-element.30.refs_1_, f32[16,640]{1,0:T(8,128)S(1)} %collective-permute-done.15.refs_2_, f32[16,640]{1,0:T(8,128)S(1)} %collective-permute-done.16.refs_3_, ...), custom_call_target="tpu_custom_call" | custom-call | tf_op jit(solution)/shard_map/pallas_call | solution.py:346
  46.6 3.1 %all-to-all-start = ((f32[32,8,128]{2,1,0:T(8,128)}), f32[32,8,128]{2,1,0:T(8,128)S(1)}, u32[]{:S(2)}, u32[]{:S(2)}) async-start(f32[32,8,128]{2,1,0:T(8,128)} %get-tuple-element.35), calls=%async_computation | async-start | bytes 262144 | tf_op jit(solution)/shard_map/all_to_all | solution.py:409
  49.8 1.8 %collective-permute-start.24 = (f32[16,640]{1,0:T(8,128)S(1)}, f32[16,640]{1,0:T(8,128)S(1)}, u32[]{:S(2)}, u32[]{:S(2)}) collective-permute-start(f32[16,640]{1,0:T(8,128)S(1)} %get-tuple-element.36.refs_0_.refs_5_), channel_id=1, source_target_pairs={{0,2},{1,3},{2,0},{3,1},{4,6},{5,7},{6,4},{7,5},{8,10},{9,11},{10,... | collective-permute-start | bytes 122888 | tf_op jit(solution)/shard_map/ppermute | solution.py:35
  51.6 2.4 %collective-permute-done.24.refs_2_.refs_7_ = f32[16,640]{1,0:T(8,128)S(1)} collective-permute-done((f32[16,640]{1,0:T(8,128)S(1)}, f32[16,640]{1,0:T(8,128)S(1)}, u32[]{:S(2)}, u32[]{:S(2)}) %collective-permute-start.24) | collective-permute-done | bytes 40992 | tf_op jit(solution)/shard_map/ppermute | solution.py:35
  54.0 4.0 %all-to-all-done.gathered_ref = f32[32,8,128]{2,1,0:T(8,128)S(1)} async-done(((f32[32,8,128]{2,1,0:T(8,128)}), f32[32,8,128]{2,1,0:T(8,128)S(1)}, u32[]{:S(2)}, u32[]{:S(2)}) %all-to-all-start) | async-done | bytes 131104 | tf_op jit(solution)/shard_map/all_to_all | solution.py:409
  58.0 0.3 collective-permute-start.22
  58.3 2.6 %shard_map.75 = (f32[64,64]{1,0:T(8,128)S(1)}, f32[64,16]{1,0:T(8,128)S(1)}, f32[64,16]{1,0:T(8,128)S(1)}) custom-call(f32[16,640]{1,0:T(8,128)S(1)} %get-tuple-element.36.refs_0_.refs_5_, f32[16,640]{1,0:T(8,128)S(1)} %collective-permute-done.23.refs_1_.refs_6_, f32[16,640]{1,0:T(8,128)S(1)} %collective-permute-done.24.refs_2_.refs_7_, ...), custom_call_target="tpu_custom_call" | custom-call | flops 1048576 | bytes 655360 | tf_op jit(solution)/shard_map/pallas_call | solution.py:346
  60.9 3.9 %shard_map.76 = (f32[16,512]{1,0:T(8,128)}, f32[16,512]{1,0:T(8,128)}) custom-call(f32[32,128]{1,0:T(8,128)S(1)} %shard_map.74.refs_0_, f32[32,128]{1,0:T(8,128)S(1)} %collective-permute-done.22.refs_1_, f32[64,64]{1,0:T(8,128)S(1)} %get-tuple-element.37.refs_2_, f32[64,16]{1,0:T(8,128)S(1)} %get-tuple-element.38.refs_3_, ...), custom_call_target="tpu_custom_call" | custom-call | tf_op jit(solution)/shard_map/pallas_call | solution.py:346
  (17 shorter events, 0.1 us)
Async XLA Ops:
  0.6 11.6 %copy-start = (f32[16,512]{1,0:T(8,128)S(1)}, f32[16,512]{1,0:T(8,128)}, u32[]{:S(2)}) copy-start(f32[16,512]{1,0:T(8,128)} %refs_9_.1) | copy-start | bytes 98308
  0.6 11.0 %collective-permute-start = (f32[16,512]{1,0:T(8,128)}, f32[16,512]{1,0:T(8,128)S(1)}, u32[]{:S(2)}, u32[]{:S(2)}) collective-permute-start(f32[16,512]{1,0:T(8,128)} %refs_9_.1), channel_id=1, source_target_pairs={{0,8},{8,0},{16,24},{24,16},{1,9},{9,1},{17,25},{25,17},{2,10},{10... | collective-permute-start | bytes 98312 | tf_op jit(solution)/shard_map/ppermute | solution.py:35
  3.8 7.9 %collective-permute-start.1 = (f32[16,512]{1,0:T(8,128)}, f32[16,512]{1,0:T(8,128)S(1)}, u32[]{:S(2)}, u32[]{:S(2)}) collective-permute-start(f32[16,512]{1,0:T(8,128)} %refs_9_.1), channel_id=1, source_target_pairs={{0,16},{8,24},{16,0},{24,8},{1,17},{9,25},{17,1},{25,9},{2,18},{10... | collective-permute-start | bytes 98312 | tf_op jit(solution)/shard_map/ppermute | solution.py:35
  6.3 5.9 %collective-permute-start.2 = (f32[16,512]{1,0:T(8,128)}, f32[16,512]{1,0:T(8,128)S(1)}, u32[]{:S(2)}, u32[]{:S(2)}) collective-permute-start(f32[16,512]{1,0:T(8,128)} %refs_9_.1), channel_id=1, source_target_pairs={{0,24},{8,16},{16,8},{24,0},{1,25},{9,17},{17,9},{25,1},{2,26},{10... | collective-permute-start | bytes 98312 | tf_op jit(solution)/shard_map/ppermute | solution.py:35
  6.4 5.9 %collective-permute-start.3 = (f32[16,512]{1,0:T(8,128)}, f32[16,512]{1,0:T(8,128)S(1)}, u32[]{:S(2)}, u32[]{:S(2)}) collective-permute-start(f32[16,512]{1,0:T(8,128)} %refs_9_.1), channel_id=1, source_target_pairs={{0,4},{4,0},{1,5},{5,1},{2,6},{6,2},{3,7},{7,3},{8,12},{12,8},{9,1... | collective-permute-start | bytes 98312 | tf_op jit(solution)/shard_map/ppermute | solution.py:35
  14.6 7.5 %collective-permute-start.4 = (f32[16,512]{1,0:T(8,128)S(1)}, f32[16,512]{1,0:T(8,128)S(1)}, u32[]{:S(2)}, u32[]{:S(2)}) collective-permute-start(f32[16,512]{1,0:T(8,128)S(1)} %get-tuple-element.24), channel_id=1, source_target_pairs={{0,8},{8,0},{16,24},{24,16},{1,9},{9,1},{17,25},{25,17},{2,10},{10... | collective-permute-start | bytes 98312 | tf_op jit(solution)/shard_map/ppermute | solution.py:35
  14.8 7.3 %collective-permute-start.9 = (f32[16,512]{1,0:T(8,128)S(1)}, f32[16,512]{1,0:T(8,128)S(1)}, u32[]{:S(2)}, u32[]{:S(2)}) collective-permute-start(f32[16,512]{1,0:T(8,128)S(1)} %get-tuple-element.28), channel_id=1, source_target_pairs={{0,2},{1,3},{2,0},{3,1},{4,6},{5,7},{6,4},{7,5},{8,10},{9,11},{10,... | collective-permute-start | bytes 98312 | tf_op jit(solution)/shard_map/ppermute | solution.py:35
  16.3 6.3 %collective-permute-start.5 = (f32[16,512]{1,0:T(8,128)S(1)}, f32[16,512]{1,0:T(8,128)S(1)}, u32[]{:S(2)}, u32[]{:S(2)}) collective-permute-start(f32[16,512]{1,0:T(8,128)S(1)} %get-tuple-element.25), channel_id=1, source_target_pairs={{0,16},{8,24},{16,0},{24,8},{1,17},{9,25},{17,1},{25,9},{2,18},{10... | collective-permute-start | bytes 98312 | tf_op jit(solution)/shard_map/ppermute | solution.py:35
  19.7 5.7 %collective-permute-start.6 = (f32[16,512]{1,0:T(8,128)S(1)}, f32[16,512]{1,0:T(8,128)S(1)}, u32[]{:S(2)}, u32[]{:S(2)}) collective-permute-start(f32[16,512]{1,0:T(8,128)S(1)} %get-tuple-element.26), channel_id=1, source_target_pairs={{0,24},{8,16},{16,8},{24,0},{1,25},{9,17},{17,9},{25,1},{2,26},{10... | collective-permute-start | bytes 98312 | tf_op jit(solution)/shard_map/ppermute | solution.py:35
  20.5 4.9 %collective-permute-start.7 = (f32[16,512]{1,0:T(8,128)S(1)}, f32[16,512]{1,0:T(8,128)S(1)}, u32[]{:S(2)}, u32[]{:S(2)}) collective-permute-start(f32[16,512]{1,0:T(8,128)S(1)} %get-tuple-element.27), channel_id=1, source_target_pairs={{0,4},{4,0},{1,5},{5,1},{2,6},{6,2},{3,7},{7,3},{8,12},{12,8},{9,1... | collective-permute-start | bytes 98312 | tf_op jit(solution)/shard_map/ppermute | solution.py:35
  22.1 3.5 %collective-permute-start.8 = (f32[16,512]{1,0:T(8,128)S(1)}, f32[16,512]{1,0:T(8,128)S(1)}, u32[]{:S(2)}, u32[]{:S(2)}) collective-permute-start(f32[16,512]{1,0:T(8,128)S(1)} %get-tuple-element.28), channel_id=1, source_target_pairs={{0,1},{1,0},{2,3},{3,2},{4,5},{5,4},{6,7},{7,6},{8,9},{9,8},{10,11... | collective-permute-start | bytes 98312 | tf_op jit(solution)/shard_map/ppermute | solution.py:35
  22.1 3.5 %collective-permute-start.10 = (f32[16,512]{1,0:T(8,128)S(1)}, f32[16,512]{1,0:T(8,128)S(1)}, u32[]{:S(2)}, u32[]{:S(2)}) collective-permute-start(f32[16,512]{1,0:T(8,128)S(1)} %collective-permute-done.9.refs_3_.refs_8_.refs_11_), channel_id=1, source_target_pairs={{0,1},{1,0},{2,3},{3,2},{4,5},{5,4},{6,7},{7,6},{8,9},{9,8},{10,11... | collective-permute-start | bytes 98312 | tf_op jit(solution)/shard_map/ppermute | solution.py:35
  25.5 5.9 %collective-permute-start.11 = (f32[16,512]{1,0:T(8,128)S(1)}, f32[16,512]{1,0:T(8,128)S(1)}, u32[]{:S(2)}, u32[]{:S(2)}) collective-permute-start(f32[16,512]{1,0:T(8,128)S(1)} %shard_map.70.refs_0_.refs_10_.refs_13_), channel_id=1, source_target_pairs={{0,8},{8,0},{16,24},{24,16},{1,9},{9,1},{17,25},{25,17},{2,10},{10... | collective-permute-start | bytes 98312 | tf_op jit(solution)/shard_map/ppermute | solution.py:35
  26.0 8.8 %collective-permute-start.14 = (f32[16,640]{1,0:T(8,128)S(1)}, f32[16,640]{1,0:T(8,128)S(1)}, u32[]{:S(2)}, u32[]{:S(2)}) collective-permute-start(f32[16,640]{1,0:T(8,128)S(1)} %shard_map.71.refs_2_), channel_id=1, source_target_pairs={{0,4},{4,0},{1,5},{5,1},{2,6},{6,2},{3,7},{7,3},{8,12},{12,8},{9,1... | collective-permute-start | bytes 122888 | tf_op jit(solution)/shard_map/ppermute | solution.py:35
  26.5 5.0 %collective-permute-start.12 = (f32[16,512]{1,0:T(8,128)S(1)}, f32[16,512]{1,0:T(8,128)S(1)}, u32[]{:S(2)}, u32[]{:S(2)}) collective-permute-start(f32[16,512]{1,0:T(8,128)S(1)} %shard_map.70.refs_0_.refs_10_.refs_13_), channel_id=1, source_target_pairs={{0,16},{8,24},{16,0},{24,8},{1,17},{9,25},{17,1},{25,9},{2,18},{10... | collective-permute-start | bytes 98312 | tf_op jit(solution)/shard_map/ppermute | solution.py:35
  29.1 5.7 %collective-permute-start.13 = (f32[16,512]{1,0:T(8,128)S(1)}, f32[16,512]{1,0:T(8,128)S(1)}, u32[]{:S(2)}, u32[]{:S(2)}) collective-permute-start(f32[16,512]{1,0:T(8,128)S(1)} %shard_map.70.refs_0_.refs_10_.refs_13_), channel_id=1, source_target_pairs={{0,24},{8,16},{16,8},{24,0},{1,25},{9,17},{17,9},{25,1},{2,26},{10... | collective-permute-start | bytes 98312 | tf_op jit(solution)/shard_map/ppermute | solution.py:35
  30.9 10.7 %collective-permute-start.20 = (f32[16,512]{1,0:T(8,128)S(1)}, f32[16,512]{1,0:T(8,128)S(1)}, u32[]{:S(2)}, u32[]{:S(2)}) collective-permute-start(f32[16,512]{1,0:T(8,128)S(1)} %shard_map.70.refs_0_.refs_10_.refs_13_), channel_id=1, source_target_pairs={{0,2},{1,3},{2,0},{3,1},{4,6},{5,7},{6,4},{7,5},{8,10},{9,11},{10,... | collective-permute-start | bytes 98312 | tf_op jit(solution)/shard_map/ppermute | solution.py:35
  31.4 10.1 %collective-permute-start.19 = (f32[16,512]{1,0:T(8,128)S(1)}, f32[16,512]{1,0:T(8,128)S(1)}, u32[]{:S(2)}, u32[]{:S(2)}) collective-permute-start(f32[16,512]{1,0:T(8,128)S(1)} %shard_map.70.refs_0_.refs_10_.refs_13_), channel_id=1, source_target_pairs={{0,1},{1,0},{2,3},{3,2},{4,5},{5,4},{6,7},{7,6},{8,9},{9,8},{10,11... | collective-permute-start | bytes 98312 | tf_op jit(solution)/shard_map/ppermute | solution.py:35
  37.1 8.4 %collective-permute-start.15 = (f32[16,640]{1,0:T(8,128)S(1)}, f32[16,640]{1,0:T(8,128)S(1)}, u32[]{:S(2)}, u32[]{:S(2)}) collective-permute-start(f32[16,640]{1,0:T(8,128)S(1)} %get-tuple-element.31), channel_id=1, source_target_pairs={{0,8},{8,0},{16,24},{24,16},{1,9},{9,1},{17,25},{25,17},{2,10},{10... | collective-permute-start | bytes 122888 | tf_op jit(solution)/shard_map/ppermute | solution.py:35
  37.2 8.4 %collective-permute-start.16 = (f32[16,640]{1,0:T(8,128)S(1)}, f32[16,640]{1,0:T(8,128)S(1)}, u32[]{:S(2)}, u32[]{:S(2)}) collective-permute-start(f32[16,640]{1,0:T(8,128)S(1)} %get-tuple-element.32), channel_id=1, source_target_pairs={{0,16},{8,24},{16,0},{24,8},{1,17},{9,25},{17,1},{25,9},{2,18},{10... | collective-permute-start | bytes 122888 | tf_op jit(solution)/shard_map/ppermute | solution.py:35
  39.5 6.0 %collective-permute-start.17 = (f32[16,640]{1,0:T(8,128)S(1)}, f32[16,640]{1,0:T(8,128)S(1)}, u32[]{:S(2)}, u32[]{:S(2)}) collective-permute-start(f32[16,640]{1,0:T(8,128)S(1)} %get-tuple-element.33), channel_id=1, source_target_pairs={{0,24},{8,16},{16,8},{24,0},{1,25},{9,17},{17,9},{25,1},{2,26},{10... | collective-permute-start | bytes 122888 | tf_op jit(solution)/shard_map/ppermute | solution.py:35
  41.5 1.6 %collective-permute-start.21 = (f32[16,512]{1,0:T(8,128)S(1)}, f32[16,512]{1,0:T(8,128)S(1)}, u32[]{:S(2)}, u32[]{:S(2)}) collective-permute-start(f32[16,512]{1,0:T(8,128)S(1)} %collective-permute-done.20.refs_12_.refs_15_), channel_id=1, source_target_pairs={{0,1},{1,0},{2,3},{3,2},{4,5},{5,4},{6,7},{7,6},{8,9},{9,8},{10,11... | collective-permute-start | bytes 98312 | tf_op jit(solution)/shard_map/ppermute | solution.py:35
  41.5 4.0 %collective-permute-start.18 = (f32[16,512]{1,0:T(8,128)S(1)}, f32[16,512]{1,0:T(8,128)S(1)}, u32[]{:S(2)}, u32[]{:S(2)}) collective-permute-start(f32[16,512]{1,0:T(8,128)S(1)} %get-tuple-element.34), channel_id=1, source_target_pairs={{0,4},{4,0},{1,5},{5,1},{2,6},{6,2},{3,7},{7,3},{8,12},{12,8},{9,1... | collective-permute-start | bytes 98312 | tf_op jit(solution)/shard_map/ppermute | solution.py:35
  46.6 11.3 %all-to-all-start = ((f32[32,8,128]{2,1,0:T(8,128)}), f32[32,8,128]{2,1,0:T(8,128)S(1)}, u32[]{:S(2)}, u32[]{:S(2)}) async-start(f32[32,8,128]{2,1,0:T(8,128)} %get-tuple-element.35), calls=%async_computation | async-start | bytes 262144 | tf_op jit(solution)/shard_map/all_to_all | solution.py:409
  49.8 4.2 %collective-permute-start.24 = (f32[16,640]{1,0:T(8,128)S(1)}, f32[16,640]{1,0:T(8,128)S(1)}, u32[]{:S(2)}, u32[]{:S(2)}) collective-permute-start(f32[16,640]{1,0:T(8,128)S(1)} %get-tuple-element.36.refs_0_.refs_5_), channel_id=1, source_target_pairs={{0,2},{1,3},{2,0},{3,1},{4,6},{5,7},{6,4},{7,5},{8,10},{9,11},{10,... | collective-permute-start | bytes 122888 | tf_op jit(solution)/shard_map/ppermute | solution.py:35
  51.6 6.7 %collective-permute-start.23 = (f32[16,640]{1,0:T(8,128)S(1)}, f32[16,640]{1,0:T(8,128)S(1)}, u32[]{:S(2)}, u32[]{:S(2)}) collective-permute-start(f32[16,640]{1,0:T(8,128)S(1)} %get-tuple-element.36.refs_0_.refs_5_), channel_id=1, source_target_pairs={{0,1},{1,0},{2,3},{3,2},{4,5},{5,4},{6,7},{7,6},{8,9},{9,8},{10,11... | collective-permute-start | bytes 122888 | tf_op jit(solution)/shard_map/ppermute | solution.py:35
  54.0 4.3 %collective-permute-start.25 = (f32[16,640]{1,0:T(8,128)S(1)}, f32[16,640]{1,0:T(8,128)S(1)}, u32[]{:S(2)}, u32[]{:S(2)}) collective-permute-start(f32[16,640]{1,0:T(8,128)S(1)} %collective-permute-done.24.refs_2_.refs_7_), channel_id=1, source_target_pairs={{0,1},{1,0},{2,3},{3,2},{4,5},{5,4},{6,7},{7,6},{8,9},{9,8},{10,11... | collective-permute-start | bytes 122888 | tf_op jit(solution)/shard_map/ppermute | solution.py:35
  58.0 2.9 %collective-permute-start.22 = (f32[32,128]{1,0:T(8,128)S(1)}, f32[32,128]{1,0:T(8,128)S(1)}, u32[]{:S(2)}, u32[]{:S(2)}) collective-permute-start(f32[32,128]{1,0:T(8,128)S(1)} %shard_map.74.refs_0_), channel_id=1, source_target_pairs={{0,1},{1,0},{2,3},{3,2},{4,5},{5,4},{6,7},{7,6},{8,9},{9,8},{10,11... | collective-permute-start | bytes 49160 | tf_op jit(solution)/shard_map/ppermute | solution.py:416

commit v6 on v5

--- a/solution.py
+++ b/solution.py
@@ -10,7 +10,8 @@
 
 BLK = 256
 SEG = 2
-PIVOT = 4
+PIVOT = 8
+PANEL = 32
 HIGHEST = lax.Precision.HIGHEST
 VMEM = pl.BlockSpec(memory_space=pltpu.VMEM)
 SMEM = pl.BlockSpec(memory_space=pltpu.SMEM)
@@ -247,15 +248,16 @@
     return solve
 
 
-def eliminate(tables, pivot):
-    size, wide = tables[0].shape
+def eliminate(table, size, pivot, panel):
+    rows, wide = table.shape
     sub = 8
     at_row = lax.broadcasted_iota(jnp.int32, (sub, wide), 0)
-    one = tables[0][:sub] * 0.0 + 1.0
-    tables = [[table[t : t + sub] for t in range(0, size, sub)] for table in tables]
-    for k in range(0, size, pivot):
-        home, base = k // sub, k % sub
-        for tiles in tables:
+    one = table[:sub] * 0.0 + 1.0
+    for start in range(0, size, panel):
+        stop = start + panel
+        tiles = [table[t : t + sub] for t in range(start, stop, sub)]
+        for k in range(start, stop, pivot):
+            home, base = (k - start) // sub, k % sub
             spread = [
                 [jnp.broadcast_to(tile[:, k + j : k + j + 1], (sub, wide)) for tile in tiles] for j in range(pivot)
             ]
@@ -268,14 +270,15 @@
             }
             solved = factor(lambda i, j: entries[i, j], pivot)(row)
             for t, tile in enumerate(tiles):
-                if t == home and pivot == sub:
-                    tiles[t] = solved[0]
-                else:
-                    tiles[t] = tile - sum(spread[j][t] * solved[j] for j in range(pivot))
+                tiles[t] = tile - sum(spread[j][t] * solved[j] for j in range(pivot))
                 if t == home:
                     for i in range(pivot):
                         tiles[t] = jnp.where(at_row == base + i, solved[i], tiles[t])
-    return [jnp.concatenate(tiles, axis=0) for tiles in tables]
+        done = jnp.concatenate(tiles, axis=0)
+        others = [table[at:to] for at, to in ((0, start), (stop, rows)) if at < to]
+        others = [part - dot_nn(part[:, start:stop], done) for part in others]
+        table = jnp.concatenate(others[:1] + [done] + others[1:] if start else [done] + others, axis=0)
+    return table
 
 
 def identity_of(size):
@@ -292,7 +295,7 @@
         place = source_of("depth", step)
         scratch[0][pl.ds(pl.multiple_of(place * width, width), width), :] = ref[:, points + size : points + 2 * size]
     gram1 = scratch[0][...]
-    (first,) = eliminate([jnp.concatenate([gram1, identity_of(size)], axis=1)], PIVOT)
+    first = eliminate(jnp.concatenate([gram1, identity_of(size)], axis=1), size, PIVOT, size)
     inverse = first[:, size:]
     outs[0][...] = inverse
     outs[1][...] = dot_nt(inverse, wide_refs[0][:, points : points + size])
@@ -317,15 +320,14 @@
 
 def finish(n_depth, *refs):
     late, solved, wide_refs, base_refs, image_refs, outs, scratch = split(
-        refs, 2, 3, n_depth, n_depth, n_depth, 2, 3
-    )
-    base, image, mapped = scratch
+        refs, 2, 3, n_depth, n_depth, n_depth, 2, 1
+    )
+    (fields,) = scratch
     solution_out, residual_out = outs
     width, _ = solution_out.shape
     size = n_depth * width
-    stack_fields(base, base_refs[0], base_refs[1:])
-    stack_fields(image, image_refs[0], image_refs[1:])
-    stack_fields(mapped, wide_refs[0], wide_refs[1:])
+    for i, refs_of in enumerate((base_refs, image_refs, wide_refs)):
+        stack_fields(fields.at[i * size : (i + 1) * size], refs_of[0], refs_of[1:])
     mine, other = (unpacked(ref[...], width // 2) for ref in late)
     even = lax.axis_index("depth") % 2 == 0
     gram2, gram3 = jnp.where(even, mine, other), jnp.where(even, other, mine)
@@ -334,12 +336,13 @@
     schur = gram3 - dot_nn(gram2, carry)
     right = gram1_own - dot_nn(gram2, start)
     fill = jnp.zeros((size, size - width), jnp.float32)
-    (second,) = eliminate([jnp.concatenate([schur, right, fill], axis=1)], PIVOT)
-    weight1 = second[:, size : size + width]
-    weight0 = start - dot_nn(carry, weight1)
-    base_all, image_all = base[...], image[...]
-    solution_out[...] = dot_tn(weight0, base_all) + dot_tn(weight1, image_all)
-    residual_out[...] = base_refs[0][...] - dot_tn(weight0, image_all) - dot_tn(weight1, mapped[...])
+    rows = [jnp.concatenate(parts, axis=1) for parts in ((schur, right, fill), (carry, start, fill))]
+    weights = eliminate(jnp.concatenate(rows, axis=0), size, PIVOT, PANEL)[:, size : size + width]
+    weight1, weight0, none = weights[:size], weights[size:], jnp.zeros((size, width), jnp.float32)
+    both = [jnp.concatenate(parts, axis=1) for parts in ((weight0, none), (weight1, weight0), (none, weight1))]
+    result = dot_tn(jnp.concatenate(both, axis=0), fields[...])
+    solution_out[...] = result[:width]
+    residual_out[...] = base_refs[0][...] - result[width:]
 
 
 def call(body, operands, in_specs, out_shapes, scratch, cost=None, out_specs=None):
@@ -416,7 +419,7 @@
     other = lax.ppermute(late, "depth", [(i, i ^ 1) for i in range(n_depth)])
     solution, residual = call(
         functools.partial(finish, n_depth),
-        [late, other] + list(solved) + mapped + base + image, [], [narrow, narrow], [fields, fields, fields],
+        [late, other] + list(solved) + mapped + base + image, [], [narrow, narrow], [pltpu.VMEM((3 * size, points), f32)],
     )
     return solution, residual
 

time: 65 us -> 64 us (0.985)
  Pallas kernels: 15.5 us -> 14.5 us
    pallas_call x9, Pallas kernels: 15.5 us -> 14.5 us  [call(): pl.pallas_call(body, out_shape=[s if hasattr(s, 'dtype') else jax.ShapeDt...]
  transfers between devices with their start and end apart: 27 -> 27, of which waited for: 7 -> 7; matrix products, arithmetic and copies ran while one was open for 0% -> 0% of each run, Pallas kernels for 13% -> 12%
where the time goes in v6:
time: 64 us; the launch traced here: 63.8 us
  starting transfers between devices  32.2 us (50%)
  waiting for transfers between devices  15.7 us (25%)
  Pallas kernels  14.5 us (23%)
  between operations  1.42 us (2%)
    ppermute x25, starting transfers between devices, send(): lax.ppermute(x, axis, [(i, partner(i, step, size)) for i in range(size)])  28.8 us
    pallas_call x9, Pallas kernels, call(): pl.pallas_call(body, out_shape=[s if hasattr(s, 'dtype') else jax.ShapeDt...  14.5 us
    ppermute x25, waiting for transfers between devices, send(): lax.ppermute(x, axis, [(i, partner(i, step, size)) for i in range(size)])  11.7 us
    all_to_all x1, waiting for transfers between devices, per_device(): late = lax.all_to_all(late, ('row', 'col', 'depth'), 0, 0)  3.96 us
    all_to_all x1, starting transfers between devices, per_device(): late = lax.all_to_all(late, ('row', 'col', 'depth'), 0, 0)  3.13 us
  transfers between devices with their start and end apart: 27, of which 7 were waited for; matrix products, arithmetic and copies ran while one was open for 0% of the time, Pallas kernels for 12%

profile of v6, /device:TPU:0, one launch (start us, length us, event | category | flops | bytes accessed | tf_op | source)
XLA Modules:
  0.0 63.8 jit_solution(9929833353625311798)
XLA Ops:
  0.6 3.1 %collective-permute-start = (f32[16,512]{1,0:T(8,128)}, f32[16,512]{1,0:T(8,128)S(1)}, u32[]{:S(2)}, u32[]{:S(2)}) collective-permute-start(f32[16,512]{1,0:T(8,128)} %refs_9_.1), channel_id=1, source_target_pairs={{0,8},{8,0},{16,24},{24,16},{1,9},{9,1},{17,25},{25,17},{2,10},{10... | collective-permute-start | bytes 98312 | tf_op jit(solution)/shard_map/ppermute | solution.py:36
  3.8 2.6 %collective-permute-start.1 = (f32[16,512]{1,0:T(8,128)}, f32[16,512]{1,0:T(8,128)S(1)}, u32[]{:S(2)}, u32[]{:S(2)}) collective-permute-start(f32[16,512]{1,0:T(8,128)} %refs_9_.1), channel_id=1, source_target_pairs={{0,16},{8,24},{16,0},{24,8},{1,17},{9,25},{17,1},{25,9},{2,18},{10... | collective-permute-start | bytes 98312 | tf_op jit(solution)/shard_map/ppermute | solution.py:36
  6.4 1.7 %collective-permute-start.3 = (f32[16,512]{1,0:T(8,128)}, f32[16,512]{1,0:T(8,128)S(1)}, u32[]{:S(2)}, u32[]{:S(2)}) collective-permute-start(f32[16,512]{1,0:T(8,128)} %refs_9_.1), channel_id=1, source_target_pairs={{0,4},{4,0},{1,5},{5,1},{2,6},{6,2},{3,7},{7,3},{8,12},{12,8},{9,1... | collective-permute-start | bytes 98312 | tf_op jit(solution)/shard_map/ppermute | solution.py:36
  8.7 2.9 %shard_map.68 = (f32[16,256,256]{2,1,0:T(8,128)S(1)}, s32[3,16]{1,0:T(4,128)S(1)}) custom-call(s32[1,1]{1,0:T(1,128)S(6)} %copy.7.count_ref, s32[1,1,16]{2,1,0:T(1,128)} %rows_ref.1, s32[1,1,16]{2,1,0:T(1,128)} %cols_ref.1, f32[1,1,16,256,256]{4,3,2,1,0:T(8,128)} %blocks_ref.1), custom_call_target="tpu_custom_call" | custom-call | bytes 8388608 | tf_op jit(solution)/shard_map/pallas_call | solution.py:349
  11.7 0.0 collective-permute-done.refs_3_
  11.7 0.0 collective-permute-done.1.refs_4_
  11.7 0.6 collective-permute-done.2.refs_5_
  12.3 0.0 collective-permute-done.3.refs_6_
  12.3 2.3 %shard_map.69 = (f32[16,512]{1,0:T(8,128)S(1)}, f32[16,512]{1,0:T(8,128)S(1)}, f32[16,512]{1,0:T(8,128)S(1)}, f32[16,512]{1,0:T(8,128)S(1)}, f32[16,512]{1,0:T(8,128)S(1)}, /*index=5*/f32[16,512]{1,0:T(8,128)S(1)}) custom-call(s32[3,16]{1,0:T(4,128)S(1)} %get-tuple-element.21.refs_0_, f32[16,256,256]{2,1,0:T(8,128)S(1)} %get-tuple-element.22.refs_1_, ...), custom_call_target="tpu_custom_call" | custom-call | tf_op jit(solution)/shard_map/pallas_call | solution.py:349
  14.6 0.2 collective-permute-start.4
  14.8 1.5 %collective-permute-start.9 = (f32[16,512]{1,0:T(8,128)S(1)}, f32[16,512]{1,0:T(8,128)S(1)}, u32[]{:S(2)}, u32[]{:S(2)}) collective-permute-start(f32[16,512]{1,0:T(8,128)S(1)} %get-tuple-element.28), channel_id=1, source_target_pairs={{0,2},{1,3},{2,0},{3,1},{4,6},{5,7},{6,4},{7,5},{8,10},{9,11},{10,... | collective-permute-start | bytes 98312 | tf_op jit(solution)/shard_map/ppermute | solution.py:36
  16.3 3.5 %collective-permute-start.5 = (f32[16,512]{1,0:T(8,128)S(1)}, f32[16,512]{1,0:T(8,128)S(1)}, u32[]{:S(2)}, u32[]{:S(2)}) collective-permute-start(f32[16,512]{1,0:T(8,128)S(1)} %get-tuple-element.25), channel_id=1, source_target_pairs={{0,16},{8,24},{16,0},{24,8},{1,17},{9,25},{17,1},{25,9},{2,18},{10... | collective-permute-start | bytes 98312 | tf_op jit(solution)/shard_map/ppermute | solution.py:36
  19.7 0.8 %collective-permute-start.6 = (f32[16,512]{1,0:T(8,128)S(1)}, f32[16,512]{1,0:T(8,128)S(1)}, u32[]{:S(2)}, u32[]{:S(2)}) collective-permute-start(f32[16,512]{1,0:T(8,128)S(1)} %get-tuple-element.26), channel_id=1, source_target_pairs={{0,24},{8,16},{16,8},{24,0},{1,25},{9,17},{17,9},{25,1},{2,26},{10... | collective-permute-start | bytes 98312 | tf_op jit(solution)/shard_map/ppermute | solution.py:36
  20.5 1.5 %collective-permute-start.7 = (f32[16,512]{1,0:T(8,128)S(1)}, f32[16,512]{1,0:T(8,128)S(1)}, u32[]{:S(2)}, u32[]{:S(2)}) collective-permute-start(f32[16,512]{1,0:T(8,128)S(1)} %get-tuple-element.27), channel_id=1, source_target_pairs={{0,4},{4,0},{1,5},{5,1},{2,6},{6,2},{3,7},{7,3},{8,12},{12,8},{9,1... | collective-permute-start | bytes 98312 | tf_op jit(solution)/shard_map/ppermute | solution.py:36
  22.1 0.0 collective-permute-done.4.refs_1_
  22.1 0.0 collective-permute-start.8
  22.1 0.0 collective-permute-done.9.refs_3_.refs_8_.refs_11_
  22.1 0.5 collective-permute-start.10
  22.6 0.0 collective-permute-done.5.refs_2_
  22.6 2.9 %collective-permute-done.6.refs_3_ = f32[16,512]{1,0:T(8,128)S(1)} collective-permute-done((f32[16,512]{1,0:T(8,128)S(1)}, f32[16,512]{1,0:T(8,128)S(1)}, u32[]{:S(2)}, u32[]{:S(2)}) %collective-permute-start.6) | collective-permute-done | bytes 32800 | tf_op jit(solution)/shard_map/ppermute | solution.py:36
  25.5 0.0 collective-permute-done.7.refs_4_
  25.5 0.1 collective-permute-start.11
  25.6 0.0 collective-permute-done.10.refs_4_.refs_9_.refs_12_
  25.6 0.4 shard_map.71.refs_2_
  26.0 0.5 collective-permute-start.14
  26.5 2.5 %collective-permute-start.12 = (f32[16,512]{1,0:T(8,128)S(1)}, f32[16,512]{1,0:T(8,128)S(1)}, u32[]{:S(2)}, u32[]{:S(2)}) collective-permute-start(f32[16,512]{1,0:T(8,128)S(1)} %shard_map.70.refs_0_.refs_10_.refs_13_), channel_id=1, source_target_pairs={{0,16},{8,24},{16,0},{24,8},{1,17},{9,25},{17,1},{25,9},{2,18},{10... | collective-permute-start | bytes 98312 | tf_op jit(solution)/shard_map/ppermute | solution.py:36
  29.1 1.8 %collective-permute-start.13 = (f32[16,512]{1,0:T(8,128)S(1)}, f32[16,512]{1,0:T(8,128)S(1)}, u32[]{:S(2)}, u32[]{:S(2)}) collective-permute-start(f32[16,512]{1,0:T(8,128)S(1)} %shard_map.70.refs_0_.refs_10_.refs_13_), channel_id=1, source_target_pairs={{0,24},{8,16},{16,8},{24,0},{1,25},{9,17},{17,9},{25,1},{2,26},{10... | collective-permute-start | bytes 98312 | tf_op jit(solution)/shard_map/ppermute | solution.py:36
  30.9 0.5 collective-permute-start.20
  31.4 0.0 collective-permute-done.11.refs_3_
  31.4 0.0 collective-permute-start.19
  31.4 0.1 collective-permute-done.12.refs_4_
  31.5 3.2 %collective-permute-done.13.refs_5_ = f32[16,512]{1,0:T(8,128)S(1)} collective-permute-done((f32[16,512]{1,0:T(8,128)S(1)}, f32[16,512]{1,0:T(8,128)S(1)}, u32[]{:S(2)}, u32[]{:S(2)}) %collective-permute-start.13) | collective-permute-done | bytes 32800 | tf_op jit(solution)/shard_map/ppermute | solution.py:36
  34.8 2.3 %shard_map.72 = (f32[16,512]{1,0:T(8,128)S(1)}, f32[16,128]{1,0:T(8,128)S(1)}, f32[16,640]{1,0:T(8,128)S(1)}, f32[16,640]{1,0:T(8,128)S(1)}, f32[16,640]{1,0:T(8,128)S(1)}, /*index=5*/f32[16,512]{1,0:T(8,128)S(1)}) custom-call(s32[3,16]{1,0:T(4,128)S(1)} %get-tuple-element.21.refs_0_, f32[16,256,256]{2,1,0:T(8,128)S(1)} %get-tuple-element.22.refs_1_, ...), custom_call_target="tpu_custom_call" | custom-call | tf_op jit(solution)/shard_map/pallas_call | solution.py:349
  37.1 0.1 collective-permute-start.15
  37.2 2.4 %collective-permute-start.16 = (f32[16,640]{1,0:T(8,128)S(1)}, f32[16,640]{1,0:T(8,128)S(1)}, u32[]{:S(2)}, u32[]{:S(2)}) collective-permute-start(f32[16,640]{1,0:T(8,128)S(1)} %get-tuple-element.32), channel_id=1, source_target_pairs={{0,16},{8,24},{16,0},{24,8},{1,17},{9,25},{17,1},{25,9},{2,18},{10... | collective-permute-start | bytes 122888 | tf_op jit(solution)/shard_map/ppermute | solution.py:36
  39.5 2.0 %collective-permute-start.17 = (f32[16,640]{1,0:T(8,128)S(1)}, f32[16,640]{1,0:T(8,128)S(1)}, u32[]{:S(2)}, u32[]{:S(2)}) collective-permute-start(f32[16,640]{1,0:T(8,128)S(1)} %get-tuple-element.33), channel_id=1, source_target_pairs={{0,24},{8,16},{16,8},{24,0},{1,25},{9,17},{17,9},{25,1},{2,26},{10... | collective-permute-start | bytes 122888 | tf_op jit(solution)/shard_map/ppermute | solution.py:36
  41.5 0.0 collective-permute-done.20.refs_12_.refs_15_
  41.5 0.0 collective-permute-start.21
  41.5 1.6 %collective-permute-start.18 = (f32[16,512]{1,0:T(8,128)S(1)}, f32[16,512]{1,0:T(8,128)S(1)}, u32[]{:S(2)}, u32[]{:S(2)}) collective-permute-start(f32[16,512]{1,0:T(8,128)S(1)} %get-tuple-element.34), channel_id=1, source_target_pairs={{0,4},{4,0},{1,5},{5,1},{2,6},{6,2},{3,7},{7,3},{8,12},{12,8},{9,1... | collective-permute-start | bytes 98312 | tf_op jit(solution)/shard_map/ppermute | solution.py:36
  43.1 2.4 %collective-permute-done.18.refs_5_ = f32[16,512]{1,0:T(8,128)S(1)} collective-permute-done((f32[16,512]{1,0:T(8,128)S(1)}, f32[16,512]{1,0:T(8,128)S(1)}, u32[]{:S(2)}, u32[]{:S(2)}) %collective-permute-start.18) | collective-permute-done | bytes 32800 | tf_op jit(solution)/shard_map/ppermute | solution.py:36
  45.5 1.1 %shard_map.73 = (f32[16,640]{1,0:T(8,128)S(1)}, f32[32,8,128]{2,1,0:T(8,128)}) custom-call(f32[16,512]{1,0:T(8,128)S(1)} %get-tuple-element.29.refs_0_, f32[16,128]{1,0:T(8,128)S(1)} %get-tuple-element.30.refs_1_, f32[16,640]{1,0:T(8,128)S(1)} %collective-permute-done.15.refs_2_, f32[16,640]{1,0:T(8,128)S(1)} %collective-permute-done.16.refs_3_, ...), custom_call_target="tpu_custom_call" | custom-call | tf_op jit(solution)/shard_map/pallas_call | solution.py:349
  46.6 3.1 %all-to-all-start = ((f32[32,8,128]{2,1,0:T(8,128)}), f32[32,8,128]{2,1,0:T(8,128)S(1)}, u32[]{:S(2)}, u32[]{:S(2)}) async-start(f32[32,8,128]{2,1,0:T(8,128)} %get-tuple-element.35), calls=%async_computation | async-start | bytes 262144 | tf_op jit(solution)/shard_map/all_to_all | solution.py:412
  49.8 1.8 %collective-permute-start.24 = (f32[16,640]{1,0:T(8,128)S(1)}, f32[16,640]{1,0:T(8,128)S(1)}, u32[]{:S(2)}, u32[]{:S(2)}) collective-permute-start(f32[16,640]{1,0:T(8,128)S(1)} %get-tuple-element.36.refs_0_.refs_5_), channel_id=1, source_target_pairs={{0,2},{1,3},{2,0},{3,1},{4,6},{5,7},{6,4},{7,5},{8,10},{9,11},{10,... | collective-permute-start | bytes 122888 | tf_op jit(solution)/shard_map/ppermute | solution.py:36
  51.6 2.4 %collective-permute-done.24.refs_2_.refs_7_ = f32[16,640]{1,0:T(8,128)S(1)} collective-permute-done((f32[16,640]{1,0:T(8,128)S(1)}, f32[16,640]{1,0:T(8,128)S(1)}, u32[]{:S(2)}, u32[]{:S(2)}) %collective-permute-start.24) | collective-permute-done | bytes 40992 | tf_op jit(solution)/shard_map/ppermute | solution.py:36
  54.0 4.0 %all-to-all-done.gathered_ref = f32[32,8,128]{2,1,0:T(8,128)S(1)} async-done(((f32[32,8,128]{2,1,0:T(8,128)}), f32[32,8,128]{2,1,0:T(8,128)S(1)}, u32[]{:S(2)}, u32[]{:S(2)}) %all-to-all-start) | async-done | bytes 131104 | tf_op jit(solution)/shard_map/all_to_all | solution.py:412
  58.0 0.3 collective-permute-start.22
  58.3 2.0 %shard_map.75 = (f32[64,64]{1,0:T(8,128)S(1)}, f32[64,16]{1,0:T(8,128)S(1)}, f32[64,16]{1,0:T(8,128)S(1)}) custom-call(f32[16,640]{1,0:T(8,128)S(1)} %get-tuple-element.36.refs_0_.refs_5_, f32[16,640]{1,0:T(8,128)S(1)} %collective-permute-done.23.refs_1_.refs_6_, f32[16,640]{1,0:T(8,128)S(1)} %collective-permute-done.24.refs_2_.refs_7_, ...), custom_call_target="tpu_custom_call" | custom-call | flops 1048576 | bytes 655360 | tf_op jit(solution)/shard_map/pallas_call | solution.py:349
  60.3 3.5 %shard_map.76 = (f32[16,512]{1,0:T(8,128)}, f32[16,512]{1,0:T(8,128)}) custom-call(f32[32,128]{1,0:T(8,128)S(1)} %shard_map.74.refs_0_, f32[32,128]{1,0:T(8,128)S(1)} %collective-permute-done.22.refs_1_, f32[64,64]{1,0:T(8,128)S(1)} %get-tuple-element.37.refs_2_, f32[64,16]{1,0:T(8,128)S(1)} %get-tuple-element.38.refs_3_, ...), custom_call_target="tpu_custom_call" | custom-call | tf_op jit(solution)/shard_map/pallas_call | solution.py:349
  (17 shorter events, 0.1 us)
Async XLA Ops:
  0.6 11.6 %copy-start = (f32[16,512]{1,0:T(8,128)S(1)}, f32[16,512]{1,0:T(8,128)}, u32[]{:S(2)}) copy-start(f32[16,512]{1,0:T(8,128)} %refs_9_.1) | copy-start | bytes 98308
  0.6 11.0 %collective-permute-start = (f32[16,512]{1,0:T(8,128)}, f32[16,512]{1,0:T(8,128)S(1)}, u32[]{:S(2)}, u32[]{:S(2)}) collective-permute-start(f32[16,512]{1,0:T(8,128)} %refs_9_.1), channel_id=1, source_target_pairs={{0,8},{8,0},{16,24},{24,16},{1,9},{9,1},{17,25},{25,17},{2,10},{10... | collective-permute-start | bytes 98312 | tf_op jit(solution)/shard_map/ppermute | solution.py:36
  3.8 7.9 %collective-permute-start.1 = (f32[16,512]{1,0:T(8,128)}, f32[16,512]{1,0:T(8,128)S(1)}, u32[]{:S(2)}, u32[]{:S(2)}) collective-permute-start(f32[16,512]{1,0:T(8,128)} %refs_9_.1), channel_id=1, source_target_pairs={{0,16},{8,24},{16,0},{24,8},{1,17},{9,25},{17,1},{25,9},{2,18},{10... | collective-permute-start | bytes 98312 | tf_op jit(solution)/shard_map/ppermute | solution.py:36
  6.3 5.9 %collective-permute-start.2 = (f32[16,512]{1,0:T(8,128)}, f32[16,512]{1,0:T(8,128)S(1)}, u32[]{:S(2)}, u32[]{:S(2)}) collective-permute-start(f32[16,512]{1,0:T(8,128)} %refs_9_.1), channel_id=1, source_target_pairs={{0,24},{8,16},{16,8},{24,0},{1,25},{9,17},{17,9},{25,1},{2,26},{10... | collective-permute-start | bytes 98312 | tf_op jit(solution)/shard_map/ppermute | solution.py:36
  6.4 5.9 %collective-permute-start.3 = (f32[16,512]{1,0:T(8,128)}, f32[16,512]{1,0:T(8,128)S(1)}, u32[]{:S(2)}, u32[]{:S(2)}) collective-permute-start(f32[16,512]{1,0:T(8,128)} %refs_9_.1), channel_id=1, source_target_pairs={{0,4},{4,0},{1,5},{5,1},{2,6},{6,2},{3,7},{7,3},{8,12},{12,8},{9,1... | collective-permute-start | bytes 98312 | tf_op jit(solution)/shard_map/ppermute | solution.py:36
  14.6 7.5 %collective-permute-start.4 = (f32[16,512]{1,0:T(8,128)S(1)}, f32[16,512]{1,0:T(8,128)S(1)}, u32[]{:S(2)}, u32[]{:S(2)}) collective-permute-start(f32[16,512]{1,0:T(8,128)S(1)} %get-tuple-element.24), channel_id=1, source_target_pairs={{0,8},{8,0},{16,24},{24,16},{1,9},{9,1},{17,25},{25,17},{2,10},{10... | collective-permute-start | bytes 98312 | tf_op jit(solution)/shard_map/ppermute | solution.py:36
  14.8 7.3 %collective-permute-start.9 = (f32[16,512]{1,0:T(8,128)S(1)}, f32[16,512]{1,0:T(8,128)S(1)}, u32[]{:S(2)}, u32[]{:S(2)}) collective-permute-start(f32[16,512]{1,0:T(8,128)S(1)} %get-tuple-element.28), channel_id=1, source_target_pairs={{0,2},{1,3},{2,0},{3,1},{4,6},{5,7},{6,4},{7,5},{8,10},{9,11},{10,... | collective-permute-start | bytes 98312 | tf_op jit(solution)/shard_map/ppermute | solution.py:36
  16.3 6.3 %collective-permute-start.5 = (f32[16,512]{1,0:T(8,128)S(1)}, f32[16,512]{1,0:T(8,128)S(1)}, u32[]{:S(2)}, u32[]{:S(2)}) collective-permute-start(f32[16,512]{1,0:T(8,128)S(1)} %get-tuple-element.25), channel_id=1, source_target_pairs={{0,16},{8,24},{16,0},{24,8},{1,17},{9,25},{17,1},{25,9},{2,18},{10... | collective-permute-start | bytes 98312 | tf_op jit(solution)/shard_map/ppermute | solution.py:36
  19.7 5.7 %collective-permute-start.6 = (f32[16,512]{1,0:T(8,128)S(1)}, f32[16,512]{1,0:T(8,128)S(1)}, u32[]{:S(2)}, u32[]{:S(2)}) collective-permute-start(f32[16,512]{1,0:T(8,128)S(1)} %get-tuple-element.26), channel_id=1, source_target_pairs={{0,24},{8,16},{16,8},{24,0},{1,25},{9,17},{17,9},{25,1},{2,26},{10... | collective-permute-start | bytes 98312 | tf_op jit(solution)/shard_map/ppermute | solution.py:36
  20.5 4.9 %collective-permute-start.7 = (f32[16,512]{1,0:T(8,128)S(1)}, f32[16,512]{1,0:T(8,128)S(1)}, u32[]{:S(2)}, u32[]{:S(2)}) collective-permute-start(f32[16,512]{1,0:T(8,128)S(1)} %get-tuple-element.27), channel_id=1, source_target_pairs={{0,4},{4,0},{1,5},{5,1},{2,6},{6,2},{3,7},{7,3},{8,12},{12,8},{9,1... | collective-permute-start | bytes 98312 | tf_op jit(solution)/shard_map/ppermute | solution.py:36
  22.1 3.5 %collective-permute-start.8 = (f32[16,512]{1,0:T(8,128)S(1)}, f32[16,512]{1,0:T(8,128)S(1)}, u32[]{:S(2)}, u32[]{:S(2)}) collective-permute-start(f32[16,512]{1,0:T(8,128)S(1)} %get-tuple-element.28), channel_id=1, source_target_pairs={{0,1},{1,0},{2,3},{3,2},{4,5},{5,4},{6,7},{7,6},{8,9},{9,8},{10,11... | collective-permute-start | bytes 98312 | tf_op jit(solution)/shard_map/ppermute | solution.py:36
  22.1 3.5 %collective-permute-start.10 = (f32[16,512]{1,0:T(8,128)S(1)}, f32[16,512]{1,0:T(8,128)S(1)}, u32[]{:S(2)}, u32[]{:S(2)}) collective-permute-start(f32[16,512]{1,0:T(8,128)S(1)} %collective-permute-done.9.refs_3_.refs_8_.refs_11_), channel_id=1, source_target_pairs={{0,1},{1,0},{2,3},{3,2},{4,5},{5,4},{6,7},{7,6},{8,9},{9,8},{10,11... | collective-permute-start | bytes 98312 | tf_op jit(solution)/shard_map/ppermute | solution.py:36
  25.5 5.9 %collective-permute-start.11 = (f32[16,512]{1,0:T(8,128)S(1)}, f32[16,512]{1,0:T(8,128)S(1)}, u32[]{:S(2)}, u32[]{:S(2)}) collective-permute-start(f32[16,512]{1,0:T(8,128)S(1)} %shard_map.70.refs_0_.refs_10_.refs_13_), channel_id=1, source_target_pairs={{0,8},{8,0},{16,24},{24,16},{1,9},{9,1},{17,25},{25,17},{2,10},{10... | collective-permute-start | bytes 98312 | tf_op jit(solution)/shard_map/ppermute | solution.py:36
  26.0 8.8 %collective-permute-start.14 = (f32[16,640]{1,0:T(8,128)S(1)}, f32[16,640]{1,0:T(8,128)S(1)}, u32[]{:S(2)}, u32[]{:S(2)}) collective-permute-start(f32[16,640]{1,0:T(8,128)S(1)} %shard_map.71.refs_2_), channel_id=1, source_target_pairs={{0,4},{4,0},{1,5},{5,1},{2,6},{6,2},{3,7},{7,3},{8,12},{12,8},{9,1... | collective-permute-start | bytes 122888 | tf_op jit(solution)/shard_map/ppermute | solution.py:36
  26.5 5.0 %collective-permute-start.12 = (f32[16,512]{1,0:T(8,128)S(1)}, f32[16,512]{1,0:T(8,128)S(1)}, u32[]{:S(2)}, u32[]{:S(2)}) collective-permute-start(f32[16,512]{1,0:T(8,128)S(1)} %shard_map.70.refs_0_.refs_10_.refs_13_), channel_id=1, source_target_pairs={{0,16},{8,24},{16,0},{24,8},{1,17},{9,25},{17,1},{25,9},{2,18},{10... | collective-permute-start | bytes 98312 | tf_op jit(solution)/shard_map/ppermute | solution.py:36
  29.1 5.7 %collective-permute-start.13 = (f32[16,512]{1,0:T(8,128)S(1)}, f32[16,512]{1,0:T(8,128)S(1)}, u32[]{:S(2)}, u32[]{:S(2)}) collective-permute-start(f32[16,512]{1,0:T(8,128)S(1)} %shard_map.70.refs_0_.refs_10_.refs_13_), channel_id=1, source_target_pairs={{0,24},{8,16},{16,8},{24,0},{1,25},{9,17},{17,9},{25,1},{2,26},{10... | collective-permute-start | bytes 98312 | tf_op jit(solution)/shard_map/ppermute | solution.py:36
  30.9 10.7 %collective-permute-start.20 = (f32[16,512]{1,0:T(8,128)S(1)}, f32[16,512]{1,0:T(8,128)S(1)}, u32[]{:S(2)}, u32[]{:S(2)}) collective-permute-start(f32[16,512]{1,0:T(8,128)S(1)} %shard_map.70.refs_0_.refs_10_.refs_13_), channel_id=1, source_target_pairs={{0,2},{1,3},{2,0},{3,1},{4,6},{5,7},{6,4},{7,5},{8,10},{9,11},{10,... | collective-permute-start | bytes 98312 | tf_op jit(solution)/shard_map/ppermute | solution.py:36
  31.4 10.1 %collective-permute-start.19 = (f32[16,512]{1,0:T(8,128)S(1)}, f32[16,512]{1,0:T(8,128)S(1)}, u32[]{:S(2)}, u32[]{:S(2)}) collective-permute-start(f32[16,512]{1,0:T(8,128)S(1)} %shard_map.70.refs_0_.refs_10_.refs_13_), channel_id=1, source_target_pairs={{0,1},{1,0},{2,3},{3,2},{4,5},{5,4},{6,7},{7,6},{8,9},{9,8},{10,11... | collective-permute-start | bytes 98312 | tf_op jit(solution)/shard_map/ppermute | solution.py:36
  37.1 8.4 %collective-permute-start.15 = (f32[16,640]{1,0:T(8,128)S(1)}, f32[16,640]{1,0:T(8,128)S(1)}, u32[]{:S(2)}, u32[]{:S(2)}) collective-permute-start(f32[16,640]{1,0:T(8,128)S(1)} %get-tuple-element.31), channel_id=1, source_target_pairs={{0,8},{8,0},{16,24},{24,16},{1,9},{9,1},{17,25},{25,17},{2,10},{10... | collective-permute-start | bytes 122888 | tf_op jit(solution)/shard_map/ppermute | solution.py:36
  37.2 8.4 %collective-permute-start.16 = (f32[16,640]{1,0:T(8,128)S(1)}, f32[16,640]{1,0:T(8,128)S(1)}, u32[]{:S(2)}, u32[]{:S(2)}) collective-permute-start(f32[16,640]{1,0:T(8,128)S(1)} %get-tuple-element.32), channel_id=1, source_target_pairs={{0,16},{8,24},{16,0},{24,8},{1,17},{9,25},{17,1},{25,9},{2,18},{10... | collective-permute-start | bytes 122888 | tf_op jit(solution)/shard_map/ppermute | solution.py:36
  39.5 6.0 %collective-permute-start.17 = (f32[16,640]{1,0:T(8,128)S(1)}, f32[16,640]{1,0:T(8,128)S(1)}, u32[]{:S(2)}, u32[]{:S(2)}) collective-permute-start(f32[16,640]{1,0:T(8,128)S(1)} %get-tuple-element.33), channel_id=1, source_target_pairs={{0,24},{8,16},{16,8},{24,0},{1,25},{9,17},{17,9},{25,1},{2,26},{10... | collective-permute-start | bytes 122888 | tf_op jit(solution)/shard_map/ppermute | solution.py:36
  41.5 1.6 %collective-permute-start.21 = (f32[16,512]{1,0:T(8,128)S(1)}, f32[16,512]{1,0:T(8,128)S(1)}, u32[]{:S(2)}, u32[]{:S(2)}) collective-permute-start(f32[16,512]{1,0:T(8,128)S(1)} %collective-permute-done.20.refs_12_.refs_15_), channel_id=1, source_target_pairs={{0,1},{1,0},{2,3},{3,2},{4,5},{5,4},{6,7},{7,6},{8,9},{9,8},{10,11... | collective-permute-start | bytes 98312 | tf_op jit(solution)/shard_map/ppermute | solution.py:36
  41.5 4.0 %collective-permute-start.18 = (f32[16,512]{1,0:T(8,128)S(1)}, f32[16,512]{1,0:T(8,128)S(1)}, u32[]{:S(2)}, u32[]{:S(2)}) collective-permute-start(f32[16,512]{1,0:T(8,128)S(1)} %get-tuple-element.34), channel_id=1, source_target_pairs={{0,4},{4,0},{1,5},{5,1},{2,6},{6,2},{3,7},{7,3},{8,12},{12,8},{9,1... | collective-permute-start | bytes 98312 | tf_op jit(solution)/shard_map/ppermute | solution.py:36
  46.6 11.3 %all-to-all-start = ((f32[32,8,128]{2,1,0:T(8,128)}), f32[32,8,128]{2,1,0:T(8,128)S(1)}, u32[]{:S(2)}, u32[]{:S(2)}) async-start(f32[32,8,128]{2,1,0:T(8,128)} %get-tuple-element.35), calls=%async_computation | async-start | bytes 262144 | tf_op jit(solution)/shard_map/all_to_all | solution.py:412
  49.8 4.2 %collective-permute-start.24 = (f32[16,640]{1,0:T(8,128)S(1)}, f32[16,640]{1,0:T(8,128)S(1)}, u32[]{:S(2)}, u32[]{:S(2)}) collective-permute-start(f32[16,640]{1,0:T(8,128)S(1)} %get-tuple-element.36.refs_0_.refs_5_), channel_id=1, source_target_pairs={{0,2},{1,3},{2,0},{3,1},{4,6},{5,7},{6,4},{7,5},{8,10},{9,11},{10,... | collective-permute-start | bytes 122888 | tf_op jit(solution)/shard_map/ppermute | solution.py:36
  51.6 6.7 %collective-permute-start.23 = (f32[16,640]{1,0:T(8,128)S(1)}, f32[16,640]{1,0:T(8,128)S(1)}, u32[]{:S(2)}, u32[]{:S(2)}) collective-permute-start(f32[16,640]{1,0:T(8,128)S(1)} %get-tuple-element.36.refs_0_.refs_5_), channel_id=1, source_target_pairs={{0,1},{1,0},{2,3},{3,2},{4,5},{5,4},{6,7},{7,6},{8,9},{9,8},{10,11... | collective-permute-start | bytes 122888 | tf_op jit(solution)/shard_map/ppermute | solution.py:36
  54.0 4.3 %collective-permute-start.25 = (f32[16,640]{1,0:T(8,128)S(1)}, f32[16,640]{1,0:T(8,128)S(1)}, u32[]{:S(2)}, u32[]{:S(2)}) collective-permute-start(f32[16,640]{1,0:T(8,128)S(1)} %collective-permute-done.24.refs_2_.refs_7_), channel_id=1, source_target_pairs={{0,1},{1,0},{2,3},{3,2},{4,5},{5,4},{6,7},{7,6},{8,9},{9,8},{10,11... | collective-permute-start | bytes 122888 | tf_op jit(solution)/shard_map/ppermute | solution.py:36
  58.0 2.3 %collective-permute-start.22 = (f32[32,128]{1,0:T(8,128)S(1)}, f32[32,128]{1,0:T(8,128)S(1)}, u32[]{:S(2)}, u32[]{:S(2)}) collective-permute-start(f32[32,128]{1,0:T(8,128)S(1)} %shard_map.74.refs_0_), channel_id=1, source_target_pairs={{0,1},{1,0},{2,3},{3,2},{4,5},{5,4},{6,7},{7,6},{8,9},{9,8},{10,11... | collective-permute-start | bytes 49160 | tf_op jit(solution)/shard_map/ppermute | solution.py:419

commit v7 on v6

--- a/solution.py
+++ b/solution.py
@@ -11,7 +11,7 @@
 BLK = 256
 SEG = 2
 PIVOT = 8
-PANEL = 32
+PANEL = 16
 HIGHEST = lax.Precision.HIGHEST
 VMEM = pl.BlockSpec(memory_space=pltpu.VMEM)
 SMEM = pl.BlockSpec(memory_space=pltpu.SMEM)
@@ -89,7 +89,7 @@
         all_ref[pl.ds(pl.multiple_of(place * width, width), width), :] = ref[:, 0:points]
 
 
-def prepare(count_ref, rows_ref, cols_ref, blocks_ref, blocks_out, table_out, rows_at, cols_at, sems):
+def prepare(count_ref, rows_ref, cols_ref, blocks_ref, blocks_out, table_out, rows_at, cols_at, places, sems):
     slots = blocks_ref.shape[2]
     copies = [pltpu.make_async_copy(blocks_ref.at[0, 0, s], blocks_out.at[s], sems.at[s]) for s in range(slots)]
     small = [
@@ -101,11 +101,14 @@
     for copy in small:
         copy.wait()
     for slot in range(slots):
-        table_out[0, slot] = rows_at[0, 0, slot]
-        table_out[1, slot] = cols_at[0, 0, slot]
-        table_out[2, slot] = count_ref[0, 0]
+        places[0, slot] = rows_at[0, 0, slot]
+        places[1, slot] = cols_at[0, 0, slot]
+        places[2, slot] = count_ref[0, 0]
+    table = pltpu.make_async_copy(places, table_out, sems.at[slots + 2])
+    table.start()
     for copy in copies:
         copy.wait()
+    table.wait()
 
 
 def products(
@@ -379,9 +382,10 @@
         [block_count] + [pltpu.with_memory_space_constraint(x, pltpu.HBM) for x in (block_rows, block_cols, blocks)],
         [SMEM] + [pl.BlockSpec(memory_space=pltpu.HBM)] * 3,
         [blocks.shape[2:], jax.ShapeDtypeStruct((3, slots), jnp.int32)],
-        [pltpu.SMEM(block_rows.shape, jnp.int32)] * 2 + [pltpu.SemaphoreType.DMA((slots + 2,))],
+        [pltpu.SMEM(block_rows.shape, jnp.int32)] * 2
+        + [pltpu.SMEM((3, slots), jnp.int32), pltpu.SemaphoreType.DMA((slots + 3,))],
         pl.CostEstimate(flops=0, transcendentals=0, bytes_accessed=8 * blocks.size),
-        [VMEM, SMEM],
+        [VMEM, VMEM],
     )
     head = [table, near]
     partial, copied, *rest = call(

time: 64 us -> 63.5 us (level)
  transfers between devices with their start and end apart: 27 -> 27, of which waited for: 7 -> 7; matrix products, arithmetic and copies ran while one was open for 0% -> 0% of each run, Pallas kernels for 12% -> 11%
where the time goes in v7:
time: 63.5 us; the launch traced here: 63.3 us
  starting transfers between devices  31.6 us (50%)
  waiting for transfers between devices  16.3 us (26%)
  Pallas kernels  14 us (22%)
  between operations  1.43 us (2%)
    ppermute x25, starting transfers between devices, send(): lax.ppermute(x, axis, [(i, partner(i, step, size)) for i in range(size)])  28.8 us
    pallas_call x9, Pallas kernels, call(): pl.pallas_call(body, out_shape=[s if hasattr(s, 'dtype') else jax.ShapeDt...  14 us
    ppermute x25, waiting for transfers between devices, send(): lax.ppermute(x, axis, [(i, partner(i, step, size)) for i in range(size)])  12.3 us
    all_to_all x1, waiting for transfers between devices, per_device(): late = lax.all_to_all(late, ('row', 'col', 'depth'), 0, 0)  3.96 us
    all_to_all x1, starting transfers between devices, per_device(): late = lax.all_to_all(late, ('row', 'col', 'depth'), 0, 0)  2.57 us
  transfers between devices with their start and end apart: 27, of which 7 were waited for; matrix products, arithmetic and copies ran while one was open for 0% of the time, Pallas kernels for 11%

profile of v7, /device:TPU:0, one launch (start us, length us, event | category | flops | bytes accessed | tf_op | source)
XLA Modules:
  0.0 63.3 jit_solution(4167899472819238826)
XLA Ops:
  0.6 3.1 %collective-permute-start = (f32[16,512]{1,0:T(8,128)}, f32[16,512]{1,0:T(8,128)S(1)}, u32[]{:S(2)}, u32[]{:S(2)}) collective-permute-start(f32[16,512]{1,0:T(8,128)} %refs_9_.1), channel_id=1, source_target_pairs={{0,8},{8,0},{16,24},{24,16},{1,9},{9,1},{17,25},{25,17},{2,10},{10... | collective-permute-start | bytes 98312 | tf_op jit(solution)/shard_map/ppermute | solution.py:36
  3.8 2.6 %collective-permute-start.1 = (f32[16,512]{1,0:T(8,128)}, f32[16,512]{1,0:T(8,128)S(1)}, u32[]{:S(2)}, u32[]{:S(2)}) collective-permute-start(f32[16,512]{1,0:T(8,128)} %refs_9_.1), channel_id=1, source_target_pairs={{0,16},{8,24},{16,0},{24,8},{1,17},{9,25},{17,1},{25,9},{2,18},{10... | collective-permute-start | bytes 98312 | tf_op jit(solution)/shard_map/ppermute | solution.py:36
  6.4 1.7 %collective-permute-start.3 = (f32[16,512]{1,0:T(8,128)}, f32[16,512]{1,0:T(8,128)S(1)}, u32[]{:S(2)}, u32[]{:S(2)}) collective-permute-start(f32[16,512]{1,0:T(8,128)} %refs_9_.1), channel_id=1, source_target_pairs={{0,4},{4,0},{1,5},{5,1},{2,6},{6,2},{3,7},{7,3},{8,12},{12,8},{9,1... | collective-permute-start | bytes 98312 | tf_op jit(solution)/shard_map/ppermute | solution.py:36
  8.7 2.3 %shard_map.68 = (f32[16,256,256]{2,1,0:T(8,128)S(1)}, s32[3,16]{1,0:T(4,128)S(1)}) custom-call(s32[1,1]{1,0:T(1,128)S(6)} %copy.7.count_ref, s32[1,1,16]{2,1,0:T(1,128)} %rows_ref.1, s32[1,1,16]{2,1,0:T(1,128)} %cols_ref.1, f32[1,1,16,256,256]{4,3,2,1,0:T(8,128)} %blocks_ref.1), custom_call_target="tpu_custom_call" | custom-call | bytes 8388608 | tf_op jit(solution)/shard_map/pallas_call | solution.py:352
  11.1 0.0 collective-permute-done.refs_3_
  11.1 1.2 %collective-permute-done.2.refs_5_ = f32[16,512]{1,0:T(8,128)S(1)} collective-permute-done((f32[16,512]{1,0:T(8,128)}, f32[16,512]{1,0:T(8,128)S(1)}, u32[]{:S(2)}, u32[]{:S(2)}) %collective-permute-start.2) | collective-permute-done | bytes 32800 | tf_op jit(solution)/shard_map/ppermute | solution.py:36
  12.3 0.0 collective-permute-done.3.refs_6_
  12.3 2.3 %shard_map.69 = (f32[16,512]{1,0:T(8,128)S(1)}, f32[16,512]{1,0:T(8,128)S(1)}, f32[16,512]{1,0:T(8,128)S(1)}, f32[16,512]{1,0:T(8,128)S(1)}, f32[16,512]{1,0:T(8,128)S(1)}, /*index=5*/f32[16,512]{1,0:T(8,128)S(1)}) custom-call(s32[3,16]{1,0:T(4,128)S(1)} %get-tuple-element.21.refs_0_, f32[16,256,256]{2,1,0:T(8,128)S(1)} %get-tuple-element.22.refs_1_, ...), custom_call_target="tpu_custom_call" | custom-call | tf_op jit(solution)/shard_map/pallas_call | solution.py:352
  14.6 0.1 collective-permute-start.4
  14.7 1.6 %collective-permute-start.9 = (f32[16,512]{1,0:T(8,128)S(1)}, f32[16,512]{1,0:T(8,128)S(1)}, u32[]{:S(2)}, u32[]{:S(2)}) collective-permute-start(f32[16,512]{1,0:T(8,128)S(1)} %get-tuple-element.28), channel_id=1, source_target_pairs={{0,2},{1,3},{2,0},{3,1},{4,6},{5,7},{6,4},{7,5},{8,10},{9,11},{10,... | collective-permute-start | bytes 98312 | tf_op jit(solution)/shard_map/ppermute | solution.py:36
  16.2 2.9 %collective-permute-start.5 = (f32[16,512]{1,0:T(8,128)S(1)}, f32[16,512]{1,0:T(8,128)S(1)}, u32[]{:S(2)}, u32[]{:S(2)}) collective-permute-start(f32[16,512]{1,0:T(8,128)S(1)} %get-tuple-element.25), channel_id=1, source_target_pairs={{0,16},{8,24},{16,0},{24,8},{1,17},{9,25},{17,1},{25,9},{2,18},{10... | collective-permute-start | bytes 98312 | tf_op jit(solution)/shard_map/ppermute | solution.py:36
  19.1 1.4 %collective-permute-start.6 = (f32[16,512]{1,0:T(8,128)S(1)}, f32[16,512]{1,0:T(8,128)S(1)}, u32[]{:S(2)}, u32[]{:S(2)}) collective-permute-start(f32[16,512]{1,0:T(8,128)S(1)} %get-tuple-element.26), channel_id=1, source_target_pairs={{0,24},{8,16},{16,8},{24,0},{1,25},{9,17},{17,9},{25,1},{2,26},{10... | collective-permute-start | bytes 98312 | tf_op jit(solution)/shard_map/ppermute | solution.py:36
  20.5 1.5 %collective-permute-start.7 = (f32[16,512]{1,0:T(8,128)S(1)}, f32[16,512]{1,0:T(8,128)S(1)}, u32[]{:S(2)}, u32[]{:S(2)}) collective-permute-start(f32[16,512]{1,0:T(8,128)S(1)} %get-tuple-element.27), channel_id=1, source_target_pairs={{0,4},{4,0},{1,5},{5,1},{2,6},{6,2},{3,7},{7,3},{8,12},{12,8},{9,1... | collective-permute-start | bytes 98312 | tf_op jit(solution)/shard_map/ppermute | solution.py:36
  22.1 0.0 collective-permute-done.4.refs_1_
  22.1 0.0 collective-permute-start.8
  22.1 0.0 collective-permute-done.9.refs_3_.refs_8_.refs_11_
  22.1 0.5 collective-permute-start.10
  22.6 0.0 collective-permute-done.5.refs_2_
  22.6 2.3 %collective-permute-done.6.refs_3_ = f32[16,512]{1,0:T(8,128)S(1)} collective-permute-done((f32[16,512]{1,0:T(8,128)S(1)}, f32[16,512]{1,0:T(8,128)S(1)}, u32[]{:S(2)}, u32[]{:S(2)}) %collective-permute-start.6) | collective-permute-done | bytes 32800 | tf_op jit(solution)/shard_map/ppermute | solution.py:36
  24.9 0.0 collective-permute-done.7.refs_4_
  24.9 0.1 collective-permute-start.11
  25.0 0.0 collective-permute-done.10.refs_4_.refs_9_.refs_12_
  25.0 0.4 shard_map.71.refs_2_
  25.4 1.1 %collective-permute-start.14 = (f32[16,640]{1,0:T(8,128)S(1)}, f32[16,640]{1,0:T(8,128)S(1)}, u32[]{:S(2)}, u32[]{:S(2)}) collective-permute-start(f32[16,640]{1,0:T(8,128)S(1)} %shard_map.71.refs_2_), channel_id=1, source_target_pairs={{0,4},{4,0},{1,5},{5,1},{2,6},{6,2},{3,7},{7,3},{8,12},{12,8},{9,1... | collective-permute-start | bytes 122888 | tf_op jit(solution)/shard_map/ppermute | solution.py:36
  26.5 2.5 %collective-permute-start.12 = (f32[16,512]{1,0:T(8,128)S(1)}, f32[16,512]{1,0:T(8,128)S(1)}, u32[]{:S(2)}, u32[]{:S(2)}) collective-permute-start(f32[16,512]{1,0:T(8,128)S(1)} %shard_map.70.refs_0_.refs_10_.refs_13_), channel_id=1, source_target_pairs={{0,16},{8,24},{16,0},{24,8},{1,17},{9,25},{17,1},{25,9},{2,18},{10... | collective-permute-start | bytes 98312 | tf_op jit(solution)/shard_map/ppermute | solution.py:36
  29.0 1.8 %collective-permute-start.13 = (f32[16,512]{1,0:T(8,128)S(1)}, f32[16,512]{1,0:T(8,128)S(1)}, u32[]{:S(2)}, u32[]{:S(2)}) collective-permute-start(f32[16,512]{1,0:T(8,128)S(1)} %shard_map.70.refs_0_.refs_10_.refs_13_), channel_id=1, source_target_pairs={{0,24},{8,16},{16,8},{24,0},{1,25},{9,17},{17,9},{25,1},{2,26},{10... | collective-permute-start | bytes 98312 | tf_op jit(solution)/shard_map/ppermute | solution.py:36
  30.9 0.5 collective-permute-start.20
  31.4 0.0 collective-permute-start.19
  31.4 0.0 collective-permute-done.12.refs_4_
  31.4 3.4 %collective-permute-done.13.refs_5_ = f32[16,512]{1,0:T(8,128)S(1)} collective-permute-done((f32[16,512]{1,0:T(8,128)S(1)}, f32[16,512]{1,0:T(8,128)S(1)}, u32[]{:S(2)}, u32[]{:S(2)}) %collective-permute-start.13) | collective-permute-done | bytes 32800 | tf_op jit(solution)/shard_map/ppermute | solution.py:36
  34.8 0.0 collective-permute-done.14.refs_6_
  34.8 2.3 %shard_map.72 = (f32[16,512]{1,0:T(8,128)S(1)}, f32[16,128]{1,0:T(8,128)S(1)}, f32[16,640]{1,0:T(8,128)S(1)}, f32[16,640]{1,0:T(8,128)S(1)}, f32[16,640]{1,0:T(8,128)S(1)}, /*index=5*/f32[16,512]{1,0:T(8,128)S(1)}) custom-call(s32[3,16]{1,0:T(4,128)S(1)} %get-tuple-element.21.refs_0_, f32[16,256,256]{2,1,0:T(8,128)S(1)} %get-tuple-element.22.refs_1_, ...), custom_call_target="tpu_custom_call" | custom-call | tf_op jit(solution)/shard_map/pallas_call | solution.py:352
  37.1 0.1 collective-permute-start.15
  37.2 2.4 %collective-permute-start.16 = (f32[16,640]{1,0:T(8,128)S(1)}, f32[16,640]{1,0:T(8,128)S(1)}, u32[]{:S(2)}, u32[]{:S(2)}) collective-permute-start(f32[16,640]{1,0:T(8,128)S(1)} %get-tuple-element.32), channel_id=1, source_target_pairs={{0,16},{8,24},{16,0},{24,8},{1,17},{9,25},{17,1},{25,9},{2,18},{10... | collective-permute-start | bytes 122888 | tf_op jit(solution)/shard_map/ppermute | solution.py:36
  39.5 2.0 %collective-permute-start.17 = (f32[16,640]{1,0:T(8,128)S(1)}, f32[16,640]{1,0:T(8,128)S(1)}, u32[]{:S(2)}, u32[]{:S(2)}) collective-permute-start(f32[16,640]{1,0:T(8,128)S(1)} %get-tuple-element.33), channel_id=1, source_target_pairs={{0,24},{8,16},{16,8},{24,0},{1,25},{9,17},{17,9},{25,1},{2,26},{10... | collective-permute-start | bytes 122888 | tf_op jit(solution)/shard_map/ppermute | solution.py:36
  41.5 0.0 collective-permute-start.21
  41.5 0.0 collective-permute-done.19.refs_11_.refs_14_
  41.5 1.0 %collective-permute-start.18 = (f32[16,512]{1,0:T(8,128)S(1)}, f32[16,512]{1,0:T(8,128)S(1)}, u32[]{:S(2)}, u32[]{:S(2)}) collective-permute-start(f32[16,512]{1,0:T(8,128)S(1)} %get-tuple-element.34), channel_id=1, source_target_pairs={{0,4},{4,0},{1,5},{5,1},{2,6},{6,2},{3,7},{7,3},{8,12},{12,8},{9,1... | collective-permute-start | bytes 98312 | tf_op jit(solution)/shard_map/ppermute | solution.py:36
  42.5 0.2 collective-permute-done.21.refs_13_.refs_16_
  42.7 2.8 %collective-permute-done.18.refs_5_ = f32[16,512]{1,0:T(8,128)S(1)} collective-permute-done((f32[16,512]{1,0:T(8,128)S(1)}, f32[16,512]{1,0:T(8,128)S(1)}, u32[]{:S(2)}, u32[]{:S(2)}) %collective-permute-start.18) | collective-permute-done | bytes 32800 | tf_op jit(solution)/shard_map/ppermute | solution.py:36
  45.5 1.1 %shard_map.73 = (f32[16,640]{1,0:T(8,128)S(1)}, f32[32,8,128]{2,1,0:T(8,128)}) custom-call(f32[16,512]{1,0:T(8,128)S(1)} %get-tuple-element.29.refs_0_, f32[16,128]{1,0:T(8,128)S(1)} %get-tuple-element.30.refs_1_, f32[16,640]{1,0:T(8,128)S(1)} %collective-permute-done.15.refs_2_, f32[16,640]{1,0:T(8,128)S(1)} %collective-permute-done.16.refs_3_, ...), custom_call_target="tpu_custom_call" | custom-call | tf_op jit(solution)/shard_map/pallas_call | solution.py:352
  46.6 2.6 %all-to-all-start = ((f32[32,8,128]{2,1,0:T(8,128)}), f32[32,8,128]{2,1,0:T(8,128)S(1)}, u32[]{:S(2)}, u32[]{:S(2)}) async-start(f32[32,8,128]{2,1,0:T(8,128)} %get-tuple-element.35), calls=%async_computation | async-start | bytes 262144 | tf_op jit(solution)/shard_map/all_to_all | solution.py:416
  49.2 1.8 %collective-permute-start.24 = (f32[16,640]{1,0:T(8,128)S(1)}, f32[16,640]{1,0:T(8,128)S(1)}, u32[]{:S(2)}, u32[]{:S(2)}) collective-permute-start(f32[16,640]{1,0:T(8,128)S(1)} %get-tuple-element.36.refs_0_.refs_5_), channel_id=1, source_target_pairs={{0,2},{1,3},{2,0},{3,1},{4,6},{5,7},{6,4},{7,5},{8,10},{9,11},{10,... | collective-permute-start | bytes 122888 | tf_op jit(solution)/shard_map/ppermute | solution.py:36
  51.0 2.4 %collective-permute-done.24.refs_2_.refs_7_ = f32[16,640]{1,0:T(8,128)S(1)} collective-permute-done((f32[16,640]{1,0:T(8,128)S(1)}, f32[16,640]{1,0:T(8,128)S(1)}, u32[]{:S(2)}, u32[]{:S(2)}) %collective-permute-start.24) | collective-permute-done | bytes 40992 | tf_op jit(solution)/shard_map/ppermute | solution.py:36
  53.5 4.0 %all-to-all-done.gathered_ref = f32[32,8,128]{2,1,0:T(8,128)S(1)} async-done(((f32[32,8,128]{2,1,0:T(8,128)}), f32[32,8,128]{2,1,0:T(8,128)S(1)}, u32[]{:S(2)}, u32[]{:S(2)}) %all-to-all-start) | async-done | bytes 131104 | tf_op jit(solution)/shard_map/all_to_all | solution.py:416
  57.4 0.3 collective-permute-start.22
  57.7 2.0 %shard_map.75 = (f32[64,64]{1,0:T(8,128)S(1)}, f32[64,16]{1,0:T(8,128)S(1)}, f32[64,16]{1,0:T(8,128)S(1)}) custom-call(f32[16,640]{1,0:T(8,128)S(1)} %get-tuple-element.36.refs_0_.refs_5_, f32[16,640]{1,0:T(8,128)S(1)} %collective-permute-done.23.refs_1_.refs_6_, f32[16,640]{1,0:T(8,128)S(1)} %collective-permute-done.24.refs_2_.refs_7_, ...), custom_call_target="tpu_custom_call" | custom-call | flops 1048576 | bytes 655360 | tf_op jit(solution)/shard_map/pallas_call | solution.py:352
  59.7 3.6 %shard_map.76 = (f32[16,512]{1,0:T(8,128)}, f32[16,512]{1,0:T(8,128)}) custom-call(f32[32,128]{1,0:T(8,128)S(1)} %shard_map.74.refs_0_, f32[32,128]{1,0:T(8,128)S(1)} %collective-permute-done.22.refs_1_, f32[64,64]{1,0:T(8,128)S(1)} %get-tuple-element.37.refs_2_, f32[64,16]{1,0:T(8,128)S(1)} %get-tuple-element.38.refs_3_, ...), custom_call_target="tpu_custom_call" | custom-call | tf_op jit(solution)/shard_map/pallas_call | solution.py:352
  (17 shorter events, 0.1 us)
Async XLA Ops:
  0.6 11.6 %copy-start = (f32[16,512]{1,0:T(8,128)S(1)}, f32[16,512]{1,0:T(8,128)}, u32[]{:S(2)}) copy-start(f32[16,512]{1,0:T(8,128)} %refs_9_.1) | copy-start | bytes 98308
  0.6 10.4 %collective-permute-start = (f32[16,512]{1,0:T(8,128)}, f32[16,512]{1,0:T(8,128)S(1)}, u32[]{:S(2)}, u32[]{:S(2)}) collective-permute-start(f32[16,512]{1,0:T(8,128)} %refs_9_.1), channel_id=1, source_target_pairs={{0,8},{8,0},{16,24},{24,16},{1,9},{9,1},{17,25},{25,17},{2,10},{10... | collective-permute-start | bytes 98312 | tf_op jit(solution)/shard_map/ppermute | solution.py:36
  3.8 7.3 %collective-permute-start.1 = (f32[16,512]{1,0:T(8,128)}, f32[16,512]{1,0:T(8,128)S(1)}, u32[]{:S(2)}, u32[]{:S(2)}) collective-permute-start(f32[16,512]{1,0:T(8,128)} %refs_9_.1), channel_id=1, source_target_pairs={{0,16},{8,24},{16,0},{24,8},{1,17},{9,25},{17,1},{25,9},{2,18},{10... | collective-permute-start | bytes 98312 | tf_op jit(solution)/shard_map/ppermute | solution.py:36
  6.3 5.9 %collective-permute-start.2 = (f32[16,512]{1,0:T(8,128)}, f32[16,512]{1,0:T(8,128)S(1)}, u32[]{:S(2)}, u32[]{:S(2)}) collective-permute-start(f32[16,512]{1,0:T(8,128)} %refs_9_.1), channel_id=1, source_target_pairs={{0,24},{8,16},{16,8},{24,0},{1,25},{9,17},{17,9},{25,1},{2,26},{10... | collective-permute-start | bytes 98312 | tf_op jit(solution)/shard_map/ppermute | solution.py:36
  6.4 5.9 %collective-permute-start.3 = (f32[16,512]{1,0:T(8,128)}, f32[16,512]{1,0:T(8,128)S(1)}, u32[]{:S(2)}, u32[]{:S(2)}) collective-permute-start(f32[16,512]{1,0:T(8,128)} %refs_9_.1), channel_id=1, source_target_pairs={{0,4},{4,0},{1,5},{5,1},{2,6},{6,2},{3,7},{7,3},{8,12},{12,8},{9,1... | collective-permute-start | bytes 98312 | tf_op jit(solution)/shard_map/ppermute | solution.py:36
  14.6 7.5 %collective-permute-start.4 = (f32[16,512]{1,0:T(8,128)S(1)}, f32[16,512]{1,0:T(8,128)S(1)}, u32[]{:S(2)}, u32[]{:S(2)}) collective-permute-start(f32[16,512]{1,0:T(8,128)S(1)} %get-tuple-element.24), channel_id=1, source_target_pairs={{0,8},{8,0},{16,24},{24,16},{1,9},{9,1},{17,25},{25,17},{2,10},{10... | collective-permute-start | bytes 98312 | tf_op jit(solution)/shard_map/ppermute | solution.py:36
  14.7 7.4 %collective-permute-start.9 = (f32[16,512]{1,0:T(8,128)S(1)}, f32[16,512]{1,0:T(8,128)S(1)}, u32[]{:S(2)}, u32[]{:S(2)}) collective-permute-start(f32[16,512]{1,0:T(8,128)S(1)} %get-tuple-element.28), channel_id=1, source_target_pairs={{0,2},{1,3},{2,0},{3,1},{4,6},{5,7},{6,4},{7,5},{8,10},{9,11},{10,... | collective-permute-start | bytes 98312 | tf_op jit(solution)/shard_map/ppermute | solution.py:36
  16.2 6.4 %collective-permute-start.5 = (f32[16,512]{1,0:T(8,128)S(1)}, f32[16,512]{1,0:T(8,128)S(1)}, u32[]{:S(2)}, u32[]{:S(2)}) collective-permute-start(f32[16,512]{1,0:T(8,128)S(1)} %get-tuple-element.25), channel_id=1, source_target_pairs={{0,16},{8,24},{16,0},{24,8},{1,17},{9,25},{17,1},{25,9},{2,18},{10... | collective-permute-start | bytes 98312 | tf_op jit(solution)/shard_map/ppermute | solution.py:36
  19.1 5.7 %collective-permute-start.6 = (f32[16,512]{1,0:T(8,128)S(1)}, f32[16,512]{1,0:T(8,128)S(1)}, u32[]{:S(2)}, u32[]{:S(2)}) collective-permute-start(f32[16,512]{1,0:T(8,128)S(1)} %get-tuple-element.26), channel_id=1, source_target_pairs={{0,24},{8,16},{16,8},{24,0},{1,25},{9,17},{17,9},{25,1},{2,26},{10... | collective-permute-start | bytes 98312 | tf_op jit(solution)/shard_map/ppermute | solution.py:36
  20.5 4.3 %collective-permute-start.7 = (f32[16,512]{1,0:T(8,128)S(1)}, f32[16,512]{1,0:T(8,128)S(1)}, u32[]{:S(2)}, u32[]{:S(2)}) collective-permute-start(f32[16,512]{1,0:T(8,128)S(1)} %get-tuple-element.27), channel_id=1, source_target_pairs={{0,4},{4,0},{1,5},{5,1},{2,6},{6,2},{3,7},{7,3},{8,12},{12,8},{9,1... | collective-permute-start | bytes 98312 | tf_op jit(solution)/shard_map/ppermute | solution.py:36
  22.1 2.9 %collective-permute-start.8 = (f32[16,512]{1,0:T(8,128)S(1)}, f32[16,512]{1,0:T(8,128)S(1)}, u32[]{:S(2)}, u32[]{:S(2)}) collective-permute-start(f32[16,512]{1,0:T(8,128)S(1)} %get-tuple-element.28), channel_id=1, source_target_pairs={{0,1},{1,0},{2,3},{3,2},{4,5},{5,4},{6,7},{7,6},{8,9},{9,8},{10,11... | collective-permute-start | bytes 98312 | tf_op jit(solution)/shard_map/ppermute | solution.py:36
  22.1 2.9 %collective-permute-start.10 = (f32[16,512]{1,0:T(8,128)S(1)}, f32[16,512]{1,0:T(8,128)S(1)}, u32[]{:S(2)}, u32[]{:S(2)}) collective-permute-start(f32[16,512]{1,0:T(8,128)S(1)} %collective-permute-done.9.refs_3_.refs_8_.refs_11_), channel_id=1, source_target_pairs={{0,1},{1,0},{2,3},{3,2},{4,5},{5,4},{6,7},{7,6},{8,9},{9,8},{10,11... | collective-permute-start | bytes 98312 | tf_op jit(solution)/shard_map/ppermute | solution.py:36
  24.9 6.5 %collective-permute-start.11 = (f32[16,512]{1,0:T(8,128)S(1)}, f32[16,512]{1,0:T(8,128)S(1)}, u32[]{:S(2)}, u32[]{:S(2)}) collective-permute-start(f32[16,512]{1,0:T(8,128)S(1)} %shard_map.70.refs_0_.refs_10_.refs_13_), channel_id=1, source_target_pairs={{0,8},{8,0},{16,24},{24,16},{1,9},{9,1},{17,25},{25,17},{2,10},{10... | collective-permute-start | bytes 98312 | tf_op jit(solution)/shard_map/ppermute | solution.py:36
  25.4 9.4 %collective-permute-start.14 = (f32[16,640]{1,0:T(8,128)S(1)}, f32[16,640]{1,0:T(8,128)S(1)}, u32[]{:S(2)}, u32[]{:S(2)}) collective-permute-start(f32[16,640]{1,0:T(8,128)S(1)} %shard_map.71.refs_2_), channel_id=1, source_target_pairs={{0,4},{4,0},{1,5},{5,1},{2,6},{6,2},{3,7},{7,3},{8,12},{12,8},{9,1... | collective-permute-start | bytes 122888 | tf_op jit(solution)/shard_map/ppermute | solution.py:36
  26.5 4.9 %collective-permute-start.12 = (f32[16,512]{1,0:T(8,128)S(1)}, f32[16,512]{1,0:T(8,128)S(1)}, u32[]{:S(2)}, u32[]{:S(2)}) collective-permute-start(f32[16,512]{1,0:T(8,128)S(1)} %shard_map.70.refs_0_.refs_10_.refs_13_), channel_id=1, source_target_pairs={{0,16},{8,24},{16,0},{24,8},{1,17},{9,25},{17,1},{25,9},{2,18},{10... | collective-permute-start | bytes 98312 | tf_op jit(solution)/shard_map/ppermute | solution.py:36
  29.0 5.7 %collective-permute-start.13 = (f32[16,512]{1,0:T(8,128)S(1)}, f32[16,512]{1,0:T(8,128)S(1)}, u32[]{:S(2)}, u32[]{:S(2)}) collective-permute-start(f32[16,512]{1,0:T(8,128)S(1)} %shard_map.70.refs_0_.refs_10_.refs_13_), channel_id=1, source_target_pairs={{0,24},{8,16},{16,8},{24,0},{1,25},{9,17},{17,9},{25,1},{2,26},{10... | collective-permute-start | bytes 98312 | tf_op jit(solution)/shard_map/ppermute | solution.py:36
  30.9 10.7 %collective-permute-start.20 = (f32[16,512]{1,0:T(8,128)S(1)}, f32[16,512]{1,0:T(8,128)S(1)}, u32[]{:S(2)}, u32[]{:S(2)}) collective-permute-start(f32[16,512]{1,0:T(8,128)S(1)} %shard_map.70.refs_0_.refs_10_.refs_13_), channel_id=1, source_target_pairs={{0,2},{1,3},{2,0},{3,1},{4,6},{5,7},{6,4},{7,5},{8,10},{9,11},{10,... | collective-permute-start | bytes 98312 | tf_op jit(solution)/shard_map/ppermute | solution.py:36
  31.4 10.1 %collective-permute-start.19 = (f32[16,512]{1,0:T(8,128)S(1)}, f32[16,512]{1,0:T(8,128)S(1)}, u32[]{:S(2)}, u32[]{:S(2)}) collective-permute-start(f32[16,512]{1,0:T(8,128)S(1)} %shard_map.70.refs_0_.refs_10_.refs_13_), channel_id=1, source_target_pairs={{0,1},{1,0},{2,3},{3,2},{4,5},{5,4},{6,7},{7,6},{8,9},{9,8},{10,11... | collective-permute-start | bytes 98312 | tf_op jit(solution)/shard_map/ppermute | solution.py:36
  37.1 8.4 %collective-permute-start.15 = (f32[16,640]{1,0:T(8,128)S(1)}, f32[16,640]{1,0:T(8,128)S(1)}, u32[]{:S(2)}, u32[]{:S(2)}) collective-permute-start(f32[16,640]{1,0:T(8,128)S(1)} %get-tuple-element.31), channel_id=1, source_target_pairs={{0,8},{8,0},{16,24},{24,16},{1,9},{9,1},{17,25},{25,17},{2,10},{10... | collective-permute-start | bytes 122888 | tf_op jit(solution)/shard_map/ppermute | solution.py:36
  37.2 8.4 %collective-permute-start.16 = (f32[16,640]{1,0:T(8,128)S(1)}, f32[16,640]{1,0:T(8,128)S(1)}, u32[]{:S(2)}, u32[]{:S(2)}) collective-permute-start(f32[16,640]{1,0:T(8,128)S(1)} %get-tuple-element.32), channel_id=1, source_target_pairs={{0,16},{8,24},{16,0},{24,8},{1,17},{9,25},{17,1},{25,9},{2,18},{10... | collective-permute-start | bytes 122888 | tf_op jit(solution)/shard_map/ppermute | solution.py:36
  39.5 6.0 %collective-permute-start.17 = (f32[16,640]{1,0:T(8,128)S(1)}, f32[16,640]{1,0:T(8,128)S(1)}, u32[]{:S(2)}, u32[]{:S(2)}) collective-permute-start(f32[16,640]{1,0:T(8,128)S(1)} %get-tuple-element.33), channel_id=1, source_target_pairs={{0,24},{8,16},{16,8},{24,0},{1,25},{9,17},{17,9},{25,1},{2,26},{10... | collective-permute-start | bytes 122888 | tf_op jit(solution)/shard_map/ppermute | solution.py:36
  41.5 1.2 %collective-permute-start.21 = (f32[16,512]{1,0:T(8,128)S(1)}, f32[16,512]{1,0:T(8,128)S(1)}, u32[]{:S(2)}, u32[]{:S(2)}) collective-permute-start(f32[16,512]{1,0:T(8,128)S(1)} %collective-permute-done.20.refs_12_.refs_15_), channel_id=1, source_target_pairs={{0,1},{1,0},{2,3},{3,2},{4,5},{5,4},{6,7},{7,6},{8,9},{9,8},{10,11... | collective-permute-start | bytes 98312 | tf_op jit(solution)/shard_map/ppermute | solution.py:36
  41.5 4.0 %collective-permute-start.18 = (f32[16,512]{1,0:T(8,128)S(1)}, f32[16,512]{1,0:T(8,128)S(1)}, u32[]{:S(2)}, u32[]{:S(2)}) collective-permute-start(f32[16,512]{1,0:T(8,128)S(1)} %get-tuple-element.34), channel_id=1, source_target_pairs={{0,4},{4,0},{1,5},{5,1},{2,6},{6,2},{3,7},{7,3},{8,12},{12,8},{9,1... | collective-permute-start | bytes 98312 | tf_op jit(solution)/shard_map/ppermute | solution.py:36
  46.6 10.8 %all-to-all-start = ((f32[32,8,128]{2,1,0:T(8,128)}), f32[32,8,128]{2,1,0:T(8,128)S(1)}, u32[]{:S(2)}, u32[]{:S(2)}) async-start(f32[32,8,128]{2,1,0:T(8,128)} %get-tuple-element.35), calls=%async_computation | async-start | bytes 262144 | tf_op jit(solution)/shard_map/all_to_all | solution.py:416
  49.2 4.2 %collective-permute-start.24 = (f32[16,640]{1,0:T(8,128)S(1)}, f32[16,640]{1,0:T(8,128)S(1)}, u32[]{:S(2)}, u32[]{:S(2)}) collective-permute-start(f32[16,640]{1,0:T(8,128)S(1)} %get-tuple-element.36.refs_0_.refs_5_), channel_id=1, source_target_pairs={{0,2},{1,3},{2,0},{3,1},{4,6},{5,7},{6,4},{7,5},{8,10},{9,11},{10,... | collective-permute-start | bytes 122888 | tf_op jit(solution)/shard_map/ppermute | solution.py:36
  51.0 6.7 %collective-permute-start.23 = (f32[16,640]{1,0:T(8,128)S(1)}, f32[16,640]{1,0:T(8,128)S(1)}, u32[]{:S(2)}, u32[]{:S(2)}) collective-permute-start(f32[16,640]{1,0:T(8,128)S(1)} %get-tuple-element.36.refs_0_.refs_5_), channel_id=1, source_target_pairs={{0,1},{1,0},{2,3},{3,2},{4,5},{5,4},{6,7},{7,6},{8,9},{9,8},{10,11... | collective-permute-start | bytes 122888 | tf_op jit(solution)/shard_map/ppermute | solution.py:36
  53.5 4.3 %collective-permute-start.25 = (f32[16,640]{1,0:T(8,128)S(1)}, f32[16,640]{1,0:T(8,128)S(1)}, u32[]{:S(2)}, u32[]{:S(2)}) collective-permute-start(f32[16,640]{1,0:T(8,128)S(1)} %collective-permute-done.24.refs_2_.refs_7_), channel_id=1, source_target_pairs={{0,1},{1,0},{2,3},{3,2},{4,5},{5,4},{6,7},{7,6},{8,9},{9,8},{10,11... | collective-permute-start | bytes 122888 | tf_op jit(solution)/shard_map/ppermute | solution.py:36
  57.4 2.3 %collective-permute-start.22 = (f32[32,128]{1,0:T(8,128)S(1)}, f32[32,128]{1,0:T(8,128)S(1)}, u32[]{:S(2)}, u32[]{:S(2)}) collective-permute-start(f32[32,128]{1,0:T(8,128)S(1)} %shard_map.74.refs_0_), channel_id=1, source_target_pairs={{0,1},{1,0},{2,3},{3,2},{4,5},{5,4},{6,7},{7,6},{8,9},{9,8},{10,11... | collective-permute-start | bytes 49160 | tf_op jit(solution)/shard_map/ppermute | solution.py:423
